TPU v7x, 32 devices: a whole 2x2x4 slice. The times are simulated.
32 devices in a mesh: dp: 8 (over z, x), ctx: 4 (over y, core).
Axes of the slice: x: 2, y: 2, z: 4, core: 2. Of those that a mesh axis runs over, the one named last changes fastest.
Arguments:
- tokens: bfloat16 [16, 1024, 960], P('dp', 'ctx'), may hold values from -6 to 6
- segment_ids: int32 [16, 1024], P('dp', 'ctx'), may hold values from 0 to 5, as said below
- positions: int32 [16, 1024], P('dp', 'ctx'), may hold values from 0 to 2047, as said below
- norm_attn: float32 [960], replicated, may hold values from 0.25 to 1.75
- w_query: bfloat16 [921600], P(('dp', 'ctx')), may hold values from -0.1875 to 0.1875
- w_key: bfloat16 [307200], P(('dp', 'ctx')), may hold values from -0.1875 to 0.1875
- w_value: bfloat16 [307200], P(('dp', 'ctx')), may hold values from -0.1875 to 0.1875
- w_out: bfloat16 [921600], P(('dp', 'ctx')), may hold values from -0.75 to 0.75
- norm_ffn: float32 [960], replicated, may hold values from 0.25 to 1.75
- w_gate: bfloat16 [2457600], P(('dp', 'ctx')), may hold values from -0.1875 to 0.1875
- w_up: bfloat16 [2457600], P(('dp', 'ctx')), may hold values from -0.1875 to 0.1875
- w_down: bfloat16 [2457600], P(('dp', 'ctx')), may hold values from -0.125 to 0.125
- cotangent: bfloat16 [16, 1024, 960], P('dp', 'ctx'), may hold values from -6 to 6
Outputs:
- output: bfloat16 [16, 1024, 960], P('dp', 'ctx')
- d_tokens: float32 [16, 1024, 960], P('dp', 'ctx')
- d_norm_attn: float32 [960], replicated
- d_w_query: float32 [921600], P(('dp', 'ctx'))
- d_w_key: float32 [307200], P(('dp', 'ctx'))
- d_w_value: float32 [307200], P(('dp', 'ctx'))
- d_w_out: float32 [921600], P(('dp', 'ctx'))
- d_norm_ffn: float32 [960], replicated
- d_w_gate: float32 [2457600], P(('dp', 'ctx'))
- d_w_up: float32 [2457600], P(('dp', 'ctx'))
- d_w_down: float32 [2457600], P(('dp', 'ctx'))
Inputs may be any that keep to these rules, and one draw needn't show every extreme that they name: `segment_ids`: within each sequence the ids start at 0 and never fall. A run of one id is one document: a sequence's first run may be the rest of a longer document and has 102 positions or more, every later run is a document of 204 to 2047 positions, cut at the sequence's end. Within each run of one segment id the positions rise by one from token to token; every run but a sequence's first starts at 0, a sequence's first run starts at most at 1024.
All inputs are finite; a program needn't handle non-finite values.
Results may differ from a plain program's by a relative error of at most 0.02.
Values may be sent and summed in bfloat16 or wider, within the bound.
No kernel may reach another device: no remote copies, remote signals or barrier semaphores. Data moves between devices by JAX's collectives and lax.ppermute only.
A program may use at most 448 MiB of HBM per device.

v0:
```python
import jax
import jax.numpy as jnp
from jax import lax
from jax.sharding import PartitionSpec as P

D = 960
HEADS = 15
KV_HEADS = 5
HEAD_DIM = 64
FF = 2560
MICRO = 2


norm_eps = 1e-05
rope_base = 100000.0
mask_fill = -1000000000.0


def rms_scale(values):
    return lax.rsqrt(jnp.mean(values * values, axis=-1, keepdims=True) + norm_eps)


def norm_back(values, scale, gain, grad):
    gain_grad = jnp.sum(grad * values * scale, axis=0)
    weighted = grad * gain
    inner = jnp.mean(weighted * values, axis=-1, keepdims=True)
    return (scale * weighted - values * (scale * scale * scale) * inner, gain_grad)


def rope_tables(position):
    freqs = rope_base ** (-jnp.arange(0, HEAD_DIM, 2, dtype=jnp.float32) / HEAD_DIM)
    angles = position.astype(jnp.float32)[..., None] * freqs
    angles = jnp.concatenate([angles, angles], axis=-1)
    return (jnp.cos(angles)[..., None, :], jnp.sin(angles)[..., None, :])


def rotate(values, cosine, sine):
    half = values.shape[-1] // 2
    turned = jnp.concatenate([-values[..., half:], values[..., :half]], axis=-1)
    return values * cosine + turned * sine


def rotate_back(grad, cosine, sine):
    half = grad.shape[-1] // 2
    scaled = grad * sine
    return grad * cosine + jnp.concatenate([scaled[..., half:], -scaled[..., :half]], axis=-1)


def product(left, right):
    return jnp.dot(left, right, preferred_element_type=jnp.float32)


def product_left(left, right):
    return lax.dot_general(
        left, right, (((0,), (0,)), ((), ())), preferred_element_type=jnp.float32
    )


def product_right(left, right):
    return lax.dot_general(
        left, right, (((1,), (1,)), ((), ())), preferred_element_type=jnp.float32
    )


def masked_scores(query_groups, key_heads, allowed, score_scale):
    scores = (
        jnp.einsum("sckgd,slkd->skgcl", query_groups, key_heads, preferred_element_type=jnp.float32)
        * score_scale
    )
    return jnp.where(allowed, scores, mask_fill)


def owner_blocks(terms):
    dp_size = lax.axis_size("dp")
    ctx_size = lax.axis_size("ctx")
    return [term.reshape(dp_size, ctx_size, -1) for term in terms]


def reduce_at_end(terms):
    blocks = owner_blocks(terms)
    moved = (
        lax.all_to_all(
            blocks[0].astype(jnp.bfloat16), "ctx", split_axis=1, concat_axis=1, tiled=True
        ).astype(jnp.float32),
        lax.all_to_all(
            blocks[1].astype(jnp.bfloat16), "ctx", split_axis=1, concat_axis=1, tiled=True
        ).astype(jnp.float32),
        lax.all_to_all(
            blocks[2].astype(jnp.bfloat16), "ctx", split_axis=1, concat_axis=1, tiled=True
        ).astype(jnp.float32),
        lax.all_to_all(
            blocks[3].astype(jnp.bfloat16), "ctx", split_axis=1, concat_axis=1, tiled=True
        ).astype(jnp.float32),
        lax.all_to_all(
            blocks[4].astype(jnp.bfloat16), "ctx", split_axis=1, concat_axis=1, tiled=True
        ).astype(jnp.float32),
        lax.all_to_all(
            blocks[5].astype(jnp.bfloat16), "ctx", split_axis=1, concat_axis=1, tiled=True
        ).astype(jnp.float32),
        lax.all_to_all(
            blocks[6].astype(jnp.bfloat16), "ctx", split_axis=1, concat_axis=1, tiled=True
        ).astype(jnp.float32),
    )
    summed = [jnp.sum(piece, axis=1) for piece in moved]
    owned = (
        lax.psum_scatter(
            summed[0].astype(jnp.bfloat16), "dp", scatter_dimension=0, tiled=True
        ).astype(jnp.float32),
        lax.psum_scatter(
            summed[1].astype(jnp.bfloat16), "dp", scatter_dimension=0, tiled=True
        ).astype(jnp.float32),
        lax.psum_scatter(
            summed[2].astype(jnp.bfloat16), "dp", scatter_dimension=0, tiled=True
        ).astype(jnp.float32),
        lax.psum_scatter(
            summed[3].astype(jnp.bfloat16), "dp", scatter_dimension=0, tiled=True
        ).astype(jnp.float32),
        lax.psum_scatter(
            summed[4].astype(jnp.bfloat16), "dp", scatter_dimension=0, tiled=True
        ).astype(jnp.float32),
        lax.psum_scatter(
            summed[5].astype(jnp.bfloat16), "dp", scatter_dimension=0, tiled=True
        ).astype(jnp.float32),
        lax.psum_scatter(
            summed[6].astype(jnp.bfloat16), "dp", scatter_dimension=0, tiled=True
        ).astype(jnp.float32),
    )
    return [piece.reshape(-1) for piece in owned]


def body(
    tokens,
    segment_ids,
    positions,
    norm_attn,
    w_query,
    w_key,
    w_value,
    w_out,
    norm_ffn,
    w_gate,
    w_up,
    w_down,
    cotangent,
):
    seq_local, block_len, width = tokens.shape
    micro_seqs = seq_local // MICRO
    groups = HEADS // KV_HEADS
    attn_width = HEADS * HEAD_DIM
    kv_width = KV_HEADS * HEAD_DIM
    length = block_len * lax.axis_size("ctx")
    rows = micro_seqs * block_len
    score_scale = HEAD_DIM ** (-0.5)
    query_index = lax.axis_index("ctx") * block_len + jnp.arange(block_len, dtype=jnp.int32)
    key_index = jnp.arange(length, dtype=jnp.int32)
    shapes = (
        (D, attn_width),
        (D, kv_width),
        (D, kv_width),
        (attn_width, D),
        (D, FF),
        (D, FF),
        (FF, D),
    )

    def forward_weights():
        flats = (
            lax.all_gather(w_query, ("dp", "ctx"), axis=0, tiled=True),
            lax.all_gather(w_key, ("dp", "ctx"), axis=0, tiled=True),
            lax.all_gather(w_value, ("dp", "ctx"), axis=0, tiled=True),
            lax.all_gather(w_out, ("dp", "ctx"), axis=0, tiled=True),
            lax.all_gather(w_gate, ("dp", "ctx"), axis=0, tiled=True),
            lax.all_gather(w_up, ("dp", "ctx"), axis=0, tiled=True),
            lax.all_gather(w_down, ("dp", "ctx"), axis=0, tiled=True),
        )
        return [flat.reshape(shape) for flat, shape in zip(flats, shapes)]

    def backward_weights():
        flats = (
            lax.all_gather(w_query, ("dp", "ctx"), axis=0, tiled=True),
            lax.all_gather(w_key, ("dp", "ctx"), axis=0, tiled=True),
            lax.all_gather(w_value, ("dp", "ctx"), axis=0, tiled=True),
            lax.all_gather(w_out, ("dp", "ctx"), axis=0, tiled=True),
            lax.all_gather(w_gate, ("dp", "ctx"), axis=0, tiled=True),
            lax.all_gather(w_up, ("dp", "ctx"), axis=0, tiled=True),
            lax.all_gather(w_down, ("dp", "ctx"), axis=0, tiled=True),
        )
        return [flat.reshape(shape) for flat, shape in zip(flats, shapes)]

    grad_totals = [jnp.zeros(shape, jnp.float32) for shape in shapes]
    shard_totals = [
        jnp.zeros(shard.shape, jnp.float32)
        for shard in (w_query, w_key, w_value, w_out, w_gate, w_up, w_down)
    ]
    attn_gain_total = jnp.zeros((D,), jnp.float32)
    ffn_gain_total = jnp.zeros((D,), jnp.float32)
    outputs = []
    input_grads = []
    for micro in range(MICRO):
        lower = micro * micro_seqs
        upper = lower + micro_seqs
        inputs = tokens[lower:upper].astype(jnp.float32).reshape(rows, D)
        segment_part = segment_ids[lower:upper]
        position_part = positions[lower:upper]
        grad_out = cotangent[lower:upper].astype(jnp.float32).reshape(rows, D)
        query_weight, key_weight, value_weight, out_weight, gate_weight, up_weight, down_weight = (
            forward_weights()
        )
        scale_attn = rms_scale(inputs)
        normed_attn = (inputs * scale_attn * norm_attn).astype(jnp.bfloat16)
        cosine, sine = rope_tables(position_part)
        query_rot = rotate(
            product(normed_attn, query_weight).reshape(micro_seqs, block_len, HEADS, HEAD_DIM),
            cosine,
            sine,
        ).astype(jnp.bfloat16)
        key_rot = (
            rotate(
                product(normed_attn, key_weight).reshape(micro_seqs, block_len, KV_HEADS, HEAD_DIM),
                cosine,
                sine,
            )
            .astype(jnp.bfloat16)
            .reshape(micro_seqs, block_len, kv_width)
        )
        value_low = (
            product(normed_attn, value_weight)
            .astype(jnp.bfloat16)
            .reshape(micro_seqs, block_len, kv_width)
        )
        key_all, value_all, segment_all = (
            lax.all_gather(key_rot, "ctx", axis=1, tiled=True),
            lax.all_gather(value_low, "ctx", axis=1, tiled=True),
            lax.all_gather(segment_part, "ctx", axis=1, tiled=True),
        )
        key_heads = key_all.reshape(micro_seqs, length, KV_HEADS, HEAD_DIM)
        value_heads = value_all.reshape(micro_seqs, length, KV_HEADS, HEAD_DIM)
        query_groups = query_rot.reshape(micro_seqs, block_len, KV_HEADS, groups, HEAD_DIM)
        allowed = (
            (segment_part[:, :, None] == segment_all[:, None, :])
            & (key_index[None, None, :] <= query_index[None, :, None])
        )[:, None, None]
        masked = masked_scores(query_groups, key_heads, allowed, score_scale)
        row_max = jnp.max(masked, axis=-1, keepdims=True)
        exponent = jnp.exp(masked - row_max)
        total = jnp.sum(exponent, axis=-1, keepdims=True)
        probs_low = (exponent / total).astype(jnp.bfloat16)
        log_total = row_max + jnp.log(total)
        attended = (
            jnp.einsum(
                "skgcl,slkd->sckgd", probs_low, value_heads, preferred_element_type=jnp.float32
            )
            .astype(jnp.bfloat16)
            .reshape(rows, attn_width)
        )
        resid = inputs + product(attended, out_weight)
        scale_ffn = rms_scale(resid)
        normed_ffn = (resid * scale_ffn * norm_ffn).astype(jnp.bfloat16)
        gate = product(normed_ffn, gate_weight)
        up = product(normed_ffn, up_weight)
        hidden = (jax.nn.silu(gate) * up).astype(jnp.bfloat16)
        outputs.append(
            (resid + product(hidden, down_weight))
            .astype(jnp.bfloat16)
            .reshape(micro_seqs, block_len, D)
        )
        query_weight, key_weight, value_weight, out_weight, gate_weight, up_weight, down_weight = (
            backward_weights()
        )
        down_grad = grad_out.astype(jnp.bfloat16)
        fresh_down = product_left(hidden, down_grad)
        hidden_grad = product_right(down_grad, down_weight)
        gate_sigmoid = jax.nn.sigmoid(gate)
        gate_grad = (hidden_grad * up * gate_sigmoid * (1.0 + gate * (1.0 - gate_sigmoid))).astype(
            jnp.bfloat16
        )
        up_grad = (hidden_grad * gate * gate_sigmoid).astype(jnp.bfloat16)
        fresh_gate = product_left(normed_ffn, gate_grad)
        fresh_up = product_left(normed_ffn, up_grad)
        normed_grad = product_right(gate_grad, gate_weight) + product_right(up_grad, up_weight)
        resid_grad, ffn_gain_grad = norm_back(resid, scale_ffn, norm_ffn, normed_grad)
        resid_grad = resid_grad + grad_out
        branch_grad = resid_grad.astype(jnp.bfloat16)
        fresh_out = product_left(attended, branch_grad)
        attended_grad = (
            product_right(branch_grad, out_weight)
            .astype(jnp.bfloat16)
            .reshape(micro_seqs, block_len, KV_HEADS, groups, HEAD_DIM)
        )
        probs = jnp.exp(masked_scores(query_groups, key_heads, allowed, score_scale) - log_total)
        probs_grad = jnp.einsum(
            "sckgd,slkd->skgcl", attended_grad, value_heads, preferred_element_type=jnp.float32
        )
        inner = jnp.sum(probs * probs_grad, axis=-1, keepdims=True)
        scores_grad = (probs * (probs_grad - inner)).astype(jnp.bfloat16)
        query_grad = (
            jnp.einsum(
                "skgcl,slkd->sckgd", scores_grad, key_heads, preferred_element_type=jnp.float32
            )
            * score_scale
        )
        key_part = (
            jnp.einsum(
                "skgcl,sckgd->slkd", scores_grad, query_groups, preferred_element_type=jnp.float32
            )
            * score_scale
        )
        value_part = jnp.einsum(
            "skgcl,sckgd->slkd",
            probs.astype(jnp.bfloat16),
            attended_grad,
            preferred_element_type=jnp.float32,
        )
        key_grad, value_grad = (
            lax.psum_scatter(
                key_part.reshape(micro_seqs, length, kv_width).astype(jnp.bfloat16),
                "ctx",
                scatter_dimension=1,
                tiled=True,
            ).astype(jnp.float32),
            lax.psum_scatter(
                value_part.reshape(micro_seqs, length, kv_width).astype(jnp.bfloat16),
                "ctx",
                scatter_dimension=1,
                tiled=True,
            ).astype(jnp.float32),
        )
        query_low = (
            rotate_back(query_grad.reshape(micro_seqs, block_len, HEADS, HEAD_DIM), cosine, sine)
            .astype(jnp.bfloat16)
            .reshape(rows, attn_width)
        )
        key_low = (
            rotate_back(key_grad.reshape(micro_seqs, block_len, KV_HEADS, HEAD_DIM), cosine, sine)
            .astype(jnp.bfloat16)
            .reshape(rows, kv_width)
        )
        value_grad_low = value_grad.astype(jnp.bfloat16).reshape(rows, kv_width)
        fresh_query = product_left(normed_attn, query_low)
        fresh_key = product_left(normed_attn, key_low)
        fresh_value = product_left(normed_attn, value_grad_low)
        attn_normed_grad = (
            product_right(query_low, query_weight)
            + product_right(key_low, key_weight)
            + product_right(value_grad_low, value_weight)
        )
        input_grad, attn_gain_grad = norm_back(inputs, scale_attn, norm_attn, attn_normed_grad)
        input_grads.append((input_grad + resid_grad).reshape(micro_seqs, block_len, D))
        attn_gain_total = attn_gain_total + attn_gain_grad
        ffn_gain_total = ffn_gain_total + ffn_gain_grad
        fresh = [fresh_query, fresh_key, fresh_value, fresh_out, fresh_gate, fresh_up, fresh_down]
        grad_totals = [running + piece for running, piece in zip(grad_totals, fresh)]
    shard_totals = reduce_at_end(grad_totals)
    attn_gain_sum, ffn_gain_sum = lax.psum((attn_gain_total, ffn_gain_total), ("dp", "ctx"))
    output = jnp.concatenate(outputs, axis=0)
    d_tokens = jnp.concatenate(input_grads, axis=0)
    return (
        output,
        d_tokens,
        attn_gain_sum,
        shard_totals[0],
        shard_totals[1],
        shard_totals[2],
        shard_totals[3],
        ffn_gain_sum,
        shard_totals[4],
        shard_totals[5],
        shard_totals[6],
    )


def solution(mesh):
    in_specs = (
        P("dp", "ctx", None),
        P("dp", "ctx"),
        P("dp", "ctx"),
        P(),
        P(("dp", "ctx")),
        P(("dp", "ctx")),
        P(("dp", "ctx")),
        P(("dp", "ctx")),
        P(),
        P(("dp", "ctx")),
        P(("dp", "ctx")),
        P(("dp", "ctx")),
        P("dp", "ctx", None),
    )
    out_specs = (
        P("dp", "ctx", None),
        P("dp", "ctx", None),
        P(),
        P(("dp", "ctx")),
        P(("dp", "ctx")),
        P(("dp", "ctx")),
        P(("dp", "ctx")),
        P(),
        P(("dp", "ctx")),
        P(("dp", "ctx")),
        P(("dp", "ctx")),
    )
    return jax.shard_map(body, mesh=mesh, in_specs=in_specs, out_specs=out_specs, check_vma=False)
```

profile of v0, /device:TPU:0, one launch (start us, length us, event | category | flops | bytes accessed | tf_op | source)
XLA Modules:
  0.0 967.7 jit_solution(10681395734420961702)
XLA Ops:
  13.2 47.4 %all-gather.4 = bf16[32,1,9600]{2,1,0:T(2,128)(2,1)S(1)} all-gather(bf16[1,1,9600]{2,1,0:T(2,128)(2,1)S(1)} %reshape.1609), channel_id=1, replica_groups=mesh['dp'=8,'ctx'=4] {'dp','ctx'}, dimensions={0}, use_global_device_ids=true | all-gather | bytes 633600 | tf_op jit(solution)/shard_map/all_gather | solution.py:170
  66.2 42.0 %all-gather.5 = bf16[32,1,9600]{2,1,0:T(2,128)(2,1)S(1)} all-gather(bf16[1,1,9600]{2,1,0:T(2,128)(2,1)S(1)} %reshape.1611), channel_id=1, replica_groups=mesh['dp'=8,'ctx'=4] {'dp','ctx'}, dimensions={0}, use_global_device_ids=true | all-gather | bytes 633600 | tf_op jit(solution)/shard_map/all_gather | solution.py:169
  117.0 8.5 all-gather.2
  126.8 10.4 %all-gather.3 = bf16[1024,320]{0,1:T(8,128)(2,1)S(1)} all-gather(bf16[256,320]{0,1:T(8,128)(2,1)S(1)} %fusion.106), channel_id=5, replica_groups=mesh['dp'=8,'ctx'=4] {'ctx'}, dimensions={0}, use_global_device_ids=true | all-gather | bytes 819200 | tf_op jit(solution)/shard_map/all_gather | solution.py:232
  147.4 8.4 all-gather
  155.9 8.7 all-gather.1
  166.0 39.5 %reduce.15 = bf16[32,28800]{1,0:T(8,128)(2,1)S(1)} reduce(bf16[32,1,28800]{2,1,0:T(2,128)(2,1)} %all-gather.20.cloned.1.call-done, bf16[]{:T(256)} %constant.80), dimensions={1}, to_apply=%all-gather.6.reduce_sub_computation | reduce | bytes 3686402 | tf_op jit(solution)/shard_map/all_gather | solution.py:168
  225.9 39.9 %reduce.16 = bf16[32,28800]{1,0:T(8,128)(2,1)S(1)} reduce(bf16[32,1,28800]{2,1,0:T(2,128)(2,1)} %all-gather.22.cloned.1.call-done, bf16[]{:T(256)} %constant.80), dimensions={1}, to_apply=%all-gather.7.reduce_sub_computation | reduce | bytes 3686402 | tf_op jit(solution)/shard_map/all_gather | solution.py:171
  268.6 8.7 fusion.44
  304.5 10.0 %reshape.1537 = bf16[960,2560]{1,0:T(8,128)(2,1)} reshape(bf16[2457600]{0:T(1024)(128)(2,1)} %all-gather.14.cloned.1.call-done) | data formatting | bytes 9830400 | tf_op jit(solution)/shard_map/reshape | solution.py:176
  314.5 10.0 %reshape.1538 = bf16[960,2560]{1,0:T(8,128)(2,1)} reshape(bf16[2457600]{0:T(1024)(128)(2,1)} %all-gather.16.cloned.1.call-done) | data formatting | bytes 9830400 | tf_op jit(solution)/shard_map/reshape | solution.py:176
  333.1 10.4 %all-gather.18.cloned.1.call-done = bf16[2457600]{0:T(1024)(128)(2,1)} async-done(((bf16[76800]{0:T(1024)(128)(2,1)}), bf16[2457600]{0:T(1024)(128)(2,1)}) %all-gather.18.cloned.1.call-update) | async-done | bytes 4915216 | tf_op jit(solution)/shard_map/all_gather | solution.py:174
  343.5 9.6 reshape.1539
  353.0 9.0 multiply_convert_fusion.2
  411.1 13.0 %fusion.3 = (f32[5,3,256]{2,1,0:T(4,128)S(1)}, f32[5,1024,256,3]{2,1,3,0:T(8,128)}) fusion(f32[1,5,3,256,1024]{3,4,2,1,0:T(8,128)} %get-tuple-element.82, f32[5,3,256]{2,1,0:T(4,128)S(1)} %log_add_fusion.1, bf16[1024,5,64,1]{0,2,3,1:T(8,128)(2,1)} %bitcast.417, bf16[256,5,3,64]{0,3,2,1:T(8,128)(2,1)S(1)} %bitcast.406), kind=kOutput, calls=%fused_computation.9 | convolution fusion | flops 515109120 | bytes 32634880 | tf_op jit(solution)/shard_map/sckgd,slkd->skgcl/dot_general | solution.py:291
  448.0 9.1 fusion.37
  478.4 9.1 fusion.34
  514.3 23.1 %all-to-all-done.3 = bf16[8,4,28800]{2,0,1:T(8,128)(2,1)} async-done(((bf16[8,4,28800]{2,0,1:T(8,128)(2,1)}), bf16[8,4,28800]{2,0,1:T(8,128)(2,1)}, u32[]{:S(2)}, u32[]{:S(2)}) %all-to-all-start.3) | async-done | bytes 1843232 | tf_op jit(solution)/shard_map/all_to_all | solution.py:91
  602.7 35.4 %all-to-all-done.4 = bf16[8,4,76800]{2,0,1:T(8,128)(2,1)} async-done(((bf16[8,4,76800]{2,0,1:T(8,128)(2,1)}), bf16[8,4,76800]{2,0,1:T(8,128)(2,1)}, u32[]{:S(2)}, u32[]{:S(2)}) %all-to-all-start.4) | async-done | bytes 4915232 | tf_op jit(solution)/shard_map/all_to_all | solution.py:94
  657.6 10.0 %convert_element_type.492 = bf16[8,4,76800]{2,1,0:T(4,128)(2,1)} reshape(bf16[2560,960]{1,0:T(8,128)(2,1)} %copy.59) | data formatting | bytes 9830400 | tf_op jit(solution)/shard_map/convert_element_type | solution.py:101
  673.6 25.5 %all-to-all-done.5 = bf16[8,4,76800]{2,0,1:T(8,128)(2,1)} async-done(((bf16[8,4,76800]{2,0,1:T(8,128)(2,1)}), bf16[8,4,76800]{2,0,1:T(8,128)(2,1)}, u32[]{:S(2)}, u32[]{:S(2)}) %all-to-all-start.5) | async-done | bytes 4915232 | tf_op jit(solution)/shard_map/all_to_all | solution.py:97
  721.3 38.7 %all-to-all-done.6 = bf16[8,4,76800]{2,0,1:T(8,128)(2,1)} async-done(((bf16[8,4,76800]{2,0,1:T(8,128)(2,1)}), bf16[8,4,76800]{2,0,1:T(8,128)(2,1)}, u32[]{:S(2)}, u32[]{:S(2)}) %all-to-all-start.6) | async-done | bytes 4915232 | tf_op jit(solution)/shard_map/all_to_all | solution.py:100
  783.1 45.0 %all-reduce.7 = (f32[960]{0:T(1024)}, f32[960]{0:T(1024)}) all-reduce(f32[960]{0:T(1024)S(1)} %add.336, f32[960]{0:T(1024)S(1)} %add.341), channel_id=1, replica_groups=mesh['dp'=8,'ctx'=4] {'dp','ctx'}, use_global_device_ids=true, to_apply=%region_20.21 | all-reduce | flops 1920 | bytes 15360 | tf_op jit(solution)/shard_map/psum | solution.py:354
  831.8 109.9 %all-reduce.11.cloned.1.call-done = (bf16[8,28800]{1,0:T(8,128)(2,1)}, bf16[8,9600]{1,0:T(8,128)(2,1)}, bf16[8,9600]{1,0:T(8,128)(2,1)}, bf16[8,28800]{1,0:T(8,1...) async-done(((bf16[8,28800]{1,0:T(8,128)(2,1)}, bf16[8,9600]{1,0:T(8,128)(2,1)}, bf16[8,9600]{1,0:T(8,128)(2,1)}, ...) | async-done | bytes 4915216
  (399 shorter events, 370.3 us)
Async XLA Ops:
  7.2 58.8 %copy-start.1 = (bf16[2,256,960]{1,2,0:T(8,128)(2,1)S(1)}, bf16[2,256,960]{1,2,0:T(8,128)(2,1)}, u32[]{:S(2)}) copy-start(bf16[2,256,960]{1,2,0:T(8,128)(2,1)} %param.13) | copy-start | bytes 2949124
  7.2 59.0 %copy-start.85 = (bf16[9600]{0:T(1024)(128)(2,1)S(1)}, bf16[9600]{0:T(1024)(128)(2,1)}, u32[]{:S(2)}) copy-start(bf16[9600]{0:T(1024)(128)(2,1)} %param.18) | copy-start | bytes 57604
  7.2 158.8 %all-gather.20.cloned.1.call-start = ((), (), s32[]{:S(2)}) async-start(), calls=%async_computation.18 | async-start | bytes 3801600 | tf_op jit(solution)/shard_map/all_gather | solution.py:168
  8.9 217.0 %all-gather.22.cloned.1.call-start = ((), (), s32[]{:S(2)}) async-start(), calls=%async_computation.19 | async-start | bytes 3801600 | tf_op jit(solution)/shard_map/all_gather | solution.py:171
  10.5 294.0 %all-gather.14.cloned.1.call-start = ((), (), s32[]{:S(2)}) async-start(), calls=%async_computation.11 | async-start | bytes 5068800 | tf_op jit(solution)/shard_map/all_gather | solution.py:172
  11.2 303.2 %all-gather.16.cloned.1.call-start = ((), (), s32[]{:S(2)}) async-start(), calls=%async_computation.12 | async-start | bytes 5068800 | tf_op jit(solution)/shard_map/all_gather | solution.py:173
  11.8 331.7 %all-gather.18.cloned.1.call-start = ((), (), s32[]{:S(2)}) async-start(), calls=%async_computation.13 | async-start | bytes 5068800 | tf_op jit(solution)/shard_map/all_gather | solution.py:174
  12.4 492.0 %reduce-scatter.9.cloned.1.call-start = ((), (), s32[]{:S(2)}) async-start(), calls=%async_computation.16 | async-start | bytes 819200 | tf_op jit(solution)/shard_map/reduce_scatter | solution.py:315
  60.6 52.8 %copy-start.72 = (f32[960]{0:T(1024)S(1)}, f32[960]{0:T(1024)}, u32[]{:S(2)}) copy-start(f32[960]{0:T(1024)} %param.16) | copy-start | bytes 11524
  113.4 94.9 %copy-start.80 = (f32[256]{0:T(256)}, f32[256]{0:T(256)S(1)}, u32[]{:S(2)}) copy-start(f32[256]{0:T(256)S(1)} %get-tuple-element.94) | copy-start | bytes 3076
  126.2 85.0 %copy-start.45 = (f32[256,64]{0,1:T(8,128)}, f32[256,64]{0,1:T(8,128)S(1)}, u32[]{:S(2)}) copy-start(f32[256,64]{0,1:T(8,128)S(1)} %get-tuple-element.59) | copy-start | bytes 196612
  137.3 143.2 %copy-start.14 = (bf16[1024,320]{0,1:T(8,128)(2,1)}, bf16[1024,320]{0,1:T(8,128)(2,1)S(1)}, u32[]{:S(2)}) copy-start(bf16[1024,320]{0,1:T(8,128)(2,1)S(1)} %all-gather.3) | copy-start | bytes 1966084
  218.2 50.4 %copy-start.74 = (f32[5,3,256]{2,1,0:T(4,128)}, f32[5,3,256]{2,1,0:T(4,128)S(1)}, u32[]{:S(2)}) copy-start(f32[5,3,256]{2,1,0:T(4,128)S(1)} %get-tuple-element.81) | copy-start | bytes 46084
  408.5 96.9 %reduce-scatter.5.cloned.1.call-start = ((), (), s32[]{:S(2)}) async-start(), calls=%async_computation.14 | async-start | bytes 819200 | tf_op jit(solution)/shard_map/reduce_scatter | solution.py:315
  442.9 98.7 %reduce-scatter.7.cloned.1.call-start = ((), (), s32[]{:S(2)}) async-start(), calls=%async_computation.15 | async-start | bytes 819200 | tf_op jit(solution)/shard_map/reduce_scatter | solution.py:321
  473.5 32.9 %all-to-all-start = ((bf16[8,4,28800]{2,0,1:T(8,128)(2,1)}), bf16[8,4,28800]{2,0,1:T(8,128)(2,1)}, u32[]{:S(2)}, u32[]{:S(2)}) async-start(bf16[8,4,28800]{2,0,1:T(8,128)(2,1)} %copy.51), calls=%async_computation.4 | async-start | bytes 3686400 | tf_op jit(solution)/shard_map/all_to_all | solution.py:82
  477.9 66.1 %reduce-scatter.11.cloned.1.call-start = ((), (), s32[]{:S(2)}) async-start(), calls=%async_computation.17 | async-start | bytes 819200 | tf_op jit(solution)/shard_map/reduce_scatter | solution.py:321
  506.5 31.0 %all-to-all-start.3 = ((bf16[8,4,28800]{2,0,1:T(8,128)(2,1)}), bf16[8,4,28800]{2,0,1:T(8,128)(2,1)}, u32[]{:S(2)}, u32[]{:S(2)}) async-start(bf16[8,4,28800]{2,0,1:T(8,128)(2,1)} %copy.56), calls=%async_computation.7 | async-start | bytes 3686400 | tf_op jit(solution)/shard_map/all_to_all | solution.py:91
  537.4 14.0 %all-to-all-start.1 = ((bf16[8,4,9600]{2,0,1:T(8,128)(2,1)}), bf16[8,4,9600]{2,0,1:T(8,128)(2,1)}, u32[]{:S(2)}, u32[]{:S(2)}) async-start(bf16[8,4,9600]{2,0,1:T(8,128)(2,1)} %copy.53), calls=%async_computation.5 | async-start | bytes 1228800 | tf_op jit(solution)/shard_map/all_to_all | solution.py:85
  551.5 25.7 %all-to-all-start.2 = ((bf16[8,4,9600]{2,0,1:T(8,128)(2,1)}), bf16[8,4,9600]{2,0,1:T(8,128)(2,1)S(1)}, u32[]{:S(2)}, u32[]{:S(2)}) async-start(bf16[8,4,9600]{2,0,1:T(8,128)(2,1)} %copy.55), calls=%async_computation.6 | async-start | bytes 1228800 | tf_op jit(solution)/shard_map/all_to_all | solution.py:88
  577.2 60.9 %all-to-all-start.4 = ((bf16[8,4,76800]{2,0,1:T(8,128)(2,1)}), bf16[8,4,76800]{2,0,1:T(8,128)(2,1)}, u32[]{:S(2)}, u32[]{:S(2)}) async-start(bf16[8,4,76800]{2,0,1:T(8,128)(2,1)} %copy.57), calls=%async_computation.8 | async-start | bytes 9830400 | tf_op jit(solution)/shard_map/all_to_all | solution.py:94
  638.1 61.0 %all-to-all-start.5 = ((bf16[8,4,76800]{2,0,1:T(8,128)(2,1)}), bf16[8,4,76800]{2,0,1:T(8,128)(2,1)}, u32[]{:S(2)}, u32[]{:S(2)}) async-start(bf16[8,4,76800]{2,0,1:T(8,128)(2,1)} %copy.58), calls=%async_computation.9 | async-start | bytes 9830400 | tf_op jit(solution)/shard_map/all_to_all | solution.py:97
  699.1 61.0 %all-to-all-start.6 = ((bf16[8,4,76800]{2,0,1:T(8,128)(2,1)}), bf16[8,4,76800]{2,0,1:T(8,128)(2,1)}, u32[]{:S(2)}, u32[]{:S(2)}) async-start(bf16[8,4,76800]{2,0,1:T(8,128)(2,1)} %copy.60), calls=%async_computation.10 | async-start | bytes 9830400 | tf_op jit(solution)/shard_map/all_to_all | solution.py:100
  704.1 237.6 %all-reduce.11.cloned.1.call-start = ((), (), s32[]{:S(2)}) async-start(), calls=%async_computation.20 | async-start | bytes 9830400
  (100 other events, 742.4 us)
Sparse Core Ops, SparseCore 0:
  11.5 66.7 all-gather.19
  81.8 60.0 all-gather.21
  144.7 66.9 all-gather.13
  214.3 63.1 all-gather.15
  280.2 63.2 all-gather.17
  408.7 21.2 reduce-scatter.8
  443.0 21.2 reduce-scatter.4
  466.9 26.0 reduce-scatter.6
  497.9 26.2 reduce-scatter.10
  764.7 176.9 all-reduce.10
where the time goes:
time: 976 us; the launch traced here: 968 us
  waiting for transfers between devices  249 us (26%)
  matrix products  188 us (19%)
  blocking collectives  180 us (18%)
  other arithmetic  175 us (18%)
  local copies, waits for them, and re-layouts  126 us (13%)
  starting transfers between devices  32.6 us (3%)
  between operations  16 us (2%)
    unnamed x11, waiting for transfers between devices  112 us
    all_gather x1, blocking collectives, forward_weights(): lax.all_gather(w_value, ('dp', 'ctx'), axis=0, tiled=True)  47.4 us
    dot_general x14, matrix products, product_left(): lax.dot_general(left, right, (((0,), (0,)), ((), ())), preferred_element_...  45.5 us
    psum x1, blocking collectives, body(): lax.psum((attn_gain_total, ffn_gain_total), ('dp', 'ctx'))  45 us
    all_gather x1, blocking collectives, forward_weights(): lax.all_gather(w_key, ('dp', 'ctx'), axis=0, tiled=True)  42 us
    all_gather x1, other arithmetic, forward_weights(): lax.all_gather(w_out, ('dp', 'ctx'), axis=0, tiled=True)  39.9 us
    all_gather x1, other arithmetic, forward_weights(): lax.all_gather(w_query, ('dp', 'ctx'), axis=0, tiled=True)  39.5 us
    all_to_all x1, waiting for transfers between devices, reduce_at_end(): lax.all_to_all(blocks[6].astype(jnp.bfloat16), 'ctx', split_axis=1, conca...  38.7 us
  transfers between devices with their start and end apart: 17, of which 7 were waited for; matrix products, arithmetic and copies ran while one was open for 40% of the time, Pallas kernels for 0%

commit v1 on v0

v1 whole, which is shorter than its diff:
```python
import jax
import jax.numpy as jnp
from jax import lax
from jax.experimental import pallas as pl
from jax.experimental.pallas import tpu as pltpu
from jax.sharding import PartitionSpec as P

D = 960
HEADS = 15
KV_HEADS = 5
HEAD_DIM = 64
FF = 2560
GROUP = HEADS // KV_HEADS
ATTN = HEADS * HEAD_DIM
KV = KV_HEADS * HEAD_DIM
AXES = ("dp", "ctx")
CORE, FIRST, SECOND = 1, 2, 4

norm_eps = 1e-05
rope_base = 100000.0
mask_fill = -1000000000.0
low = jnp.bfloat16
wide = jnp.float32


def rms_scale(values):
    return lax.rsqrt(jnp.mean(values * values, axis=-1, keepdims=True) + norm_eps)


def norm_back(values, scale, gain, grad):
    gain_grad = jnp.sum(grad * values * scale, axis=0)
    weighted = grad * gain
    inner = jnp.mean(weighted * values, axis=-1, keepdims=True)
    return (scale * weighted - values * (scale * scale * scale) * inner, gain_grad)


def rope_tables(position):
    freqs = rope_base ** (-jnp.arange(0, HEAD_DIM, 2, dtype=wide) / HEAD_DIM)
    angles = position.astype(wide)[..., None] * freqs
    angles = jnp.concatenate([angles, angles], axis=-1)
    return (jnp.cos(angles)[..., None, :], jnp.sin(angles)[..., None, :])


def rotate(values, cosine, sine):
    half = values.shape[-1] // 2
    turned = jnp.concatenate([-values[..., half:], values[..., :half]], axis=-1)
    return values * cosine + turned * sine


def rotate_back(grad, cosine, sine):
    half = grad.shape[-1] // 2
    scaled = grad * sine
    return grad * cosine + jnp.concatenate([scaled[..., half:], -scaled[..., :half]], axis=-1)


def product(left, right):
    return jnp.dot(left, right, preferred_element_type=wide)


def product_left(left, right):
    return lax.dot_general(left, right, (((0,), (0,)), ((), ())), preferred_element_type=wide)


def product_right(left, right):
    return lax.dot_general(left, right, (((1,), (1,)), ((), ())), preferred_element_type=wide)


def swap(value, mask):
    n = lax.axis_size(AXES)
    return lax.ppermute(value, AXES, [(i, i ^ mask) for i in range(n)])


def add_low(left, right):
    return (left.astype(wide) + right.astype(wide)).astype(low)


def far_masks():
    n = lax.axis_size(AXES)
    masks, m = [], 8
    while m < n:
        masks.append(m)
        m *= 2
    return masks


def block_owner(place):
    far = far_masks()
    owner = jnp.zeros_like(place)
    for bit, mask in enumerate(far + [SECOND, FIRST, CORE]):
        owner = owner | (((place >> bit) & 1) * mask)
    return owner


def gather_far(piece):
    now = piece[None]
    for mask in far_masks():
        now = jnp.concatenate([now, swap(now, mask)], axis=0)
    return now


def gather_near(now, route):
    n = now.shape[0]
    if route == 0:
        now = jnp.concatenate([now, swap(now, SECOND)], axis=0)
        half = jnp.concatenate([now, swap(now, FIRST)], axis=0)
    else:
        side = swap(now, FIRST)
        rest = swap(jnp.concatenate([now, side], axis=0), SECOND)
        half = jnp.concatenate([now, rest[:n], side, rest[n:]], axis=0)
    return half, swap(half, CORE)


def scatter_sum(mine, theirs, route):
    now = add_low(mine, swap(theirs, CORE))
    n = now.shape[0] // 4
    if route == 0:
        now = add_low(now[: 2 * n], swap(now[2 * n :], FIRST))
        now = add_low(now[:n], swap(now[n:], SECOND))
    else:
        send = jnp.concatenate([now[n : 2 * n], now[3 * n :]], axis=0)
        keep = jnp.concatenate([now[:n], now[2 * n : 3 * n]], axis=0)
        now = add_low(keep, swap(send, SECOND))
        now = add_low(now[:n], swap(now[n:], FIRST))
    for mask in far_masks()[::-1]:
        n = now.shape[0] // 2
        now = now[:n].astype(wide) + swap(now[n:], mask).astype(wide)
        if n > 1:
            now = now.astype(low)
    return now[0]


def ctx_masks():
    m, masks = lax.axis_size("ctx") // 2, []
    while m >= 1:
        masks.append(m)
        m //= 2
    return masks


def ctx_gather(value):
    now = value[None]
    for mask in ctx_masks():
        now = jnp.concatenate([now, swap(now, mask)], axis=0)
    return now


def ctx_scatter(value):
    now = value
    for mask in ctx_masks()[::-1]:
        n = now.shape[0] // 2
        now = now[:n].astype(wide) + swap(now[n:], mask).astype(wide)
        if n > 1:
            now = now.astype(low)
    return now[0]


def ctx_owner(places):
    owner = jnp.zeros_like(places)
    for bit, mask in enumerate(ctx_masks()):
        owner = owner | (((places >> bit) & 1) * mask)
    return owner


def move_blocks(parts, order, outs):
    parts = list(parts)
    if outs is None:
        each = parts[0].shape[0]
        total = each * len(parts)
        shapes = [jax.ShapeDtypeStruct((total,) + parts[0].shape[1:], parts[0].dtype)]
    else:
        total = parts[0].shape[0]
        each = total // outs
        shapes = [jax.ShapeDtypeStruct((each,) + parts[0].shape[1:], parts[0].dtype)] * outs
    n_in = len(parts)

    def kernel(order_ref, *refs):
        ins, out, sem = refs[:n_in], refs[n_in:-1], refs[-1]
        copies = []
        for p in range(total):
            if outs is None:
                src, dst = ins[p // each].at[p % each], out[0].at[order_ref[p]]
            else:
                src, dst = ins[0].at[order_ref[p]], out[p // each].at[p % each]
            copies.append(pltpu.make_async_copy(src, dst, sem.at[p]))
        for copy in copies:
            copy.start()
        for copy in copies:
            copy.wait()

    size = sum(p.size for p in parts) * 2
    return pl.pallas_call(
        kernel,
        out_shape=shapes,
        in_specs=[pl.BlockSpec(memory_space=pltpu.SMEM)]
        + [pl.BlockSpec(memory_space=pl.ANY)] * n_in,
        out_specs=[pl.BlockSpec(memory_space=pl.ANY)] * len(shapes),
        scratch_shapes=[pltpu.SemaphoreType.DMA((total,))],
        cost_estimate=pl.CostEstimate(flops=0, bytes_accessed=2 * size, transcendentals=0),
        name="move_blocks",
    )(order, *parts)


def body(
    tokens,
    segment_ids,
    positions,
    norm_attn,
    w_query,
    w_key,
    w_value,
    w_out,
    norm_ffn,
    w_gate,
    w_up,
    w_down,
    cotangent,
):
    seqs, block_len, width = tokens.shape
    n_dev = lax.axis_size(AXES)
    ctx_size = lax.axis_size("ctx")
    me = lax.axis_index(AXES)
    rows = seqs * block_len
    length = block_len * ctx_size
    score_scale = HEAD_DIM ** (-0.5)
    ctx_here = lax.axis_index("ctx")
    places = jnp.arange(n_dev, dtype=jnp.int32)
    blocked = n_dev >= 8 and (n_dev & (n_dev - 1)) == 0 and D % n_dev == 0 and FF % n_dev == 0

    if blocked:
        cut, cut_ff = D // n_dev, FF // n_dev
        pad = -(-cut // 16) * 16
        half_ff = cut_ff // 2
        order = block_owner(places) ^ me
        slot = jnp.arange(n_dev * pad, dtype=jnp.int32)
        source = jnp.where(slot % pad < cut, jnp.repeat(order, pad) * cut + slot % pad, -1)
        perm = (jnp.arange(D, dtype=jnp.int32)[:, None] == source[None, :]).astype(low)

        def spread(value):
            return product(value, perm).astype(low)

        def collect(value):
            return product_right(value, perm)

        def rows_of(shard, columns):
            return jnp.pad(shard.reshape(cut, columns), ((0, pad - cut), (0, 0)))

        own = [
            rows_of(w_query, ATTN),
            jnp.concatenate([rows_of(w_key, KV), rows_of(w_value, KV)], axis=1),
            rows_of(w_out, D),
            rows_of(w_gate, FF),
            rows_of(w_up, FF),
            w_down.reshape(cut_ff, D)[:half_ff],
            w_down.reshape(cut_ff, D)[half_ff:],
        ]
        routes = [0, 1, 1, 0, 1, 0, 1]
        full = []
        before = None
        for piece, route in zip(own, routes):
            if before is not None:
                piece, _ = lax.optimization_barrier((piece, before))
            now = gather_far(piece)
            before = now
            full.append(gather_near(now, route))
        rel = [jnp.concatenate(f, axis=0).reshape(-1, f[0].shape[-1]) for f in full[:5]]
        query_weight, kv_weight, out_weight, gate_weight, up_weight = rel
        down_halves = [
            move_blocks(full[5], order, None)[0],
            move_blocks(full[6], order, None)[0],
        ]
        down_weight = jnp.concatenate(down_halves, axis=1).reshape(FF, D)
    else:
        perm = None

        def spread(value):
            return value

        def collect(value):
            return value.astype(wide)

        def whole(shard, columns):
            return lax.all_gather(shard, AXES, axis=0, tiled=True).reshape(-1, columns)

        query_weight = whole(w_query, ATTN)
        kv_weight = jnp.concatenate([whole(w_key, KV), whole(w_value, KV)], axis=1)
        out_weight = whole(w_out, D)
        gate_weight, up_weight = whole(w_gate, FF), whole(w_up, FF)
        down_weight = whole(w_down, D)

    def collect_wide(value):
        if perm is None:
            return value
        high = lax.reduce_precision(value, 8, 7)
        return collect(high.astype(low)) + collect((value - high).astype(low))

    inputs = tokens.astype(wide).reshape(rows, D)
    grad_out = cotangent.astype(wide).reshape(rows, D)
    segment_all = ctx_gather(segment_ids)
    scale_attn = rms_scale(inputs)
    normed_attn = spread((inputs * scale_attn * norm_attn).astype(low))
    cosine, sine = rope_tables(positions)
    key_value = product(normed_attn, kv_weight).reshape(seqs, block_len, 2 * KV_HEADS, HEAD_DIM)
    key_rot = rotate(key_value[:, :, :KV_HEADS], cosine, sine).astype(low)
    both = jnp.concatenate([key_rot, key_value[:, :, KV_HEADS:].astype(low)], axis=2)
    both_all = ctx_gather(both.reshape(seqs, block_len, 2 * KV))
    query_rot = rotate(
        product(normed_attn, query_weight).reshape(seqs, block_len, HEADS, HEAD_DIM), cosine, sine
    ).astype(low)
    both_all = both_all.transpose(1, 0, 2, 3).reshape(seqs, length, 2, KV_HEADS, HEAD_DIM)
    key_heads, value_heads = both_all[:, :, 0], both_all[:, :, 1]
    segment_all = segment_all.transpose(1, 0, 2).reshape(seqs, length)
    query_index = ctx_here * block_len + jnp.arange(block_len, dtype=jnp.int32)
    key_block = ctx_owner(jnp.arange(ctx_size, dtype=jnp.int32)) ^ ctx_here
    key_index = (
        key_block[:, None] * block_len + jnp.arange(block_len, dtype=jnp.int32)[None, :]
    ).reshape(length)
    query_groups = query_rot.reshape(seqs, block_len, KV_HEADS, GROUP, HEAD_DIM)
    allowed = (
        (segment_ids[:, :, None] == segment_all[:, None, :])
        & (key_index[None, None, :] <= query_index[None, :, None])
    )[:, None, None]

    def masked_scores():
        scores = (
            jnp.einsum("sckgd,slkd->skgcl", query_groups, key_heads, preferred_element_type=wide)
            * score_scale
        )
        return jnp.where(allowed, scores, mask_fill)

    masked = masked_scores()
    row_max = jnp.max(masked, axis=-1, keepdims=True)
    exponent = jnp.exp(masked - row_max)
    total = jnp.sum(exponent, axis=-1, keepdims=True)
    probs_low = (exponent / total).astype(low)
    log_total = row_max + jnp.log(total)
    attended = spread(
        jnp.einsum("skgcl,slkd->sckgd", probs_low, value_heads, preferred_element_type=wide)
        .astype(low)
        .reshape(rows, ATTN)
    )
    resid = inputs + product(attended, out_weight)
    scale_ffn = rms_scale(resid)
    normed_ffn = spread((resid * scale_ffn * norm_ffn).astype(low))
    gate = product(normed_ffn, gate_weight)
    up = product(normed_ffn, up_weight)
    gate_sigmoid = jax.nn.sigmoid(gate)
    hidden = (gate * gate_sigmoid * up).astype(low)
    output = (resid + product(hidden, down_weight)).astype(low).reshape(seqs, block_len, D)

    down_grad = cotangent.reshape(rows, D)
    fresh_down = product_left(hidden, down_grad).astype(low)
    hidden_grad = product_right(down_grad, down_weight)
    gate_grad = (hidden_grad * up * gate_sigmoid * (1.0 + gate * (1.0 - gate_sigmoid))).astype(low)
    up_grad = (hidden_grad * gate * gate_sigmoid).astype(low)

    if blocked:
        split = n_dev * pad // 2

        def weight_grad(left, right, route):
            mine = product_left(left[:, :split], right).astype(low)
            theirs = product_left(left[:, split:], right).astype(low)
            shape = (n_dev // 2, pad, right.shape[-1])
            return scatter_sum(mine.reshape(shape), theirs.reshape(shape), route)[:cut]

        def down_scatter():
            blocks = fresh_down.reshape(n_dev, cut_ff, D)
            first = move_blocks([blocks[:, :half_ff]], order, 2)
            second = move_blocks([blocks[:, half_ff:]], order, 2)
            return jnp.concatenate([scatter_sum(*first, 0), scatter_sum(*second, 1)], axis=0)
    else:

        def weight_grad(left, right, route):
            del route
            full_grad = product_left(left, right).astype(low)
            return full_grad

        def down_scatter():
            return fresh_down

    def finish(grad):
        if blocked:
            return grad.reshape(-1)
        flat = grad.reshape(n_dev, -1)
        return lax.psum_scatter(flat, AXES, scatter_dimension=0, tiled=True).astype(wide).reshape(-1)

    d_down = finish(down_scatter())
    d_gate = finish(weight_grad(normed_ffn, gate_grad, 0))
    d_up = finish(weight_grad(normed_ffn, up_grad, 1))
    normed_grad = collect_wide(
        product_right(gate_grad, gate_weight) + product_right(up_grad, up_weight)
    )
    resid_grad, ffn_gain_grad = norm_back(resid, scale_ffn, norm_ffn, normed_grad)
    resid_grad = resid_grad + grad_out
    branch_grad = resid_grad.astype(low)
    d_out = finish(weight_grad(attended, branch_grad, 1))
    attended_grad = (
        collect(product_right(branch_grad, out_weight).astype(low))
        .astype(low)
        .reshape(seqs, block_len, KV_HEADS, GROUP, HEAD_DIM)
    )
    probs = jnp.exp(masked_scores() - log_total)
    probs_grad = jnp.einsum(
        "sckgd,slkd->skgcl", attended_grad, value_heads, preferred_element_type=wide
    )
    inner = jnp.sum(probs * probs_grad, axis=-1, keepdims=True)
    scores_grad = (probs * (probs_grad - inner)).astype(low)
    query_grad = (
        jnp.einsum("skgcl,slkd->sckgd", scores_grad, key_heads, preferred_element_type=wide)
        * score_scale
    )
    key_part = (
        jnp.einsum("skgcl,sckgd->slkd", scores_grad, query_groups, preferred_element_type=wide)
        * score_scale
    )
    value_part = jnp.einsum(
        "skgcl,sckgd->slkd", probs.astype(low), attended_grad, preferred_element_type=wide
    )
    both_part = jnp.concatenate([key_part, value_part], axis=2).astype(low)
    both_part = both_part.reshape(seqs, ctx_size, block_len, 2 * KV).transpose(1, 0, 2, 3)
    both_grad = ctx_scatter(both_part).reshape(seqs, block_len, 2 * KV_HEADS, HEAD_DIM)
    query_low = (
        rotate_back(query_grad.reshape(seqs, block_len, HEADS, HEAD_DIM), cosine, sine)
        .astype(low)
        .reshape(rows, ATTN)
    )
    key_low = rotate_back(both_grad[:, :, :KV_HEADS], cosine, sine).astype(low)
    both_low = jnp.concatenate([key_low, both_grad[:, :, KV_HEADS:].astype(low)], axis=2)
    both_low = both_low.reshape(rows, 2 * KV)
    d_query = finish(weight_grad(normed_attn, query_low, 0))
    d_both = weight_grad(normed_attn, both_low, 1)
    d_key, d_value = finish(d_both[:, :KV]), finish(d_both[:, KV:])
    attn_normed_grad = collect_wide(
        product_right(query_low, query_weight) + product_right(both_low, kv_weight)
    )
    input_grad, attn_gain_grad = norm_back(inputs, scale_attn, norm_attn, attn_normed_grad)
    d_tokens = (input_grad + resid_grad).reshape(seqs, block_len, D)
    attn_gain_sum, ffn_gain_sum = lax.psum((attn_gain_grad, ffn_gain_grad), AXES)
    return (
        output,
        d_tokens,
        attn_gain_sum,
        d_query,
        d_key,
        d_value,
        d_out,
        ffn_gain_sum,
        d_gate,
        d_up,
        d_down,
    )


def solution(mesh):
    one = P(AXES)
    tok = P("dp", "ctx", None)
    ids = P("dp", "ctx")
    in_specs = (tok, ids, ids, P(), one, one, one, one, P(), one, one, one, tok)
    out_specs = (tok, tok, P(), one, one, one, one, P(), one, one, one)
    return jax.shard_map(body, mesh=mesh, in_specs=in_specs, out_specs=out_specs, check_vma=False)
```

time: 976 us -> 1050 us (1.076)
  Pallas kernels: 0 us -> 326 us
  blocking collectives: 180 us -> 39 us
  other arithmetic: 175 us -> 98.1 us
  waiting for transfers between devices: 249 us -> 213 us
  starting transfers between devices: 32.6 us -> 64.8 us
  matrix products: 188 us -> 172 us
  between operations: 16 us -> 3.18 us
    pallas_call x0 -> x4, Pallas kernels: none -> 326 us  [move_blocks(): pl.pallas_call(kernel, out_shape=shapes, in_specs=[pl.BlockSpec(memory_sp...]
    ppermute x0 -> x76, waiting for transfers between devices: none -> 213 us  [swap(): return lax.ppermute(value, AXES, [(i, i ^ mask) for i in range(n)])]
    all_gather x8 -> x0, blocking collectives: 136 us -> none  [the longest x1 47.4 us: forward_weights(): lax.all_gather(w_value, ('dp', 'ctx'), axis=0, tiled=True)]
    all_to_all x7 -> x0, waiting for transfers between devices: 126 us -> none  [the longest x1 38.7 us: reduce_at_end(): lax.all_to_all(blocks[6].astype(jnp.bfloat16), 'ctx', split_axis=1, conca...]
    unnamed x11 -> x0, waiting for transfers between devices: 112 us -> none
    all_gather x4 -> x0, other arithmetic: 86.8 us -> none  [the longest x1 39.9 us: forward_weights(): lax.all_gather(w_out, ('dp', 'ctx'), axis=0, tiled=True)]
    ppermute x0 -> x76, starting transfers between devices: none -> 64.8 us  [swap(): return lax.ppermute(value, AXES, [(i, i ^ mask) for i in range(n)])]
    convert_element_type x10 -> x35, other arithmetic: 3.43 us -> 51.3 us  [the longest x1 27 us: body(): scores_grad = (probs * (probs_grad - inner)).astype(low)]
  transfers between devices with their start and end apart: 17 -> 76, of which waited for: 7 -> 37; matrix products, arithmetic and copies ran while one was open for 40% -> 24% of each run, Pallas kernels for 0% -> 31%
where the time goes in v1:
time: 1050 us
  Pallas kernels  326 us (31%)
  waiting for transfers between devices  213 us (20%)
  matrix products  172 us (16%)
  local copies, waits for them, and re-layouts  131 us (12%)
  other arithmetic  98.1 us (9%)
  starting transfers between devices  64.8 us (6%)
  blocking collectives  39 us (4%)
    pallas_call x4, Pallas kernels, move_blocks(): pl.pallas_call(kernel, out_shape=shapes, in_specs=[pl.BlockSpec(memory_sp...  326 us
    ppermute x76, waiting for transfers between devices, swap(): return lax.ppermute(value, AXES, [(i, i ^ mask) for i in range(n)])  213 us
    ppermute x76, starting transfers between devices, swap(): return lax.ppermute(value, AXES, [(i, i ^ mask) for i in range(n)])  64.8 us
    psum x1, blocking collectives, body(): lax.psum((attn_gain_grad, ffn_gain_grad), AXES)  39 us
    unnamed x229, local copies, waits for them, and re-layouts  38.3 us
    dot_general x10, matrix products, product_right(): lax.dot_general(left, right, (((1,), (1,)), ((), ())), preferred_element_...  30.8 us
    dot_general x9, matrix products, product(): return jnp.dot(left, right, preferred_element_type=wide)  30.5 us
    dot_general x11, matrix products, product_left(): lax.dot_general(left, right, (((0,), (0,)), ((), ())), preferred_element_...  28 us
  transfers between devices with their start and end apart: 76, of which 37 were waited for; matrix products, arithmetic and copies ran while one was open for 24% of the time, Pallas kernels for 31%

profile of v1, /device:TPU:0, one launch (start us, length us, event | category | flops | bytes accessed | tf_op | source)
XLA Modules:
  0.0 1046.4 jit_solution(8042692803820855197)
XLA Ops:
  140.1 29.8 %collective-permute-done.36 = bf16[4,40,960]{2,1,0:T(8,128)(2,1)S(1)} collective-permute-done((bf16[4,40,960]{2,1,0:T(8,128)(2,1)S(1)}, bf16[4,40,960]{2,1,0:T(8,128)(2,1)S(1)}, u32[]{:S(2)}, u32[]{:S(2)}) %collective-permute-start.36) | collective-permute-done | bytes 307232 | tf_op jit(solution)/shard_map/ppermute | solution.py:70
  202.3 14.6 %fusion.124 = (f32[2,5,3,256]{3,2,1,0:T(4,128)S(1)}, f32[2,5,3,256,1024]{3,4,2,1,0:T(8,128)}) fusion(bf16[2,256,5,3,64]{1,4,3,2,0:T(8,128)(2,1)} %bitcast.241, bf16[2,1024,2,5,64]{1,4,3,2,0:T(8,128)(2,1)S(1)} %reshape.389, pred[2,256,1024]{1,2,0:T(8,128)(4,1)S(1)} %copy-done.28), kind=kOutput, calls=%fused_computation.352 | convolution fusion | flops 1030218240 | bytes 34306048 | tf_op jit(solution)/shard_map/sckgd,slkd->skgcl/dot_general | solution.py:325
  216.9 12.8 %fusion.3 = f32[2,5,3,256]{3,2,1,0:T(4,128)S(1)} fusion(f32[2,5,3,256,1024]{3,4,2,1,0:T(8,128)} %get-tuple-element.164, f32[2,5,3,256]{3,2,1,0:T(4,128)S(1)} %get-tuple-element.163), kind=kLoop, calls=%fused_computation.9 | loop fusion | flops 15720960 | bytes 31518720 | tf_op jit(solution)/shard_map/reduce_sum | solution.py:333
  229.7 12.9 %fusion.53 = bf16[2,256,5,3,64]{1,4,3,2,0:T(8,128)(2,1)S(1)} fusion(f32[2,5,3,256,1024]{3,4,2,1,0:T(8,128)} %get-tuple-element.164, f32[2,5,3,256]{3,2,1,0:T(4,128)S(1)} %fusion.3, f32[2,5,3,256]{3,2,1,0:T(4,128)S(1)} %get-tuple-element.163, bf16[2,1024,2,5,64]{1,4,3,2,0:T(8,128)(2,1)S(1)} %reshape.389), kind=kOutput, calls=%fused_computation.112 | convolution fusion | flops 1030717440 | bytes 33832960 | tf_op jit(solution)/shard_map/skgcl,slkd->sckgd/dot_general | solution.py:337
  258.1 81.5 %move_blocks.4 = bf16[32,40,960]{2,1,0:T(8,128)(2,1)} custom-call(s32[32]{0:T(128)} %fusion.104.order_ref, bf16[16,40,960]{2,1,0:T(8,128)(2,1)} %constant_dynamic-update-slice_fusion.53.refs_0_, bf16[16,40,960]{2,1,0:T(8,128)(2,1)} %collective-permute-done.33.refs_1_), custom_call_target="tpu_custom_call" | custom-call | bytes 4915200 | tf_op jit(solution)/shard_map/move_blocks/pallas_call | solution.py:191
  339.6 81.6 %move_blocks.5 = bf16[32,40,960]{2,1,0:T(8,128)(2,1)} custom-call(s32[32]{0:T(128)} %fusion.104.order_ref, bf16[16,40,960]{2,1,0:T(8,128)(2,1)} %slice_dynamic-update-slice_fusion.4.refs_0_, bf16[16,40,960]{2,1,0:T(8,128)(2,1)} %collective-permute-done.38.refs_1_), custom_call_target="tpu_custom_call" | custom-call | bytes 4915200 | tf_op jit(solution)/shard_map/move_blocks/pallas_call | solution.py:191
  437.3 8.2 fusion.13
  445.6 6.9 fusion.129
  488.5 14.0 %fusion.49 = bf16[2,1024,5,64]{1,3,2,0:T(8,128)(2,1)} fusion(f32[2,5,3,256,1024]{3,4,2,1,0:T(8,128)} %get-tuple-element.164, f32[2,5,3,256]{3,2,1,0:T(4,128)S(1)} %log_add_fusion, bf16[2,256,5,3,64]{1,0,4,3,2:T(2,128)(2,1)} %reshape.403), kind=kOutput, calls=%fused_computation.108 | convolution fusion | flops 1023016960 | bytes 33781760 | tf_op jit(solution)/shard_map/skgcl,sckgd->slkd/dot_general | solution.py:415
  502.6 21.3 %fusion = (f32[2,5,3,256]{3,2,1,0:T(4,128)S(1)}, f32[2,5,1024,256,3]{3,2,4,1,0:T(8,128)}) fusion(f32[2,5,3,256,1024]{3,4,2,1,0:T(8,128)} %get-tuple-element.164, f32[2,5,3,256]{3,2,1,0:T(4,128)S(1)} %log_add_fusion, bf16[2,256,5,3,64]{1,0,4,3,2:T(2,128)(2,1)} %reshape.403, bf16[2,1024,2,5,64]{1,4,3,2,0:T(8,128)(2,1)S(1)} %copy-done.3), kind=kOutput, calls=%fused_computation.2 | convolution fusion | flops 1030218240 | bytes 65280000 | tf_op jit(solution)/shard_map/sckgd,slkd->skgcl/dot_general | solution.py:402
  523.9 27.0 %fusion.2 = bf16[2,5,3,256,1024]{3,4,2,1,0:T(8,128)(2,1)} fusion(f32[2,5,1024,256,3]{3,2,4,1,0:T(8,128)} %get-tuple-element.169, f32[2,5,3,256,1024]{3,4,2,1,0:T(8,128)} %get-tuple-element.164, f32[2,5,3,256]{3,2,1,0:T(4,128)S(1)} %get-tuple-element.168, f32[2,5,3,256]{3,2,1,0:T(4,128)S(1)} %log_add_fusion), kind=kLoop, calls=%fused_computation.4 | loop fusion | flops 31457280 | bytes 78704640 | tf_op jit(solution)/shard_map/convert_element_type | solution.py:406
  550.9 8.3 convolution_multiply_fusion
  559.2 11.4 %fusion.52 = bf16[2,1024,5,64]{1,3,2,0:T(8,128)(2,1)} fusion(bf16[2,256,5,3,64]{1,4,3,2,0:T(8,128)(2,1)S(1)} %bitcast.242, bf16[2,5,3,256,1024]{3,4,2,1,0:T(8,128)(2,1)} %fusion.2), kind=kOutput, calls=%fused_computation.109 | convolution fusion | flops 1007943680 | bytes 18022400 | tf_op jit(solution)/shard_map/skgcl,sckgd->slkd/dot_general | solution.py:412
  577.6 7.9 copy.95
  591.0 81.6 %move_blocks.6 = (bf16[16,40,960]{2,1,0:T(8,128)(2,1)}, bf16[16,40,960]{2,1,0:T(8,128)(2,1)}) custom-call(s32[32]{0:T(128)} %fusion.104.order_ref, bf16[32,40,960]{2,1,0:T(8,128)(2,1)} %get-tuple-element.73.refs_0_), custom_call_target="tpu_custom_call" | custom-call | bytes 4915200 | tf_op jit(solution)/shard_map/move_blocks/pallas_call | solution.py:191
  672.6 81.5 %move_blocks.7 = (bf16[16,40,960]{2,1,0:T(8,128)(2,1)}, bf16[16,40,960]{2,1,0:T(8,128)(2,1)}) custom-call(s32[32]{0:T(128)} %fusion.104.order_ref, bf16[32,40,960]{2,1,0:T(8,128)(2,1)} %get-tuple-element.74.refs_0_), custom_call_target="tpu_custom_call" | custom-call | bytes 4915200 | tf_op jit(solution)/shard_map/move_blocks/pallas_call | solution.py:191
  803.4 8.8 collective-permute-done.52
  818.6 16.3 %collective-permute-done.53 = bf16[4,32,960]{2,1,0:T(8,128)(2,1)S(1)} collective-permute-done((bf16[4,32,960]{2,1,0:T(8,128)(2,1)S(1)}, bf16[4,32,960]{2,1,0:T(8,128)(2,1)S(1)}, u32[]{:S(2)}, u32[]{:S(2)}) %collective-permute-start.53) | collective-permute-done | bytes 245792 | tf_op jit(solution)/shard_map/ppermute | solution.py:70
  839.0 12.0 %collective-permute-done.72 = bf16[8,40,960]{2,1,0:T(8,128)(2,1)S(1)} collective-permute-done((bf16[8,40,960]{2,1,0:T(8,128)(2,1)S(1)}, bf16[8,40,960]{2,1,0:T(8,128)(2,1)S(1)}, u32[]{:S(2)}, u32[]{:S(2)}) %collective-permute-start.72) | collective-permute-done | bytes 614432 | tf_op jit(solution)/shard_map/ppermute | solution.py:70
  886.6 39.0 %all-reduce.6 = (f32[960]{0:T(1024)}, f32[960]{0:T(1024)}) all-reduce(f32[960]{0:T(1024)S(1)} %get-tuple-element.66, f32[960]{0:T(1024)S(1)} %copy-done.80), channel_id=1, replica_groups=mesh['dp'=8,'ctx'=4] {'dp','ctx'}, use_global_device_ids=true, to_apply=%region_8.9 | all-reduce | flops 1920 | bytes 15360 | tf_op jit(solution)/shard_map/psum | solution.py:437
  931.0 10.2 collective-permute-done.69
  978.1 13.1 %collective-permute-done.62 = bf16[8,32,2560]{2,1,0:T(8,128)(2,1)} collective-permute-done((bf16[8,32,2560]{2,1,0:T(8,128)(2,1)}, bf16[8,32,2560]{2,1,0:T(8,128)(2,1)}, u32[]{:S(2)}, u32[]{:S(2)}) %collective-permute-start.62) | collective-permute-done | bytes 1310752 | tf_op jit(solution)/shard_map/ppermute | solution.py:70
  993.5 8.7 collective-permute-done.57
  1017.1 15.4 %collective-permute-done.64 = bf16[2,32,2560]{2,1,0:T(8,128)(2,1)S(1)} collective-permute-done((bf16[2,32,2560]{2,1,0:T(8,128)(2,1)S(1)}, bf16[2,32,2560]{2,1,0:T(8,128)(2,1)S(1)}, u32[]{:S(2)}, u32[]{:S(2)}) %collective-permute-start.64) | collective-permute-done | bytes 327712 | tf_op jit(solution)/shard_map/ppermute | solution.py:70
  (597 shorter events, 418.6 us)
Async XLA Ops:
  66.8 52.9 %collective-permute-start.13 = (bf16[16,32,960]{2,1,0:T(8,128)(2,1)}, bf16[16,32,960]{2,1,0:T(8,128)(2,1)}, u32[]{:S(2)}, u32[]{:S(2)}) collective-permute-start(bf16[16,32,960]{2,1,0:T(8,128)(2,1)} %get-tuple-element.109), channel_id=1, source_target_pairs={{0,1},{1,0},{2,3},{3,2},{4,5},{5,4},{6,7},{7,6},{8,9},{9,8},{10,11... | collective-permute-start | bytes 2949128 | tf_op jit(solution)/shard_map/ppermute | solution.py:70
  73.9 27.6 %collective-permute-start.21 = (bf16[4,32,2560]{2,1,0:T(8,128)(2,1)}, bf16[4,32,2560]{2,1,0:T(8,128)(2,1)}, u32[]{:S(2)}, u32[]{:S(2)}) collective-permute-start(bf16[4,32,2560]{2,1,0:T(8,128)(2,1)} %pad_maximum_fusion.8), channel_id=1, source_target_pairs={{0,4},{1,5},{2,6},{3,7},{4,0},{5,1},{6,2},{7,3},{8,12},{9,13},{10,... | collective-permute-start | bytes 1966088 | tf_op jit(solution)/shard_map/ppermute | solution.py:70
  87.1 86.0 %collective-permute-start.18 = (bf16[16,32,960]{2,1,0:T(8,128)(2,1)}, bf16[16,32,960]{2,1,0:T(8,128)(2,1)}, u32[]{:S(2)}, u32[]{:S(2)}) collective-permute-start(bf16[16,32,960]{2,1,0:T(8,128)(2,1)} %get-tuple-element.107), channel_id=1, source_target_pairs={{0,1},{1,0},{2,3},{3,2},{4,5},{5,4},{6,7},{7,6},{8,9},{9,8},{10,11... | collective-permute-start | bytes 2949128 | tf_op jit(solution)/shard_map/ppermute | solution.py:70
  93.3 45.3 %collective-permute-start.7 = (bf16[1,2,256,640]{3,2,1,0:T(8,128)(2,1)S(1)}, bf16[1,2,256,640]{3,2,1,0:T(8,128)(2,1)}, u32[]{:S(2)}, u32[]{:S(2)}) collective-permute-start(bf16[1,2,256,640]{3,2,1,0:T(8,128)(2,1)S(1)} %copy.71), channel_id=1, source_target_pairs={{0,2},{1,3},{2,0},{3,1},{4,6},{5,7},{6,4},{7,5},{8,10},{9,11},{10,... | collective-permute-start | bytes 1966088 | tf_op jit(solution)/shard_map/ppermute | solution.py:70
  99.8 71.1 %collective-permute-start.26 = (bf16[4,32,2560]{2,1,0:T(8,128)(2,1)}, bf16[4,32,2560]{2,1,0:T(8,128)(2,1)S(1)}, u32[]{:S(2)}, u32[]{:S(2)}) collective-permute-start(bf16[4,32,2560]{2,1,0:T(8,128)(2,1)} %pad_maximum_fusion.9), channel_id=1, source_target_pairs={{0,2},{1,3},{2,0},{3,1},{4,6},{5,7},{6,4},{7,5},{8,10},{9,11},{10,... | collective-permute-start | bytes 1966088 | tf_op jit(solution)/shard_map/ppermute | solution.py:70
  131.2 59.6 %collective-permute-start.22 = (bf16[8,32,2560]{2,1,0:T(8,128)(2,1)S(1)}, bf16[8,32,2560]{2,1,0:T(8,128)(2,1)S(1)}, u32[]{:S(2)}, u32[]{:S(2)}) collective-permute-start(bf16[8,32,2560]{2,1,0:T(8,128)(2,1)S(1)} %copy-done.54), channel_id=1, source_target_pairs={{0,2},{1,3},{2,0},{3,1},{4,6},{5,7},{6,4},{7,5},{8,10},{9,11},{10,... | collective-permute-start | bytes 3932168 | tf_op jit(solution)/shard_map/ppermute | solution.py:70
  134.0 35.9 %collective-permute-start.36 = (bf16[4,40,960]{2,1,0:T(8,128)(2,1)S(1)}, bf16[4,40,960]{2,1,0:T(8,128)(2,1)S(1)}, u32[]{:S(2)}, u32[]{:S(2)}) collective-permute-start(bf16[4,40,960]{2,1,0:T(8,128)(2,1)S(1)} %pad_maximum_fusion.21), channel_id=1, source_target_pairs={{0,2},{1,3},{2,0},{3,1},{4,6},{5,7},{6,4},{7,5},{8,10},{9,11},{10,... | collective-permute-start | bytes 921608 | tf_op jit(solution)/shard_map/ppermute | solution.py:70
  138.5 42.4 %collective-permute-start.32 = (bf16[8,40,960]{2,1,0:T(8,128)(2,1)S(1)}, bf16[8,40,960]{2,1,0:T(8,128)(2,1)S(1)}, u32[]{:S(2)}, u32[]{:S(2)}) collective-permute-start(bf16[8,40,960]{2,1,0:T(8,128)(2,1)S(1)} %pad_maximum_fusion.10), channel_id=1, source_target_pairs={{0,2},{1,3},{2,0},{3,1},{4,6},{5,7},{6,4},{7,5},{8,10},{9,11},{10,... | collective-permute-start | bytes 1843208 | tf_op jit(solution)/shard_map/ppermute | solution.py:70
  173.1 76.7 %collective-permute-start.27 = (bf16[8,32,2560]{2,1,0:T(8,128)(2,1)}, bf16[8,32,2560]{2,1,0:T(8,128)(2,1)}, u32[]{:S(2)}, u32[]{:S(2)}) collective-permute-start(bf16[8,32,2560]{2,1,0:T(8,128)(2,1)} %pad_maximum_fusion.5), channel_id=1, source_target_pairs={{0,4},{1,5},{2,6},{3,7},{4,0},{5,1},{6,2},{7,3},{8,12},{9,13},{10,... | collective-permute-start | bytes 3932168 | tf_op jit(solution)/shard_map/ppermute | solution.py:70
  181.8 76.3 %collective-permute-start.33 = (bf16[16,40,960]{2,1,0:T(8,128)(2,1)}, bf16[16,40,960]{2,1,0:T(8,128)(2,1)}, u32[]{:S(2)}, u32[]{:S(2)}) collective-permute-start(bf16[16,40,960]{2,1,0:T(8,128)(2,1)} %constant_dynamic-update-slice_fusion.53.refs_0_), channel_id=1, source_target_pairs={{0,1},{1,0},{2,3},{3,2},{4,5},{5,4},{6,7},{7,6},{8,9},{9,8},{10,11... | collective-permute-start | bytes 3686408 | tf_op jit(solution)/shard_map/ppermute | solution.py:70
  190.8 148.8 %collective-permute-start.38 = (bf16[16,40,960]{2,1,0:T(8,128)(2,1)}, bf16[16,40,960]{2,1,0:T(8,128)(2,1)}, u32[]{:S(2)}, u32[]{:S(2)}) collective-permute-start(bf16[16,40,960]{2,1,0:T(8,128)(2,1)} %slice_dynamic-update-slice_fusion.4.refs_0_), channel_id=1, source_target_pairs={{0,1},{1,0},{2,3},{3,2},{4,5},{5,4},{6,7},{7,6},{8,9},{9,8},{10,11... | collective-permute-start | bytes 3686408 | tf_op jit(solution)/shard_map/ppermute | solution.py:70
  192.6 236.2 %collective-permute-start.23 = (bf16[16,32,2560]{2,1,0:T(8,128)(2,1)}, bf16[16,32,2560]{2,1,0:T(8,128)(2,1)}, u32[]{:S(2)}, u32[]{:S(2)}) collective-permute-start(bf16[16,32,2560]{2,1,0:T(8,128)(2,1)} %get-tuple-element.89), channel_id=1, source_target_pairs={{0,1},{1,0},{2,3},{3,2},{4,5},{5,4},{6,7},{7,6},{8,9},{9,8},{10,11... | collective-permute-start | bytes 7864328 | tf_op jit(solution)/shard_map/ppermute | solution.py:70
  255.2 178.7 %collective-permute-start.28 = (bf16[16,32,2560]{2,1,0:T(8,128)(2,1)}, bf16[16,32,2560]{2,1,0:T(8,128)(2,1)}, u32[]{:S(2)}, u32[]{:S(2)}) collective-permute-start(bf16[16,32,2560]{2,1,0:T(8,128)(2,1)} %get-tuple-element.91), channel_id=1, source_target_pairs={{0,1},{1,0},{2,3},{3,2},{4,5},{5,4},{6,7},{7,6},{8,9},{9,8},{10,11... | collective-permute-start | bytes 7864328 | tf_op jit(solution)/shard_map/ppermute | solution.py:70
  577.1 218.4 %collective-permute-start.51 = (bf16[16,32,960]{2,1,0:T(8,128)(2,1)}, bf16[16,32,960]{2,1,0:T(8,128)(2,1)}, u32[]{:S(2)}, u32[]{:S(2)}) collective-permute-start(bf16[16,32,960]{2,1,0:T(8,128)(2,1)} %bitcast.59), channel_id=1, source_target_pairs={{0,1},{1,0},{2,3},{3,2},{4,5},{5,4},{6,7},{7,6},{8,9},{9,8},{10,11... | collective-permute-start | bytes 2949128 | tf_op jit(solution)/shard_map/ppermute | solution.py:70
  754.1 43.8 %collective-permute-start.66 = (bf16[16,40,960]{2,1,0:T(8,128)(2,1)}, bf16[16,40,960]{2,1,0:T(8,128)(2,1)}, u32[]{:S(2)}, u32[]{:S(2)}) collective-permute-start(bf16[16,40,960]{2,1,0:T(8,128)(2,1)} %get-tuple-element.28), channel_id=1, source_target_pairs={{0,1},{1,0},{2,3},{3,2},{4,5},{5,4},{6,7},{7,6},{8,9},{9,8},{10,11... | collective-permute-start | bytes 3686408 | tf_op jit(solution)/shard_map/ppermute | solution.py:70
  754.1 46.7 %collective-permute-start.71 = (bf16[16,40,960]{2,1,0:T(8,128)(2,1)}, bf16[16,40,960]{2,1,0:T(8,128)(2,1)}, u32[]{:S(2)}, u32[]{:S(2)}) collective-permute-start(bf16[16,40,960]{2,1,0:T(8,128)(2,1)} %get-tuple-element.30), channel_id=1, source_target_pairs={{0,1},{1,0},{2,3},{3,2},{4,5},{5,4},{6,7},{7,6},{8,9},{9,8},{10,11... | collective-permute-start | bytes 3686408 | tf_op jit(solution)/shard_map/ppermute | solution.py:70
  754.6 193.7 %collective-permute-start.61 = (bf16[16,32,2560]{2,1,0:T(8,128)(2,1)}, bf16[16,32,2560]{2,1,0:T(8,128)(2,1)}, u32[]{:S(2)}, u32[]{:S(2)}) collective-permute-start(bf16[16,32,2560]{2,1,0:T(8,128)(2,1)} %bitcast.284), channel_id=1, source_target_pairs={{0,1},{1,0},{2,3},{3,2},{4,5},{5,4},{6,7},{7,6},{8,9},{9,8},{10,11... | collective-permute-start | bytes 7864328 | tf_op jit(solution)/shard_map/ppermute | solution.py:70
  793.0 173.5 %collective-permute-start.56 = (bf16[16,32,2560]{2,1,0:T(8,128)(2,1)}, bf16[16,32,2560]{2,1,0:T(8,128)(2,1)}, u32[]{:S(2)}, u32[]{:S(2)}) collective-permute-start(bf16[16,32,2560]{2,1,0:T(8,128)(2,1)} %bitcast.283), channel_id=1, source_target_pairs={{0,1},{1,0},{2,3},{3,2},{4,5},{5,4},{6,7},{7,6},{8,9},{9,8},{10,11... | collective-permute-start | bytes 7864328 | tf_op jit(solution)/shard_map/ppermute | solution.py:70
  835.9 35.2 %collective-permute-start.40 = (bf16[1,2,256,640]{2,3,1,0:T(8,128)(2,1)}, bf16[1,2,256,640]{2,3,1,0:T(8,128)(2,1)}, u32[]{:S(2)}, u32[]{:S(2)}) collective-permute-start(bf16[1,2,256,640]{2,3,1,0:T(8,128)(2,1)} %slice.489), channel_id=1, source_target_pairs={{0,2},{1,3},{2,0},{3,1},{4,6},{5,7},{6,4},{7,5},{8,10},{9,11},{10,... | collective-permute-start | bytes 1966088 | tf_op jit(solution)/shard_map/ppermute | solution.py:70
  855.5 70.1 %collective-permute-start.68 = (bf16[4,40,960]{2,1,0:T(8,128)(2,1)}, bf16[4,40,960]{2,1,0:T(8,128)(2,1)}, u32[]{:S(2)}, u32[]{:S(2)}) collective-permute-start(bf16[4,40,960]{2,1,0:T(8,128)(2,1)} %slice.562), channel_id=1, source_target_pairs={{0,4},{1,5},{2,6},{3,7},{4,0},{5,1},{6,2},{7,3},{8,12},{9,13},{10,... | collective-permute-start | bytes 921608 | tf_op jit(solution)/shard_map/ppermute | solution.py:70
  867.6 61.3 %collective-permute-start.73 = (bf16[4,40,960]{2,1,0:T(8,128)(2,1)}, bf16[4,40,960]{2,1,0:T(8,128)(2,1)}, u32[]{:S(2)}, u32[]{:S(2)}) collective-permute-start(bf16[4,40,960]{2,1,0:T(8,128)(2,1)} %slice.573), channel_id=1, source_target_pairs={{0,2},{1,3},{2,0},{3,1},{4,6},{5,7},{6,4},{7,5},{8,10},{9,11},{10,... | collective-permute-start | bytes 921608 | tf_op jit(solution)/shard_map/ppermute | solution.py:70
  876.6 74.3 %collective-permute-start.46 = (bf16[16,32,640]{2,1,0:T(8,128)(2,1)}, bf16[16,32,640]{2,1,0:T(8,128)(2,1)}, u32[]{:S(2)}, u32[]{:S(2)}) collective-permute-start(bf16[16,32,640]{2,1,0:T(8,128)(2,1)} %bitcast.56), channel_id=1, source_target_pairs={{0,1},{1,0},{2,3},{3,2},{4,5},{5,4},{6,7},{7,6},{8,9},{9,8},{10,11... | collective-permute-start | bytes 1966088 | tf_op jit(solution)/shard_map/ppermute | solution.py:70
  963.3 27.9 %collective-permute-start.62 = (bf16[8,32,2560]{2,1,0:T(8,128)(2,1)}, bf16[8,32,2560]{2,1,0:T(8,128)(2,1)}, u32[]{:S(2)}, u32[]{:S(2)}) collective-permute-start(bf16[8,32,2560]{2,1,0:T(8,128)(2,1)} %pad_maximum_fusion.6), channel_id=1, source_target_pairs={{0,4},{1,5},{2,6},{3,7},{4,0},{5,1},{6,2},{7,3},{8,12},{9,13},{10,... | collective-permute-start | bytes 3932168 | tf_op jit(solution)/shard_map/ppermute | solution.py:70
  970.2 32.0 %collective-permute-start.57 = (bf16[8,32,2560]{2,1,0:T(8,128)(2,1)}, bf16[8,32,2560]{2,1,0:T(8,128)(2,1)}, u32[]{:S(2)}, u32[]{:S(2)}) collective-permute-start(bf16[8,32,2560]{2,1,0:T(8,128)(2,1)} %slice.537), channel_id=1, source_target_pairs={{0,2},{1,3},{2,0},{3,1},{4,6},{5,7},{6,4},{7,5},{8,10},{9,11},{10,... | collective-permute-start | bytes 3932168 | tf_op jit(solution)/shard_map/ppermute | solution.py:70
  (143 other events, 1594.5 us)

commit v2 on v1

v2 whole, which is shorter than its diff:
```python
import jax
import jax.numpy as jnp
from jax import lax
from jax.experimental import pallas as pl
from jax.experimental.pallas import tpu as pltpu
from jax.sharding import PartitionSpec as P

D = 960
HEADS = 15
KV_HEADS = 5
HEAD_DIM = 64
FF = 2560
GROUP = HEADS // KV_HEADS
ATTN = HEADS * HEAD_DIM
KV = KV_HEADS * HEAD_DIM
AXES = ("dp", "ctx")
CORE, FIRST, SECOND = 1, 2, 4

norm_eps = 1e-05
rope_base = 100000.0
mask_fill = -1000000000.0
low = jnp.bfloat16
wide = jnp.float32


def rms_scale(values):
    return lax.rsqrt(jnp.mean(values * values, axis=-1, keepdims=True) + norm_eps)


def norm_back(values, scale, gain, grad):
    gain_grad = jnp.sum(grad * values * scale, axis=0)
    weighted = grad * gain
    inner = jnp.mean(weighted * values, axis=-1, keepdims=True)
    return (scale * weighted - values * (scale * scale * scale) * inner, gain_grad)


def rope_tables(position):
    freqs = rope_base ** (-jnp.arange(0, HEAD_DIM, 2, dtype=wide) / HEAD_DIM)
    angles = freqs[:, None] * position.astype(wide)[None, :]
    angles = jnp.concatenate([angles, angles], axis=0)
    return jnp.cos(angles), jnp.sin(angles)


def by_head(values):
    return values.reshape(-1, HEAD_DIM, values.shape[-1])


def rotate(values, cosine, sine):
    values = by_head(values)
    half = HEAD_DIM // 2
    turned = jnp.concatenate([-values[:, half:], values[:, :half]], axis=1)
    return (values * cosine + turned * sine).reshape(-1, values.shape[-1])


def rotate_back(grad, cosine, sine):
    grad = by_head(grad)
    half = HEAD_DIM // 2
    scaled = grad * sine
    turned = jnp.concatenate([scaled[:, half:], -scaled[:, :half]], axis=1)
    return (grad * cosine + turned).reshape(-1, grad.shape[-1])


def product(left, right):
    return jnp.dot(left, right, preferred_element_type=wide)


def product_left(left, right):
    return lax.dot_general(left, right, (((0,), (0,)), ((), ())), preferred_element_type=wide)


def product_right(left, right):
    return lax.dot_general(left, right, (((1,), (1,)), ((), ())), preferred_element_type=wide)


def swap(value, mask):
    n = lax.axis_size(AXES)
    return lax.ppermute(value, AXES, [(i, i ^ mask) for i in range(n)])


def add_low(left, right):
    return (left.astype(wide) + right.astype(wide)).astype(low)


def far_masks():
    n = lax.axis_size(AXES)
    masks, m = [], 8
    while m < n:
        masks.append(m)
        m *= 2
    return masks


def block_owner(place):
    far = far_masks()
    owner = jnp.zeros_like(place)
    for bit, mask in enumerate(far + [SECOND, FIRST, CORE]):
        owner = owner | (((place >> bit) & 1) * mask)
    return owner


def tie(value, deps):
    if not deps:
        return value
    return lax.optimization_barrier((value, tuple(deps)))[0]


def gather_units(units):
    far_done, near_done, results = [], [], []
    for unit in units:
        now = [tie(piece[None], far_done) for piece, _ in unit]
        for mask in far_masks():
            came = [swap(value, mask) for value in now]
            now = [jnp.concatenate(pair, axis=0) for pair in zip(now, came)]
            far_done = came
        now = [tie(value, near_done) for value in now]
        n = now[0].shape[0]
        routes = [route for _, route in unit]
        side = [swap(v, FIRST if r else SECOND) for v, r in zip(now, routes)]
        two = [jnp.concatenate(pair, axis=0) for pair in zip(now, side)]
        rest = [swap(v, SECOND if r else FIRST) for v, r in zip(two, routes)]
        near_done = rest
        half = [
            jnp.concatenate([v, e[:n], d, e[n:]] if r else [t, e], axis=0)
            for v, d, t, e, r in zip(now, side, two, rest, routes)
        ]
        results.append([(h, swap(h, CORE)) for h in half])
    return results


def scatter_core(terms):
    return [(add_low(mine, swap(theirs, CORE)), route) for mine, theirs, route in terms]


def scatter_near(terms, deps):
    out, first_came, last_came = [], [], []
    mid = []
    for now, route in terms:
        n = now.shape[0] // 4
        if route == 0:
            keep, send, mask, then = now[: 2 * n], now[2 * n :], FIRST, SECOND
        else:
            send = jnp.concatenate([now[n : 2 * n], now[3 * n :]], axis=0)
            keep = jnp.concatenate([now[:n], now[2 * n : 3 * n]], axis=0)
            mask, then = SECOND, FIRST
        came = swap(tie(send, deps), mask)
        first_came.append(came)
        mid.append((add_low(keep, came), then))
    for now, then in mid:
        n = now.shape[0] // 2
        came = swap(now[n:], then)
        last_came.append(came)
        out.append(add_low(now[:n], came))
    return out, first_came, last_came


def scatter_far(terms):
    for mask in far_masks()[::-1]:
        n = terms[0].shape[0] // 2
        came = [swap(now[n:], mask) for now in terms]
        terms = [now[:n].astype(wide) + c.astype(wide) for now, c in zip(terms, came)]
        if n > 1:
            terms = [now.astype(low) for now in terms]
    return [now[0] for now in terms]


def sum_all(value):
    n, mask = lax.axis_size(AXES), 1
    while mask < n:
        value = value + swap(value, mask)
        mask *= 2
    return value


def ctx_masks():
    m, masks = lax.axis_size("ctx") // 2, []
    while m >= 1:
        masks.append(m)
        m //= 2
    return masks


def ctx_gather(value):
    now = value[None]
    for mask in ctx_masks():
        now = jnp.concatenate([now, swap(now, mask)], axis=0)
    return now


def ctx_scatter(value):
    now = value
    for mask in ctx_masks()[::-1]:
        n = now.shape[0] // 2
        now = now[:n].astype(wide) + swap(now[n:], mask).astype(wide)
        if n > 1:
            now = now.astype(low)
    return now[0]


def ctx_owner(places):
    owner = jnp.zeros_like(places)
    for bit, mask in enumerate(ctx_masks()):
        owner = owner | (((places >> bit) & 1) * mask)
    return owner


def whole_spec():
    return pl.BlockSpec(memory_space=pltpu.VMEM)


def join_blocks(parts, order):
    (a, b), (c, d) = parts
    half, top, columns = a.shape
    bottom = c.shape[1]

    def kernel(order_ref, a_ref, b_ref, c_ref, d_ref, out_ref):
        def step(p, _):
            near, far = order_ref[p], order_ref[p + half]
            out_ref[near, :top, :] = a_ref[p]
            out_ref[near, top:, :] = c_ref[p]
            out_ref[far, :top, :] = b_ref[p]
            out_ref[far, top:, :] = d_ref[p]
            return 0

        lax.fori_loop(0, half, step, 0)

    shape = (2 * half, top + bottom, columns)
    return pl.pallas_call(
        kernel,
        out_shape=jax.ShapeDtypeStruct(shape, a.dtype),
        in_specs=[pl.BlockSpec(memory_space=pltpu.SMEM)] + [whole_spec()] * 4,
        out_specs=whole_spec(),
        compiler_params=pltpu.CompilerParams(vmem_limit_bytes=24 * 2**20),
        cost_estimate=pl.CostEstimate(
            flops=0, bytes_accessed=4 * shape[0] * shape[1] * columns, transcendentals=0
        ),
        name="join_blocks",
    )(order, a, b, c, d)


def part_blocks(value, order, top):
    total, tall, columns = value.shape
    half = total // 2

    def kernel(order_ref, in_ref, a_ref, b_ref, c_ref, d_ref):
        def step(p, _):
            near, far = order_ref[p], order_ref[p + half]
            a_ref[p] = in_ref[near, :top, :]
            c_ref[p] = in_ref[near, top:, :]
            b_ref[p] = in_ref[far, :top, :]
            d_ref[p] = in_ref[far, top:, :]
            return 0

        lax.fori_loop(0, half, step, 0)

    first = jax.ShapeDtypeStruct((half, top, columns), value.dtype)
    second = jax.ShapeDtypeStruct((half, tall - top, columns), value.dtype)
    return pl.pallas_call(
        kernel,
        out_shape=[first, first, second, second],
        in_specs=[pl.BlockSpec(memory_space=pltpu.SMEM), whole_spec()],
        out_specs=[whole_spec()] * 4,
        compiler_params=pltpu.CompilerParams(vmem_limit_bytes=24 * 2**20),
        cost_estimate=pl.CostEstimate(
            flops=0, bytes_accessed=4 * value.size, transcendentals=0
        ),
        name="part_blocks",
    )(order, value)


def head_rows(ref, head):
    return ref[head * HEAD_DIM : (head + 1) * HEAD_DIM, :]


def key_blocks(kv_ref, start):
    blocks = [kv_ref[b, start : start + HEAD_DIM, :] for b in range(kv_ref.shape[0])]
    return jnp.concatenate(blocks, axis=1)


def turn(value):
    return value.astype(wide).T.astype(low)


def attend_kernel(q_ref, kv_ref, bias_ref, o_ref, lse_ref):
    for g in range(KV_HEADS):
        keys = turn(key_blocks(kv_ref, g * HEAD_DIM))
        values_t = key_blocks(kv_ref, KV + g * HEAD_DIM)
        for h in range(g * GROUP, (g + 1) * GROUP):
            scores = product(keys, head_rows(q_ref, h)) + bias_ref[0]
            top = jnp.max(scores, axis=0, keepdims=True)
            weight = jnp.exp(scores - top)
            total = jnp.sum(weight, axis=0, keepdims=True)
            mixed = product(values_t, weight.astype(low)) / total
            o_ref[h * HEAD_DIM : (h + 1) * HEAD_DIM, :] = mixed.astype(low)
            lse_ref[0, h : h + 1, :] = top + jnp.log(total)


def attend_back_kernel(q_ref, kv_ref, bias_ref, o_ref, lse_ref, do_ref, dq_ref, dkv_ref):
    width = q_ref.shape[1]
    for g in range(KV_HEADS):
        keys_t = key_blocks(kv_ref, g * HEAD_DIM)
        keys = turn(keys_t)
        values = turn(key_blocks(kv_ref, KV + g * HEAD_DIM))
        key_grad, value_grad = None, None
        for h in range(g * GROUP, (g + 1) * GROUP):
            query, grad = head_rows(q_ref, h), head_rows(do_ref, h)
            scores = product(keys, query) + bias_ref[0]
            probs = jnp.exp(scores - lse_ref[0, h : h + 1, :])
            inner = jnp.sum(
                grad.astype(wide) * head_rows(o_ref, h).astype(wide), axis=0, keepdims=True
            )
            scores_grad = (probs * (product(values, grad) - inner)).astype(low)
            dq_ref[h * HEAD_DIM : (h + 1) * HEAD_DIM, :] = product(keys_t, scores_grad)
            from_keys = product_right(scores_grad, query)
            from_values = product_right(probs.astype(low), grad)
            key_grad = from_keys if key_grad is None else key_grad + from_keys
            value_grad = from_values if value_grad is None else value_grad + from_values
        for start, value in ((g * HEAD_DIM, key_grad), (KV + g * HEAD_DIM, value_grad)):
            turned = value.T.astype(low)
            for b in range(kv_ref.shape[0]):
                dkv_ref[b, start : start + HEAD_DIM, :] = turned[:, b * width : (b + 1) * width]


def attention_specs(blocks, block_len, length):
    columns = pl.BlockSpec((ATTN, block_len), lambda s: (0, s))
    pairs = pl.BlockSpec((blocks, 2 * KV, block_len), lambda s: (0, 0, s))
    bias = pl.BlockSpec((1, length, block_len), lambda s: (s, 0, 0))
    logs = pl.BlockSpec((1, HEADS, block_len), lambda s: (s, 0, 0))
    return columns, pairs, bias, logs


def attend(query_t, pairs_t, bias):
    seqs, length, block_len = bias.shape
    columns, pairs, bias_spec, logs = attention_specs(pairs_t.shape[0], block_len, length)
    work = seqs * HEADS * length * block_len
    return pl.pallas_call(
        attend_kernel,
        grid=(seqs,),
        in_specs=[columns, pairs, bias_spec],
        out_specs=[columns, logs],
        out_shape=[
            jax.ShapeDtypeStruct(query_t.shape, low),
            jax.ShapeDtypeStruct((seqs, HEADS, block_len), wide),
        ],
        compiler_params=pltpu.CompilerParams(vmem_limit_bytes=40 * 2**20),
        cost_estimate=pl.CostEstimate(
            flops=4 * work * HEAD_DIM, bytes_accessed=8 * 2**20, transcendentals=work
        ),
        name="attend",
    )(query_t, pairs_t, bias)


def attend_back(query_t, pairs_t, bias, mixed_t, logs_all, grad_t):
    seqs, length, block_len = bias.shape
    columns, pairs, bias_spec, logs = attention_specs(pairs_t.shape[0], block_len, length)
    work = seqs * HEADS * length * block_len
    return pl.pallas_call(
        attend_back_kernel,
        grid=(seqs,),
        in_specs=[columns, pairs, bias_spec, columns, logs, columns],
        out_specs=[columns, pairs],
        out_shape=[
            jax.ShapeDtypeStruct(query_t.shape, wide),
            jax.ShapeDtypeStruct(pairs_t.shape, low),
        ],
        compiler_params=pltpu.CompilerParams(vmem_limit_bytes=48 * 2**20),
        cost_estimate=pl.CostEstimate(
            flops=10 * work * HEAD_DIM, bytes_accessed=14 * 2**20, transcendentals=work
        ),
        name="attend_back",
    )(query_t, pairs_t, bias, mixed_t, logs_all, grad_t)


def body(
    tokens,
    segment_ids,
    positions,
    norm_attn,
    w_query,
    w_key,
    w_value,
    w_out,
    norm_ffn,
    w_gate,
    w_up,
    w_down,
    cotangent,
):
    seqs, block_len, width = tokens.shape
    n_dev = lax.axis_size(AXES)
    ctx_size = lax.axis_size("ctx")
    me = lax.axis_index(AXES)
    rows = seqs * block_len
    length = block_len * ctx_size
    score_scale = HEAD_DIM ** (-0.5)
    ctx_here = lax.axis_index("ctx")
    places = jnp.arange(n_dev, dtype=jnp.int32)
    blocked = n_dev >= 8 and D % n_dev == 0 and FF % (16 * n_dev) == 0

    if blocked:
        cut, cut_ff = D // n_dev, FF // n_dev
        pad = -(-cut // 16) * 16
        top_ff = (cut_ff * 3 // 5) // 8 * 8
        order = block_owner(places) ^ me
        slot = jnp.arange(n_dev * pad, dtype=jnp.int32)
        source = jnp.where(slot % pad < cut, jnp.repeat(order, pad) * cut + slot % pad, -1)
        perm = (jnp.arange(D, dtype=jnp.int32)[:, None] == source[None, :]).astype(low)

        def spread(value):
            return product(value, perm).astype(low)

        def spread_t(value):
            return product_left(value, perm).astype(low)

        def collect(value):
            return product_right(value, perm)

        def collect_t(value):
            return product_right(perm, value)

        def rows_of(shard, columns):
            return jnp.pad(shard.reshape(cut, columns), ((0, pad - cut), (0, 0)))

        down_block = w_down.reshape(cut_ff, D)
        pairs_block = jnp.concatenate([rows_of(w_key, KV), rows_of(w_value, KV)], axis=1)
        units = gather_units(
            [
                [(rows_of(w_query, ATTN), 0), (pairs_block, 1)],
                [(down_block[:top_ff], 0), (rows_of(w_out, D), 1)],
                [(rows_of(w_gate, FF), 0), (rows_of(w_up, FF), 1)],
                [(down_block[top_ff:], 1)],
            ]
        )

        def stacked(halves):
            return jnp.concatenate(halves, axis=0).reshape(-1, halves[0].shape[-1])

        query_weight, kv_weight = stacked(units[0][0]), stacked(units[0][1])
        out_weight = stacked(units[1][1])
        gate_weight, up_weight = stacked(units[2][0]), stacked(units[2][1])
        down_weight = join_blocks((units[1][0], units[3][0]), order).reshape(FF, D)
    else:
        perm = None

        def spread(value):
            return value

        def spread_t(value):
            return value.T

        def collect(value):
            return value.astype(wide)

        def collect_t(value):
            return value.T

        def whole(shard, columns):
            return lax.all_gather(shard, AXES, axis=0, tiled=True).reshape(-1, columns)

        query_weight = whole(w_query, ATTN)
        kv_weight = jnp.concatenate([whole(w_key, KV), whole(w_value, KV)], axis=1)
        out_weight = whole(w_out, D)
        gate_weight, up_weight = whole(w_gate, FF), whole(w_up, FF)
        down_weight = whole(w_down, D)

    def collect_wide(value):
        if perm is None:
            return value
        high = lax.reduce_precision(value, 8, 7)
        return collect(high.astype(low)) + collect((value - high).astype(low))

    inputs = tokens.astype(wide).reshape(rows, D)
    grad_out = cotangent.astype(wide).reshape(rows, D)
    scale_attn = rms_scale(inputs)
    normed_attn = spread((inputs * scale_attn * norm_attn).astype(low))
    cosine, sine = rope_tables(positions.reshape(rows))
    segment_all = ctx_gather(segment_ids).transpose(1, 0, 2).reshape(seqs, length)
    query_index = ctx_here * block_len + jnp.arange(block_len, dtype=jnp.int32)
    key_block = ctx_owner(jnp.arange(ctx_size, dtype=jnp.int32)) ^ ctx_here
    key_index = (
        key_block[:, None] * block_len + jnp.arange(block_len, dtype=jnp.int32)[None, :]
    ).reshape(length)
    allowed = (segment_all[:, :, None] == segment_ids[:, None, :]) & (
        key_index[None, :, None] <= query_index[None, None, :]
    )
    bias = jnp.where(allowed, 0.0, mask_fill)

    def across(weight):
        return lax.dot_general(
            weight, normed_attn, (((0,), (1,)), ((), ())), preferred_element_type=wide
        )

    pairs_t = across(kv_weight)
    pairs_t = jnp.concatenate(
        [rotate(pairs_t[:KV], cosine, sine).astype(low), pairs_t[KV:].astype(low)], axis=0
    )
    pairs_all = ctx_gather(pairs_t)
    query_t = (rotate(across(query_weight), cosine, sine) * score_scale).astype(low)
    mixed_t, logs = attend(query_t, pairs_all, bias)
    attended = spread_t(mixed_t)
    resid = inputs + product(attended, out_weight)
    scale_ffn = rms_scale(resid)
    normed_ffn = spread((resid * scale_ffn * norm_ffn).astype(low))
    gate = product(normed_ffn, gate_weight)
    up = product(normed_ffn, up_weight)
    gate_sigmoid = jax.nn.sigmoid(gate)
    hidden = (gate * gate_sigmoid * up).astype(low)
    output = (resid + product(hidden, down_weight)).astype(low).reshape(seqs, block_len, D)

    down_grad = cotangent.reshape(rows, D)
    fresh_down = product_left(hidden, down_grad).astype(low)
    hidden_grad = product_right(down_grad, down_weight)
    gate_grad = (hidden_grad * up * gate_sigmoid * (1.0 + gate * (1.0 - gate_sigmoid))).astype(low)
    up_grad = (hidden_grad * gate * gate_sigmoid).astype(low)

    if blocked:
        split = n_dev * pad // 2

        def terms(left, right, contract, route):
            dims = (((0,), (contract,)), ((), ()))
            both = []
            for piece in (left[:, :split], left[:, split:]):
                grad = lax.dot_general(piece, right, dims, preferred_element_type=wide).astype(low)
                both.append(grad.reshape(n_dev // 2, pad, -1))
            return (*both, route)

        def flat(grad):
            return grad[:cut].reshape(-1)

        parted = part_blocks(fresh_down.reshape(n_dev, cut_ff, D), order, top_ff)
        core_down = scatter_core([(parted[0], parted[1], 0), (parted[2], parted[3], 1)])
        core_pair = scatter_core(
            [terms(normed_ffn, gate_grad, 0, 0), terms(normed_ffn, up_grad, 0, 1)]
        )
        near_down, _, last_down = scatter_near(core_down, [])
        near_pair, first_pair, last_pair = scatter_near(core_pair, last_down)
        d_down = jnp.concatenate(scatter_far(near_down), axis=0).reshape(-1)
        d_gate, d_up = [flat(g) for g in scatter_far(near_pair)]
    else:

        def finish(left, right, contract):
            grad = lax.dot_general(
                left, right, (((0,), (contract,)), ((), ())), preferred_element_type=wide
            )
            return scatter_whole(grad.astype(low))

        def scatter_whole(grad):
            grad = grad.reshape(n_dev, -1)
            return lax.psum_scatter(grad, AXES, scatter_dimension=0, tiled=True).astype(wide)

        d_down = scatter_whole(fresh_down).reshape(-1)
        d_gate = finish(normed_ffn, gate_grad, 0).reshape(-1)
        d_up = finish(normed_ffn, up_grad, 0).reshape(-1)
        last_down, first_pair, last_pair = [], [], []
    normed_grad = collect_wide(
        product_right(gate_grad, gate_weight) + product_right(up_grad, up_weight)
    )
    resid_grad, ffn_gain_grad = norm_back(resid, scale_ffn, norm_ffn, normed_grad)
    resid_grad = resid_grad + grad_out
    branch_grad = resid_grad.astype(low)
    grad_t = collect_t(product_right(branch_grad, out_weight).astype(low)).astype(low)
    grad_t = tie(grad_t, last_down)
    query_grad_t, pairs_part = attend_back(query_t, pairs_all, bias, mixed_t, logs, grad_t)
    pairs_grad = ctx_scatter(pairs_part)
    query_low = rotate_back(query_grad_t * score_scale, cosine, sine).astype(low)
    pairs_low = jnp.concatenate(
        [rotate_back(pairs_grad[:KV], cosine, sine).astype(low), pairs_grad[KV:].astype(low)],
        axis=0,
    )
    if blocked:
        core_out = scatter_core([terms(attended, branch_grad, 0, 1)])
        near_out, _, last_out = scatter_near(core_out, last_pair)
        core_last = scatter_core(
            [terms(normed_attn, query_low, 1, 0), terms(normed_attn, pairs_low, 1, 1)]
        )
        near_last, _, _ = scatter_near(core_last, last_out)
        d_out = flat(scatter_far(near_out)[0])
        d_query, d_pairs = scatter_far(near_last)
        d_query, d_key, d_value = flat(d_query), flat(d_pairs[:, :KV]), flat(d_pairs[:, KV:])
    else:
        d_out = finish(attended, branch_grad, 0).reshape(-1)
        d_query = finish(normed_attn, query_low, 1).reshape(-1)
        d_key = finish(normed_attn, pairs_low[:KV], 1).reshape(-1)
        d_value = finish(normed_attn, pairs_low[KV:], 1).reshape(-1)

    def back_through(grad_t, weight):
        return lax.dot_general(
            grad_t, weight, (((0,), (1,)), ((), ())), preferred_element_type=wide
        )

    attn_normed_grad = collect_wide(
        back_through(query_low, query_weight) + back_through(pairs_low, kv_weight)
    )
    input_grad, attn_gain_grad = norm_back(inputs, scale_attn, norm_attn, attn_normed_grad)
    d_tokens = (input_grad + resid_grad).reshape(seqs, block_len, D)
    attn_gain_sum, ffn_gain_sum = sum_all(attn_gain_grad), sum_all(ffn_gain_grad)
    return (
        output,
        d_tokens,
        attn_gain_sum,
        d_query,
        d_key,
        d_value,
        d_out,
        ffn_gain_sum,
        d_gate,
        d_up,
        d_down,
    )


def solution(mesh):
    one = P(AXES)
    tok = P("dp", "ctx", None)
    ids = P("dp", "ctx")
    in_specs = (tok, ids, ids, P(), one, one, one, one, P(), one, one, one, tok)
    out_specs = (tok, tok, P(), one, one, one, one, P(), one, one, one)
    return jax.shard_map(body, mesh=mesh, in_specs=in_specs, out_specs=out_specs, check_vma=False)
```

time: 1050 us -> 584 us (0.56)
  Pallas kernels: 326 us -> 50 us
  matrix products: 172 us -> 83.8 us
  local copies, waits for them, and re-layouts: 131 us -> 76.3 us
  other arithmetic: 98.1 us -> 49.4 us
  blocking collectives: 39 us -> 0 us
  waiting for transfers between devices: 213 us -> 237 us
  starting transfers between devices: 64.8 us -> 79.7 us
    pallas_call x4, Pallas kernels: 326 us -> 50 us  [the longest x1 24.8 us: attend_back(): pl.pallas_call(attend_back_kernel, grid=(seqs,), in_specs=[columns, pairs...]
    dot_general x6 -> x14, matrix products: 82.5 us -> 32.8 us  [the longest x10 24.9 us: terms(): lax.dot_general(piece, right, dims, preferred_element_type=wide).astype(low)]
    psum x1 -> x0, blocking collectives: 39 us -> none  [body(): lax.psum((attn_gain_grad, ffn_gain_grad), AXES)]
    convert_element_type x13 -> x11, other arithmetic: 29.8 us -> 3.59 us  [the longest x7 2.17 us: scatter_far(): terms = [now.astype(low) for now in terms]]
    ppermute x76 -> x86, waiting for transfers between devices: 213 us -> 237 us  [swap(): return lax.ppermute(value, AXES, [(i, i ^ mask) for i in range(n)])]
    dot_general x11 -> x2, matrix products: 28 us -> 5.9 us  [product_left(): lax.dot_general(left, right, (((0,), (0,)), ((), ())), preferred_element_...]
    unnamed x229 -> x170, local copies, waits for them, and re-layouts: 38.3 us -> 20.1 us
    ppermute x76 -> x86, starting transfers between devices: 64.8 us -> 79.7 us  [swap(): return lax.ppermute(value, AXES, [(i, i ^ mask) for i in range(n)])]
  transfers between devices with their start and end apart: 76 -> 86, of which waited for: 37 -> 41; matrix products, arithmetic and copies ran while one was open for 24% -> 28% of each run, Pallas kernels for 31% -> 9%
where the time goes in v2:
time: 584 us; the launch traced here: 579 us
  waiting for transfers between devices  237 us (41%)
  matrix products  83.8 us (14%)
  starting transfers between devices  79.7 us (14%)
  local copies, waits for them, and re-layouts  76.3 us (13%)
  Pallas kernels  50 us (9%)
  other arithmetic  49.4 us (8%)
    ppermute x86, waiting for transfers between devices, swap(): return lax.ppermute(value, AXES, [(i, i ^ mask) for i in range(n)])  237 us
    ppermute x86, starting transfers between devices, swap(): return lax.ppermute(value, AXES, [(i, i ^ mask) for i in range(n)])  79.7 us
    dot_general x10, matrix products, terms(): lax.dot_general(piece, right, dims, preferred_element_type=wide).astype(low)  24.9 us
    pallas_call x1, Pallas kernels, attend_back(): pl.pallas_call(attend_back_kernel, grid=(seqs,), in_specs=[columns, pairs...  24.8 us
    dot_general x8, matrix products, product_right(): lax.dot_general(left, right, (((1,), (1,)), ((), ())), preferred_element_...  23.2 us
    dot_general x6, matrix products, product(): return jnp.dot(left, right, preferred_element_type=wide)  21.9 us
    pallas_call x1, Pallas kernels, attend(): pl.pallas_call(attend_kernel, grid=(seqs,), in_specs=[columns, pairs, bia...  20.9 us
    unnamed x170, local copies, waits for them, and re-layouts  20.1 us
  transfers between devices with their start and end apart: 86, of which 41 were waited for; matrix products, arithmetic and copies ran while one was open for 28% of the time, Pallas kernels for 9%

profile of v2, /device:TPU:0, one launch (start us, length us, event | category | flops | bytes accessed | tf_op | source)
XLA Modules:
  0.0 578.9 jit_solution(490356079878249639)
XLA Ops:
  29.7 7.0 %collective-permute-done.6 = bf16[2,32,640]{2,1,0:T(8,128)(2,1)S(1)} collective-permute-done((bf16[2,32,640]{2,1,0:T(8,128)(2,1)S(1)}, bf16[2,32,640]{2,1,0:T(8,128)(2,1)S(1)}, u32[]{:S(2)}, u32[]{:S(2)}) %collective-permute-start.6) | collective-permute-done | bytes 81952 | tf_op jit(solution)/shard_map/ppermute | solution.py:77
  49.6 9.3 %collective-permute-done.15 = bf16[2,32,960]{2,1,0:T(8,128)(2,1)S(1)} collective-permute-done((bf16[2,32,960]{2,1,0:T(8,128)(2,1)S(1)}, bf16[2,32,960]{2,1,0:T(8,128)(2,1)S(1)}, u32[]{:S(2)}, u32[]{:S(2)}) %collective-permute-start.15) | collective-permute-done | bytes 122912 | tf_op jit(solution)/shard_map/ppermute | solution.py:77
  78.5 15.8 %collective-permute-done.29 = bf16[2,32,2560]{2,1,0:T(8,128)(2,1)S(1)} collective-permute-done((bf16[2,32,2560]{2,1,0:T(8,128)(2,1)S(1)}, bf16[2,32,2560]{2,1,0:T(8,128)(2,1)S(1)}, u32[]{:S(2)}, u32[]{:S(2)}) %collective-permute-start.29) | collective-permute-done | bytes 327712 | tf_op jit(solution)/shard_map/ppermute | solution.py:77
  105.5 5.5 collective-permute-done.35
  134.5 14.0 %collective-permute-done.24 = bf16[8,48,960]{2,1,0:T(8,128)(2,1)} collective-permute-done((bf16[8,48,960]{2,1,0:T(8,128)(2,1)}, bf16[8,48,960]{2,1,0:T(8,128)(2,1)}, u32[]{:S(2)}, u32[]{:S(2)}) %collective-permute-start.24) | collective-permute-done | bytes 737312 | tf_op jit(solution)/shard_map/ppermute | solution.py:77
  155.6 5.8 %collective-permute-done.30 = bf16[4,32,2560]{2,1,0:T(8,128)(2,1)S(1)} collective-permute-done((bf16[4,32,2560]{2,1,0:T(8,128)(2,1)S(1)}, bf16[4,32,2560]{2,1,0:T(8,128)(2,1)S(1)}, u32[]{:S(2)}, u32[]{:S(2)}) %collective-permute-start.30) | collective-permute-done | bytes 655392 | tf_op jit(solution)/shard_map/ppermute | solution.py:77
  162.1 6.0 %collective-permute-done.25 = bf16[4,32,2560]{2,1,0:T(8,128)(2,1)S(1)} collective-permute-done((bf16[4,32,2560]{2,1,0:T(8,128)(2,1)S(1)}, bf16[4,32,2560]{2,1,0:T(8,128)(2,1)S(1)}, u32[]{:S(2)}, u32[]{:S(2)}) %collective-permute-start.25) | collective-permute-done | bytes 655392 | tf_op jit(solution)/shard_map/ppermute | solution.py:77
  171.4 20.9 %attend.1 = (bf16[960,512]{1,0:T(8,128)(2,1)S(1)}, f32[2,15,256]{2,1,0:T(8,128)S(1)}) custom-call(bf16[960,512]{1,0:T(8,128)(2,1)S(1)} %bitcast.152, bf16[4,640,512]{2,1,0:T(8,128)(2,1)S(1)} %pad_maximum_fusion.1.kv_ref, f32[2,1024,256]{2,1,0:T(8,128)S(1)} %copy-done.2), custom_call_target="tpu_custom_call" | custom-call | flops 2013265920 | bytes 8388608 | tf_op jit(solution)/shard_map/attend/pallas_call | solution.py:335
  208.1 7.9 %collective-permute-done.37 = bf16[8,32,960]{2,1,0:T(8,128)(2,1)S(1)} collective-permute-done((bf16[8,32,960]{2,1,0:T(8,128)(2,1)S(1)}, bf16[8,32,960]{2,1,0:T(8,128)(2,1)S(1)}, u32[]{:S(2)}, u32[]{:S(2)}) %collective-permute-start.37) | collective-permute-done | bytes 491552 | tf_op jit(solution)/shard_map/ppermute | solution.py:77
  220.9 4.7 fusion.117
  235.4 8.4 %fusion.4 = (bf16[512,2560]{1,0:T(8,128)(2,1)S(1)}, bf16[512,2560]{1,0:T(8,128)(2,1)S(1)}, bf16[512,2560]{1,0:T(8,128)(2,1)S(1)}) fusion(f32[2560,512]{0,1:T(8,128)} %fusion.117, f32[512,2560]{1,0:T(8,128)} %fusion.116, bf16[512,1024]{1,0:T(8,128)(2,1)S(1)} %fusion.32, bf16[1024,2560]{1,0:T(8,128)(2,1)} %bitcast.184), kind=kOutput, calls=%fused_computation.10 | convolution fusion | flops 2705326080 | bytes 24641536 | tf_op jit(solution)/shard_map/dot_general | solution.py:64
  268.2 5.7 fusion.35.do_ref
  273.9 5.0 convolution_convert_fusion.2
  283.9 7.8 %copy.34 = bf16[2560,960]{1,0:T(8,128)(2,1)} copy(bf16[2560,960]{0,1:T(8,128)(2,1)} %convolution_convert_fusion) | data formatting | bytes 9830400 | tf_op jit(solution)/shard_map/convert_element_type | solution.py:510
  327.5 8.1 %collective-permute-done.43 = bf16[8,32,960]{2,1,0:T(8,128)(2,1)S(1)} collective-permute-done((bf16[8,32,960]{2,1,0:T(8,128)(2,1)S(1)}, bf16[8,32,960]{2,1,0:T(8,128)(2,1)S(1)}, u32[]{:S(2)}, u32[]{:S(2)}) %collective-permute-start.43) | collective-permute-done | bytes 491552 | tf_op jit(solution)/shard_map/ppermute | solution.py:77
  337.3 14.8 %collective-permute-done.44 = bf16[4,32,960]{2,1,0:T(8,128)(2,1)S(1)} collective-permute-done((bf16[4,32,960]{2,1,0:T(8,128)(2,1)S(1)}, bf16[4,32,960]{2,1,0:T(8,128)(2,1)S(1)}, u32[]{:S(2)}, u32[]{:S(2)}) %collective-permute-start.44) | collective-permute-done | bytes 245792 | tf_op jit(solution)/shard_map/ppermute | solution.py:77
  354.5 5.5 collective-permute-done.84
  366.4 24.8 %attend_back.1 = (f32[960,512]{1,0:T(8,128)S(1)}, bf16[4,640,512]{2,1,0:T(8,128)(2,1)}) custom-call(bf16[960,512]{1,0:T(8,128)(2,1)S(1)} %bitcast.153, bf16[4,640,512]{2,1,0:T(8,128)(2,1)} %copy-done.1, f32[2,1024,256]{2,1,0:T(8,128)} %and_select_fusion.bias_ref, bf16[960,512]{1,0:T(8,128)(2,1)S(1)} %copy-done.6, ...), custom_call_target="tpu_custom_call" | custom-call | flops 5033164800 | bytes 14680064 | tf_op jit(solution)/shard_map/attend_back/pallas_call | solution.py:356
  425.2 16.3 %collective-permute-done.58 = bf16[8,32,2560]{2,1,0:T(8,128)(2,1)} collective-permute-done((bf16[8,32,2560]{2,1,0:T(8,128)(2,1)}, bf16[8,32,2560]{2,1,0:T(8,128)(2,1)}, u32[]{:S(2)}, u32[]{:S(2)}) %collective-permute-start.58) | collective-permute-done | bytes 1310752 | tf_op jit(solution)/shard_map/ppermute | solution.py:77
  443.8 19.1 %collective-permute-done.46 = bf16[1,640,512]{2,1,0:T(8,128)(2,1)S(1)} collective-permute-done((bf16[1,640,512]{2,1,0:T(8,128)(2,1)S(1)}, bf16[1,640,512]{2,1,0:T(8,128)(2,1)S(1)}, u32[]{:S(2)}, u32[]{:S(2)}) %collective-permute-start.46) | collective-permute-done | bytes 655392 | tf_op jit(solution)/shard_map/ppermute | solution.py:77
  480.3 10.7 %collective-permute-done.49 = f32[960]{0:T(1024)S(1)} collective-permute-done((f32[960]{0:T(1024)S(1)}, f32[960]{0:T(1024)S(1)}, u32[]{:S(2)}, u32[]{:S(2)}) %collective-permute-start.49) | collective-permute-done | bytes 3872 | tf_op jit(solution)/shard_map/ppermute | solution.py:77
  503.7 20.1 %collective-permute-done.80 = bf16[2,32,2560]{2,1,0:T(8,128)(2,1)S(1)} collective-permute-done((bf16[2,32,2560]{2,1,0:T(8,128)(2,1)S(1)}, bf16[2,32,2560]{2,1,0:T(8,128)(2,1)S(1)}, u32[]{:S(2)}, u32[]{:S(2)}) %collective-permute-start.80) | collective-permute-done | bytes 327712 | tf_op jit(solution)/shard_map/ppermute | solution.py:77
  523.9 5.6 collective-permute-done.78
  551.1 8.0 %collective-permute-done.68 = bf16[4,32,640]{2,1,0:T(8,128)(2,1)S(1)} collective-permute-done((bf16[4,32,640]{2,1,0:T(8,128)(2,1)S(1)}, bf16[4,32,640]{2,1,0:T(8,128)(2,1)S(1)}, u32[]{:S(2)}, u32[]{:S(2)}) %collective-permute-start.68) | collective-permute-done | bytes 163872 | tf_op jit(solution)/shard_map/ppermute | solution.py:77
  (552 shorter events, 319.3 us)
Async XLA Ops:
  64.3 49.0 %collective-permute-start.9 = (bf16[16,32,640]{2,1,0:T(8,128)(2,1)S(1)}, bf16[16,32,640]{2,1,0:T(8,128)(2,1)S(1)}, u32[]{:S(2)}, u32[]{:S(2)}) collective-permute-start(bf16[16,32,640]{2,1,0:T(8,128)(2,1)S(1)} %get-tuple-element.128), channel_id=1, source_target_pairs={{0,1},{1,0},{2,3},{3,2},{4,5},{5,4},{6,7},{7,6},{8,9},{9,8},{10,11... | collective-permute-start | bytes 1966088 | tf_op jit(solution)/shard_map/ppermute | solution.py:77
  71.3 27.7 %collective-permute-start.22 = (bf16[2,32,2560]{2,1,0:T(8,128)(2,1)S(1)}, bf16[2,32,2560]{2,1,0:T(8,128)(2,1)S(1)}, u32[]{:S(2)}, u32[]{:S(2)}) collective-permute-start(bf16[2,32,2560]{2,1,0:T(8,128)(2,1)S(1)} %pad_maximum_fusion.23), channel_id=1, source_target_pairs={{0,16},{1,17},{2,18},{3,19},{4,20},{5,21},{6,22},{7,23},{8,24},{9,... | collective-permute-start | bytes 983048 | tf_op jit(solution)/shard_map/ppermute | solution.py:77
  74.8 36.9 %collective-permute-start.16 = (bf16[4,32,960]{2,1,0:T(8,128)(2,1)S(1)}, bf16[4,32,960]{2,1,0:T(8,128)(2,1)S(1)}, u32[]{:S(2)}, u32[]{:S(2)}) collective-permute-start(bf16[4,32,960]{2,1,0:T(8,128)(2,1)S(1)} %pad_maximum_fusion.28), channel_id=1, source_target_pairs={{0,2},{1,3},{2,0},{3,1},{4,6},{5,7},{6,4},{7,5},{8,10},{9,11},{10,... | collective-permute-start | bytes 737288 | tf_op jit(solution)/shard_map/ppermute | solution.py:77
  75.3 41.7 %collective-permute-start.23 = (bf16[4,48,960]{2,1,0:T(8,128)(2,1)S(1)}, bf16[4,48,960]{2,1,0:T(8,128)(2,1)S(1)}, u32[]{:S(2)}, u32[]{:S(2)}) collective-permute-start(bf16[4,48,960]{2,1,0:T(8,128)(2,1)S(1)} %pad_maximum_fusion.21), channel_id=1, source_target_pairs={{0,4},{1,5},{2,6},{3,7},{4,0},{5,1},{6,2},{7,3},{8,12},{9,13},{10,... | collective-permute-start | bytes 1105928 | tf_op jit(solution)/shard_map/ppermute | solution.py:77
  94.4 30.0 %collective-permute-start.4 = (bf16[16,32,960]{2,1,0:T(8,128)(2,1)S(1)}, bf16[16,32,960]{2,1,0:T(8,128)(2,1)S(1)}, u32[]{:S(2)}, u32[]{:S(2)}) collective-permute-start(bf16[16,32,960]{2,1,0:T(8,128)(2,1)S(1)} %get-tuple-element.122), channel_id=1, source_target_pairs={{0,1},{1,0},{2,3},{3,2},{4,5},{5,4},{6,7},{7,6},{8,9},{9,8},{10,11... | collective-permute-start | bytes 2949128 | tf_op jit(solution)/shard_map/ppermute | solution.py:77
  116.6 32.5 %collective-permute-start.10 = (bf16[1,640,512]{2,1,0:T(8,128)(2,1)}, bf16[1,640,512]{2,1,0:T(8,128)(2,1)}, u32[]{:S(2)}, u32[]{:S(2)}) collective-permute-start(bf16[1,640,512]{2,1,0:T(8,128)(2,1)} %maximum_bitcast_fusion), channel_id=1, source_target_pairs={{0,2},{1,3},{2,0},{3,1},{4,6},{5,7},{6,4},{7,5},{8,10},{9,11},{10,... | collective-permute-start | bytes 1966088 | tf_op jit(solution)/shard_map/ppermute | solution.py:77
  118.0 30.5 %collective-permute-start.24 = (bf16[8,48,960]{2,1,0:T(8,128)(2,1)}, bf16[8,48,960]{2,1,0:T(8,128)(2,1)}, u32[]{:S(2)}, u32[]{:S(2)}) collective-permute-start(bf16[8,48,960]{2,1,0:T(8,128)(2,1)} %pad_maximum_fusion.11), channel_id=1, source_target_pairs={{0,2},{1,3},{2,0},{3,1},{4,6},{5,7},{6,4},{7,5},{8,10},{9,11},{10,... | collective-permute-start | bytes 2211848 | tf_op jit(solution)/shard_map/ppermute | solution.py:77
  124.3 29.9 %collective-permute-start.18 = (bf16[16,32,960]{2,1,0:T(8,128)(2,1)}, bf16[16,32,960]{2,1,0:T(8,128)(2,1)}, u32[]{:S(2)}, u32[]{:S(2)}) collective-permute-start(bf16[16,32,960]{2,1,0:T(8,128)(2,1)} %pad_maximum_fusion.9), channel_id=1, source_target_pairs={{0,1},{1,0},{2,3},{3,2},{4,5},{5,4},{6,7},{7,6},{8,9},{9,8},{10,11... | collective-permute-start | bytes 2949128 | tf_op jit(solution)/shard_map/ppermute | solution.py:77
  154.1 64.0 %collective-permute-start.33 = (bf16[16,48,960]{2,1,0:T(8,128)(2,1)}, bf16[16,48,960]{2,1,0:T(8,128)(2,1)S(1)}, u32[]{:S(2)}, u32[]{:S(2)}) collective-permute-start(bf16[16,48,960]{2,1,0:T(8,128)(2,1)} %constant_dynamic-update-slice_fusion.30.a_ref), channel_id=1, source_target_pairs={{0,1},{1,0},{2,3},{3,2},{4,5},{5,4},{6,7},{7,6},{8,9},{9,8},{10,11... | collective-permute-start | bytes 4423688 | tf_op jit(solution)/shard_map/ppermute | solution.py:77
  161.5 34.9 %collective-permute-start.31 = (bf16[8,32,2560]{2,1,0:T(8,128)(2,1)S(1)}, bf16[8,32,2560]{2,1,0:T(8,128)(2,1)S(1)}, u32[]{:S(2)}, u32[]{:S(2)}) collective-permute-start(bf16[8,32,2560]{2,1,0:T(8,128)(2,1)S(1)} %pad_maximum_fusion.7), channel_id=1, source_target_pairs={{0,4},{1,5},{2,6},{3,7},{4,0},{5,1},{6,2},{7,3},{8,12},{9,13},{10,... | collective-permute-start | bytes 3932168 | tf_op jit(solution)/shard_map/ppermute | solution.py:77
  168.3 30.0 %collective-permute-start.26 = (bf16[8,32,2560]{2,1,0:T(8,128)(2,1)S(1)}, bf16[8,32,2560]{2,1,0:T(8,128)(2,1)S(1)}, u32[]{:S(2)}, u32[]{:S(2)}) collective-permute-start(bf16[8,32,2560]{2,1,0:T(8,128)(2,1)S(1)} %pad_maximum_fusion.6), channel_id=1, source_target_pairs={{0,2},{1,3},{2,0},{3,1},{4,6},{5,7},{6,4},{7,5},{8,10},{9,11},{10,... | collective-permute-start | bytes 3932168 | tf_op jit(solution)/shard_map/ppermute | solution.py:77
  313.5 91.5 %collective-permute-start.57 = (bf16[16,32,2560]{2,1,0:T(8,128)(2,1)}, bf16[16,32,2560]{2,1,0:T(8,128)(2,1)}, u32[]{:S(2)}, u32[]{:S(2)}) collective-permute-start(bf16[16,32,2560]{2,1,0:T(8,128)(2,1)} %bitcast.38), channel_id=1, source_target_pairs={{0,1},{1,0},{2,3},{3,2},{4,5},{5,4},{6,7},{7,6},{8,9},{9,8},{10,11... | collective-permute-start | bytes 7864328 | tf_op jit(solution)/shard_map/ppermute | solution.py:77
  318.9 94.4 %collective-permute-start.54 = (bf16[16,32,2560]{2,1,0:T(8,128)(2,1)}, bf16[16,32,2560]{2,1,0:T(8,128)(2,1)}, u32[]{:S(2)}, u32[]{:S(2)}) collective-permute-start(bf16[16,32,2560]{2,1,0:T(8,128)(2,1)} %bitcast.169), channel_id=1, source_target_pairs={{0,1},{1,0},{2,3},{3,2},{4,5},{5,4},{6,7},{7,6},{8,9},{9,8},{10,11... | collective-permute-start | bytes 7864328 | tf_op jit(solution)/shard_map/ppermute | solution.py:77
  326.9 25.6 %collective-permute-start.40 = (bf16[8,48,960]{2,1,0:T(8,128)(2,1)S(1)}, bf16[8,48,960]{2,1,0:T(8,128)(2,1)S(1)}, u32[]{:S(2)}, u32[]{:S(2)}) collective-permute-start(bf16[8,48,960]{2,1,0:T(8,128)(2,1)S(1)} %slice.441), channel_id=1, source_target_pairs={{0,2},{1,3},{2,0},{3,1},{4,6},{5,7},{6,4},{7,5},{8,10},{9,11},{10,... | collective-permute-start | bytes 2211848 | tf_op jit(solution)/shard_map/ppermute | solution.py:77
  365.9 45.7 %collective-permute-start.82 = (bf16[2,48,960]{2,1,0:T(8,128)(2,1)}, bf16[2,48,960]{2,1,0:T(8,128)(2,1)}, u32[]{:S(2)}, u32[]{:S(2)}) collective-permute-start(bf16[2,48,960]{2,1,0:T(8,128)(2,1)} %slice.520), channel_id=1, source_target_pairs={{0,16},{1,17},{2,18},{3,19},{4,20},{5,21},{6,22},{7,23},{8,24},{9,... | collective-permute-start | bytes 552968 | tf_op jit(solution)/shard_map/ppermute | solution.py:77
  393.7 28.1 %collective-permute-start.45 = (bf16[2,640,512]{2,1,0:T(8,128)(2,1)}, bf16[2,640,512]{2,1,0:T(8,128)(2,1)}, u32[]{:S(2)}, u32[]{:S(2)}) collective-permute-start(bf16[2,640,512]{2,1,0:T(8,128)(2,1)} %slice.351), channel_id=1, source_target_pairs={{0,1},{1,0},{2,3},{3,2},{4,5},{5,4},{6,7},{7,6},{8,9},{9,8},{10,11... | collective-permute-start | bytes 3932168 | tf_op jit(solution)/shard_map/ppermute | solution.py:77
  410.0 31.5 %collective-permute-start.58 = (bf16[8,32,2560]{2,1,0:T(8,128)(2,1)}, bf16[8,32,2560]{2,1,0:T(8,128)(2,1)}, u32[]{:S(2)}, u32[]{:S(2)}) collective-permute-start(bf16[8,32,2560]{2,1,0:T(8,128)(2,1)} %pad_maximum_fusion.8), channel_id=1, source_target_pairs={{0,4},{1,5},{2,6},{3,7},{4,0},{5,1},{6,2},{7,3},{8,12},{9,13},{10,... | collective-permute-start | bytes 3932168 | tf_op jit(solution)/shard_map/ppermute | solution.py:77
  417.0 55.0 %collective-permute-start.55 = (bf16[8,32,2560]{2,1,0:T(8,128)(2,1)}, bf16[8,32,2560]{2,1,0:T(8,128)(2,1)}, u32[]{:S(2)}, u32[]{:S(2)}) collective-permute-start(bf16[8,32,2560]{2,1,0:T(8,128)(2,1)} %slice.469), channel_id=1, source_target_pairs={{0,2},{1,3},{2,0},{3,1},{4,6},{5,7},{6,4},{7,5},{8,10},{9,11},{10,... | collective-permute-start | bytes 3932168 | tf_op jit(solution)/shard_map/ppermute | solution.py:77
  423.6 39.2 %collective-permute-start.46 = (bf16[1,640,512]{2,1,0:T(8,128)(2,1)S(1)}, bf16[1,640,512]{2,1,0:T(8,128)(2,1)S(1)}, u32[]{:S(2)}, u32[]{:S(2)}) collective-permute-start(bf16[1,640,512]{2,1,0:T(8,128)(2,1)S(1)} %slice.451), channel_id=1, source_target_pairs={{0,2},{1,3},{2,0},{3,1},{4,6},{5,7},{6,4},{7,5},{8,10},{9,11},{10,... | collective-permute-start | bytes 1966088 | tf_op jit(solution)/shard_map/ppermute | solution.py:77
  443.2 56.5 %collective-permute-start.59 = (bf16[4,32,2560]{2,1,0:T(8,128)(2,1)S(1)}, bf16[4,32,2560]{2,1,0:T(8,128)(2,1)S(1)}, u32[]{:S(2)}, u32[]{:S(2)}) collective-permute-start(bf16[4,32,2560]{2,1,0:T(8,128)(2,1)S(1)} %slice.475), channel_id=1, source_target_pairs={{0,2},{1,3},{2,0},{3,1},{4,6},{5,7},{6,4},{7,5},{8,10},{9,11},{10,... | collective-permute-start | bytes 1966088 | tf_op jit(solution)/shard_map/ppermute | solution.py:77
  473.8 28.0 %collective-permute-start.56 = (bf16[4,32,2560]{2,1,0:T(8,128)(2,1)S(1)}, bf16[4,32,2560]{2,1,0:T(8,128)(2,1)S(1)}, u32[]{:S(2)}, u32[]{:S(2)}) collective-permute-start(bf16[4,32,2560]{2,1,0:T(8,128)(2,1)S(1)} %slice.470), channel_id=1, source_target_pairs={{0,4},{1,5},{2,6},{3,7},{4,0},{5,1},{6,2},{7,3},{8,12},{9,13},{10,... | collective-permute-start | bytes 1966088 | tf_op jit(solution)/shard_map/ppermute | solution.py:77
  480.2 52.9 %collective-permute-start.66 = (bf16[16,32,640]{2,1,0:T(8,128)(2,1)S(1)}, bf16[16,32,640]{2,1,0:T(8,128)(2,1)S(1)}, u32[]{:S(2)}, u32[]{:S(2)}) collective-permute-start(bf16[16,32,640]{2,1,0:T(8,128)(2,1)S(1)} %bitcast.198), channel_id=1, source_target_pairs={{0,1},{1,0},{2,3},{3,2},{4,5},{5,4},{6,7},{7,6},{8,9},{9,8},{10,11... | collective-permute-start | bytes 1966088 | tf_op jit(solution)/shard_map/ppermute | solution.py:77
  501.9 27.6 %collective-permute-start.78 = (bf16[2,32,2560]{2,1,0:T(8,128)(2,1)S(1)}, bf16[2,32,2560]{2,1,0:T(8,128)(2,1)S(1)}, u32[]{:S(2)}, u32[]{:S(2)}) collective-permute-start(bf16[2,32,2560]{2,1,0:T(8,128)(2,1)S(1)} %slice.506), channel_id=1, source_target_pairs={{0,16},{1,17},{2,18},{3,19},{4,20},{5,21},{6,22},{7,23},{8,24},{9,... | collective-permute-start | bytes 983048 | tf_op jit(solution)/shard_map/ppermute | solution.py:77
  503.2 26.6 %collective-permute-start.60 = (bf16[8,32,960]{2,1,0:T(8,128)(2,1)S(1)}, bf16[8,32,960]{2,1,0:T(8,128)(2,1)S(1)}, u32[]{:S(2)}, u32[]{:S(2)}) collective-permute-start(bf16[8,32,960]{2,1,0:T(8,128)(2,1)S(1)} %copy-done.48), channel_id=1, source_target_pairs={{0,4},{1,5},{2,6},{3,7},{4,0},{5,1},{6,2},{7,3},{8,12},{9,13},{10,... | collective-permute-start | bytes 1474568 | tf_op jit(solution)/shard_map/ppermute | solution.py:77
  (138 other events, 1616.1 us)

commit v3 on v2

v3 whole, which is shorter than its diff:
```python
import jax
import jax.numpy as jnp
from jax import lax
from jax.experimental import pallas as pl
from jax.experimental.pallas import tpu as pltpu
from jax.sharding import PartitionSpec as P

D = 960
HEADS = 15
KV_HEADS = 5
HEAD_DIM = 64
FF = 2560
GROUP = HEADS // KV_HEADS
ATTN = HEADS * HEAD_DIM
KV = KV_HEADS * HEAD_DIM
AXES = ("dp", "ctx")
CORE, FIRST, SECOND = 1, 2, 4

norm_eps = 1e-05
rope_base = 100000.0
mask_fill = -1000000000.0
low = jnp.bfloat16
wide = jnp.float32


def rms_scale(values):
    return lax.rsqrt(jnp.mean(values * values, axis=-1, keepdims=True) + norm_eps)


def norm_back(values, scale, gain, grad):
    gain_grad = jnp.sum(grad * values * scale, axis=0)
    weighted = grad * gain
    inner = jnp.mean(weighted * values, axis=-1, keepdims=True)
    return (scale * weighted - values * (scale * scale * scale) * inner, gain_grad)


def rope_tables(position):
    freqs = rope_base ** (-jnp.arange(0, HEAD_DIM, 2, dtype=wide) / HEAD_DIM)
    angles = freqs[:, None] * position.astype(wide)[None, :]
    angles = jnp.concatenate([angles, angles], axis=0)
    return jnp.cos(angles), jnp.sin(angles)


def by_head(values):
    return values.reshape(-1, HEAD_DIM, values.shape[-1])


def rotate(values, cosine, sine):
    values = by_head(values)
    half = HEAD_DIM // 2
    turned = jnp.concatenate([-values[:, half:], values[:, :half]], axis=1)
    return (values * cosine + turned * sine).reshape(-1, values.shape[-1])


def rotate_back(grad, cosine, sine):
    grad = by_head(grad)
    half = HEAD_DIM // 2
    scaled = grad * sine
    turned = jnp.concatenate([scaled[:, half:], -scaled[:, :half]], axis=1)
    return (grad * cosine + turned).reshape(-1, grad.shape[-1])


def product(left, right):
    return jnp.dot(left, right, preferred_element_type=wide)


def product_left(left, right):
    return lax.dot_general(left, right, (((0,), (0,)), ((), ())), preferred_element_type=wide)


def product_right(left, right):
    return lax.dot_general(left, right, (((1,), (1,)), ((), ())), preferred_element_type=wide)


def swap(value, mask):
    n = lax.axis_size(AXES)
    return lax.ppermute(value, AXES, [(i, i ^ mask) for i in range(n)])


def add_low(left, right):
    return (left.astype(wide) + right.astype(wide)).astype(low)


def far_masks():
    n = lax.axis_size(AXES)
    masks, m = [], 8
    while m < n:
        masks.append(m)
        m *= 2
    return masks


def block_owner(place):
    far = far_masks()
    owner = jnp.zeros_like(place)
    for bit, mask in enumerate(far + [SECOND, FIRST, CORE]):
        owner = owner | (((place >> bit) & 1) * mask)
    return owner


class Slots:
    def __init__(self):
        self.deps = ()

    def send(self, pairs):
        values = tuple(value for value, _ in pairs)
        if self.deps:
            values = lax.optimization_barrier((values, self.deps))[0]
        came = [swap(value, mask) for value, (_, mask) in zip(values, pairs)]
        self.deps = tuple(came)
        return came

    def hold(self, *values):
        self.deps = self.deps + values

    def after(self, value):
        return lax.optimization_barrier((value, self.deps))[0]

    def run(self, moves, extra=()):
        pairs = [piece.give(stage) for piece, stage in moves]
        came = self.send(pairs + list(extra))
        for (piece, stage), value in zip(moves, came):
            piece.take(stage, value)
        return came[len(moves) :]


class Gathered:
    def __init__(self, block, route):
        self.now, self.route = block[None], route

    def give(self, stage):
        near = (FIRST, SECOND) if self.route else (SECOND, FIRST)
        return self.now, (8, 16, *near, CORE)[stage]

    def take(self, stage, came):
        if stage == 2:
            self.own, self.side = self.now, came
        if stage == 3 and self.route:
            n = came.shape[0] // 2
            parts = [self.own, came[:n], self.side, came[n:]]
        else:
            parts = [self.now, came]
        if stage == 4:
            self.mine, self.theirs = self.now, came
        else:
            self.now = jnp.concatenate(parts, axis=0)

    def weight(self):
        whole = jnp.concatenate([self.mine, self.theirs], axis=0)
        return whole.reshape(-1, whole.shape[-1])


class Reduced:
    def __init__(self, mine, theirs, route):
        self.mine, self.theirs, self.route = mine, theirs, route

    def give(self, stage):
        near = (SECOND, FIRST) if self.route else (FIRST, SECOND)
        mask = (CORE, *near, 16, 8)[stage]
        if stage == 0:
            return self.theirs, mask
        n = self.now.shape[0] // 2
        if stage == 1 and self.route:
            q = n // 2
            self.keep = jnp.concatenate([self.now[:q], self.now[n : n + q]], axis=0)
            return jnp.concatenate([self.now[q:n], self.now[n + q :]], axis=0), mask
        self.keep = self.now[:n]
        return self.now[n:], mask

    def take(self, stage, came):
        if stage == 0:
            self.now = add_low(self.mine, came)
        elif stage == 4:
            self.result = self.keep[0].astype(wide) + came[0].astype(wide)
        else:
            self.now = add_low(self.keep, came)


def ctx_masks():
    m, masks = lax.axis_size("ctx") // 2, []
    while m >= 1:
        masks.append(m)
        m //= 2
    return masks


def ctx_gather(value):
    now = value[None]
    for mask in ctx_masks():
        now = jnp.concatenate([now, swap(now, mask)], axis=0)
    return now


def ctx_scatter(value):
    now = value
    for mask in ctx_masks()[::-1]:
        n = now.shape[0] // 2
        now = now[:n].astype(wide) + swap(now[n:], mask).astype(wide)
        if n > 1:
            now = now.astype(low)
    return now[0]


def whole_spec():
    return pl.BlockSpec(memory_space=pltpu.VMEM)


def join_blocks(parts, order):
    (a, b), (c, d) = parts
    half, top, columns = a.shape
    bottom = c.shape[1]

    def kernel(order_ref, a_ref, b_ref, c_ref, d_ref, out_ref):
        def step(p, _):
            near, far = order_ref[p], order_ref[p + half]
            out_ref[near, :top, :] = a_ref[p]
            out_ref[near, top:, :] = c_ref[p]
            out_ref[far, :top, :] = b_ref[p]
            out_ref[far, top:, :] = d_ref[p]
            return 0

        lax.fori_loop(0, half, step, 0)

    shape = (2 * half, top + bottom, columns)
    return pl.pallas_call(
        kernel,
        out_shape=jax.ShapeDtypeStruct(shape, a.dtype),
        in_specs=[pl.BlockSpec(memory_space=pltpu.SMEM)] + [whole_spec()] * 4,
        out_specs=whole_spec(),
        compiler_params=pltpu.CompilerParams(vmem_limit_bytes=24 * 2**20),
        cost_estimate=pl.CostEstimate(
            flops=0, bytes_accessed=4 * shape[0] * shape[1] * columns, transcendentals=0
        ),
        name="join_blocks",
    )(order, a, b, c, d)


def down_grad_blocks(hidden, grad, place, top):
    rows, hidden_width = hidden.shape
    columns = grad.shape[1]
    total = place.shape[0]
    tall = hidden_width // total
    group = 8

    def kernel(place_ref, h_ref, g_ref, a_ref, b_ref):
        value = product_left(h_ref[...], g_ref[...]).astype(low)
        first = pl.program_id(0) * group
        for b in range(group):
            to = place_ref[first + b]
            a_ref[to] = value[b * tall : b * tall + top]
            b_ref[to] = value[b * tall + top : (b + 1) * tall]

    return pl.pallas_call(
        kernel,
        grid=(total // group,),
        in_specs=[
            pl.BlockSpec(memory_space=pltpu.SMEM),
            pl.BlockSpec((rows, group * tall), lambda i: (0, i)),
            pl.BlockSpec((rows, columns), lambda i: (0, 0)),
        ],
        out_specs=[
            pl.BlockSpec((total, top, columns), lambda i: (0, 0, 0)),
            pl.BlockSpec((total, tall - top, columns), lambda i: (0, 0, 0)),
        ],
        out_shape=[
            jax.ShapeDtypeStruct((total, top, columns), low),
            jax.ShapeDtypeStruct((total, tall - top, columns), low),
        ],
        compiler_params=pltpu.CompilerParams(vmem_limit_bytes=32 * 2**20),
        cost_estimate=pl.CostEstimate(
            flops=2 * rows * hidden_width * columns,
            bytes_accessed=2 * (rows * (hidden_width + columns) + hidden_width * columns),
            transcendentals=0,
        ),
        name="down_grad_blocks",
    )(place, hidden, grad)


def head_rows(ref, head):
    return ref[head * HEAD_DIM : (head + 1) * HEAD_DIM, :]


def key_blocks(kv_ref, start):
    blocks = [kv_ref[b, start : start + HEAD_DIM, :] for b in range(kv_ref.shape[0])]
    return jnp.concatenate(blocks, axis=1)


def turn(value):
    return value.astype(wide).T.astype(low)


def attend_kernel(q_ref, kv_ref, bias_ref, o_ref, lse_ref):
    for g in range(KV_HEADS):
        keys = turn(key_blocks(kv_ref, g * HEAD_DIM))
        values_t = key_blocks(kv_ref, KV + g * HEAD_DIM)
        for h in range(g * GROUP, (g + 1) * GROUP):
            scores = product(keys, head_rows(q_ref, h)) + bias_ref[0]
            top = jnp.max(scores, axis=0, keepdims=True)
            weight = jnp.exp(scores - top)
            total = jnp.sum(weight, axis=0, keepdims=True)
            mixed = product(values_t, weight.astype(low)) / total
            o_ref[h * HEAD_DIM : (h + 1) * HEAD_DIM, :] = mixed.astype(low)
            lse_ref[0, h : h + 1, :] = top + jnp.log(total)


def attend_back_kernel(q_ref, kv_ref, bias_ref, o_ref, lse_ref, do_ref, dq_ref, dkv_ref):
    width = q_ref.shape[1]
    for g in range(KV_HEADS):
        keys_t = key_blocks(kv_ref, g * HEAD_DIM)
        keys = turn(keys_t)
        values = turn(key_blocks(kv_ref, KV + g * HEAD_DIM))
        key_grad, value_grad = None, None
        for h in range(g * GROUP, (g + 1) * GROUP):
            query, grad = head_rows(q_ref, h), head_rows(do_ref, h)
            scores = product(keys, query) + bias_ref[0]
            probs = jnp.exp(scores - lse_ref[0, h : h + 1, :])
            inner = jnp.sum(
                grad.astype(wide) * head_rows(o_ref, h).astype(wide), axis=0, keepdims=True
            )
            scores_grad = (probs * (product(values, grad) - inner)).astype(low)
            dq_ref[h * HEAD_DIM : (h + 1) * HEAD_DIM, :] = product(keys_t, scores_grad)
            from_keys = product_right(scores_grad, query)
            from_values = product_right(probs.astype(low), grad)
            key_grad = from_keys if key_grad is None else key_grad + from_keys
            value_grad = from_values if value_grad is None else value_grad + from_values
        for start, value in ((g * HEAD_DIM, key_grad), (KV + g * HEAD_DIM, value_grad)):
            turned = value.T.astype(low)
            for b in range(kv_ref.shape[0]):
                dkv_ref[b, start : start + HEAD_DIM, :] = turned[:, b * width : (b + 1) * width]


def attention_specs(blocks, block_len, length, seq):
    columns = pl.BlockSpec((ATTN, block_len), lambda i: (0, seq))
    pairs = pl.BlockSpec((blocks, 2 * KV, block_len), lambda i: (0, 0, seq))
    bias = pl.BlockSpec((1, length, block_len), lambda i: (seq, 0, 0))
    own = pl.BlockSpec((ATTN, block_len), lambda i: (0, 0))
    own_pairs = pl.BlockSpec((blocks, 2 * KV, block_len), lambda i: (0, 0, 0))
    logs = pl.BlockSpec((1, HEADS, block_len), lambda i: (0, 0, 0))
    return columns, pairs, bias, own, own_pairs, logs


def attend(query_t, pairs_t, bias, seq):
    _, length, block_len = bias.shape
    columns, pairs, bias_spec, own, _, logs = attention_specs(
        pairs_t.shape[0], block_len, length, seq
    )
    work = HEADS * length * block_len
    return pl.pallas_call(
        attend_kernel,
        grid=(1,),
        in_specs=[columns, pairs, bias_spec],
        out_specs=[own, logs],
        out_shape=[
            jax.ShapeDtypeStruct((ATTN, block_len), low),
            jax.ShapeDtypeStruct((1, HEADS, block_len), wide),
        ],
        compiler_params=pltpu.CompilerParams(vmem_limit_bytes=40 * 2**20),
        cost_estimate=pl.CostEstimate(
            flops=16 * work * HEAD_DIM, bytes_accessed=8 * 2**20, transcendentals=work
        ),
        name="attend",
    )(query_t, pairs_t, bias)


def attend_back(query_t, pairs_t, bias, mixed_t, logs_all, grad_t, seq):
    _, length, block_len = bias.shape
    columns, pairs, bias_spec, own, own_pairs, logs = attention_specs(
        pairs_t.shape[0], block_len, length, seq
    )
    work = HEADS * length * block_len
    return pl.pallas_call(
        attend_back_kernel,
        grid=(1,),
        in_specs=[columns, pairs, bias_spec, own, logs, columns],
        out_specs=[own, own_pairs],
        out_shape=[
            jax.ShapeDtypeStruct((ATTN, block_len), wide),
            jax.ShapeDtypeStruct((pairs_t.shape[0], 2 * KV, block_len), low),
        ],
        compiler_params=pltpu.CompilerParams(vmem_limit_bytes=48 * 2**20),
        cost_estimate=pl.CostEstimate(
            flops=40 * work * HEAD_DIM, bytes_accessed=14 * 2**20, transcendentals=work
        ),
        name="attend_back",
    )(query_t, pairs_t, bias, mixed_t, logs_all, grad_t)


def key_bias(segment_all, segment_ids, ctx_here, masks):
    blocks, seqs, block_len = segment_all.shape
    place = jnp.arange(blocks, dtype=jnp.int32)
    owner = jnp.zeros_like(place)
    for bit, mask in enumerate(masks):
        owner = owner | (((place >> bit) & 1) * mask)
    inside = jnp.arange(block_len, dtype=jnp.int32)
    key_index = ((owner ^ ctx_here)[:, None] * block_len + inside[None, :]).reshape(-1)
    query_index = ctx_here * block_len + inside
    segments = segment_all.transpose(1, 0, 2).reshape(seqs, -1)
    allowed = (segments[:, :, None] == segment_ids[:, None, :]) & (
        key_index[None, :, None] <= query_index[None, None, :]
    )
    return jnp.where(allowed, 0.0, mask_fill)


def contract(left, right, left_dim, right_dim):
    return lax.dot_general(
        left, right, (((left_dim,), (right_dim,)), ((), ())), preferred_element_type=wide
    )


def silu_parts(gate, up):
    sigmoid = jax.nn.sigmoid(gate)
    return sigmoid, (gate * sigmoid * up).astype(low)


def silu_back(hidden_grad, gate, up, sigmoid):
    gate_grad = (hidden_grad * up * sigmoid * (1.0 + gate * (1.0 - sigmoid))).astype(low)
    return gate_grad, (hidden_grad * gate * sigmoid).astype(low)


def body_blocked(
    tokens, segment_ids, positions, norm_attn, w_query, w_key, w_value, w_out,
    norm_ffn, w_gate, w_up, w_down, cotangent,
):
    seqs, block_len, _ = tokens.shape
    n_dev = lax.axis_size(AXES)
    me, ctx_here = lax.axis_index(AXES), lax.axis_index("ctx")
    rows = seqs * block_len
    score_scale = HEAD_DIM ** (-0.5)
    cut, cut_ff = D // n_dev, FF // n_dev
    pad = -(-cut // 16) * 16
    top_ff = (cut_ff * 3 // 5) // 8 * 8
    half_ff = FF // 2
    split = n_dev * pad // 2
    slots = Slots()

    def rows_of(shard, columns):
        return jnp.pad(shard.reshape(cut, columns), ((0, pad - cut), (0, 0)))

    query_piece = Gathered(rows_of(w_query, ATTN), 0)
    pairs_piece = Gathered(
        jnp.concatenate([rows_of(w_key, KV), rows_of(w_value, KV)], axis=1), 1
    )
    slots.run([(query_piece, 0), (pairs_piece, 0)])
    down_block = w_down.reshape(cut_ff, D)
    top_piece, out_piece = Gathered(down_block[:top_ff], 0), Gathered(rows_of(w_out, D), 1)
    gate_block, up_block = rows_of(w_gate, FF), rows_of(w_up, FF)
    first_pair = Gathered(gate_block[:, :half_ff], 0), Gathered(up_block[:, :half_ff], 1)
    second_pair = Gathered(gate_block[:, half_ff:], 0), Gathered(up_block[:, half_ff:], 1)
    low_piece = Gathered(down_block[top_ff:], 1)

    def at(stage, *pieces):
        return [(piece, stage) for piece in pieces]

    (seg_y,) = slots.run(at(1, query_piece, pairs_piece), [(segment_ids, FIRST)])
    segments = jnp.stack([segment_ids, seg_y])
    places = jnp.arange(n_dev, dtype=jnp.int32)
    order = block_owner(places) ^ me
    place = jnp.sum(jnp.where(order[:, None] == places[None, :], places[:, None], 0), axis=0)
    slot = jnp.arange(n_dev * pad, dtype=jnp.int32)
    source = jnp.where(slot % pad < cut, jnp.repeat(order, pad) * cut + slot % pad, -1)
    perm = (jnp.arange(D, dtype=jnp.int32)[:, None] == source[None, :]).astype(low)
    inputs = tokens.astype(wide).reshape(rows, D)
    scale_attn = rms_scale(inputs)
    normed_attn = product((inputs * scale_attn * norm_attn).astype(low), perm).astype(low)
    (seg_c,) = slots.run(
        at(2, query_piece, pairs_piece) + at(0, top_piece, out_piece), [(segments, CORE)]
    )
    segments = jnp.concatenate([segments, seg_c], axis=0)
    slots.hold(normed_attn)
    slots.run(at(3, query_piece, pairs_piece) + at(1, top_piece, out_piece))
    cosine, sine = rope_tables(positions.reshape(rows))
    bias = key_bias(segments, segment_ids, ctx_here, (2, 1))
    slots.hold(cosine, sine)
    slots.run(at(4, query_piece, pairs_piece) + at(2, top_piece, out_piece) + at(0, *first_pair))
    query_weight, kv_weight = query_piece.weight(), pairs_piece.weight()
    slots.hold(bias)
    slots.run(at(3, top_piece, out_piece) + at(1, *first_pair))
    pairs_t = contract(kv_weight, normed_attn, 0, 1)
    pairs_t = jnp.concatenate(
        [rotate(pairs_t[:KV], cosine, sine).astype(low), pairs_t[KV:].astype(low)], axis=0
    )[None]
    (came,) = slots.run(
        at(2, *first_pair) + at(0, *second_pair) + at(4, top_piece, out_piece), [(pairs_t, FIRST)]
    )
    pairs_all = jnp.concatenate([pairs_t, came], axis=0)
    query_t = contract(query_weight, normed_attn, 0, 1)
    query_t = (rotate(query_t, cosine, sine) * score_scale).astype(low)
    slots.hold(query_t)
    (came,) = slots.run(at(3, *first_pair) + at(1, *second_pair), [(pairs_all, CORE)])
    pairs_all = jnp.concatenate([pairs_all, came], axis=0)
    out_weight = out_piece.weight()
    mixed, logs = [None] * seqs, [None] * seqs
    ahead = (seqs + 1) // 2
    for seq in range(ahead):
        mixed[seq], logs[seq] = attend(query_t, pairs_all, bias, seq)
    slots.run(at(2, *second_pair) + at(0, low_piece) + at(4, *first_pair))
    slots.hold(*mixed[:ahead])
    for seq in range(ahead, seqs):
        mixed[seq], logs[seq] = attend(query_t, pairs_all, bias, seq)
    slots.run(at(3, *second_pair) + at(1, low_piece))
    slots.hold(*mixed[ahead:])
    attended = jnp.concatenate([contract(m, perm, 0, 0).astype(low) for m in mixed], axis=0)
    resid = inputs + product(attended, out_weight)
    scale_ffn = rms_scale(resid)
    normed_ffn = product((resid * scale_ffn * norm_ffn).astype(low), perm).astype(low)
    slots.run(at(2, low_piece) + at(4, *second_pair))
    slots.hold(normed_ffn)
    gate_w, up_w = [first_pair[0].weight()], [first_pair[1].weight()]
    gate, up = [product(normed_ffn, gate_w[0])], [product(normed_ffn, up_w[0])]
    slots.run(at(3, low_piece))
    slots.hold(gate[0], up[0])
    slots.run(at(4, low_piece))
    gate_w.append(second_pair[0].weight())
    up_w.append(second_pair[1].weight())
    gate.append(product(normed_ffn, gate_w[1]))
    up.append(product(normed_ffn, up_w[1]))
    down_weight = join_blocks(
        ((top_piece.mine, top_piece.theirs), (low_piece.mine, low_piece.theirs)), order
    ).reshape(FF, D)
    parts = [silu_parts(g, u) for g, u in zip(gate, up)]
    hidden = jnp.concatenate([h for _, h in parts], axis=1)
    down_grad = cotangent.reshape(rows, D)
    top_grad, low_grad = down_grad_blocks(hidden, down_grad, place, top_ff)
    slots.hold(top_grad)

    half = n_dev // 2
    top_sum = Reduced(top_grad[:half], top_grad[half:], 0)
    low_sum = Reduced(low_grad[:half], low_grad[half:], 1)

    def reduced(left, right, right_dim, route):
        both = []
        for piece in (left[:, :split], left[:, split:]):
            grad = contract(piece, right, 0, right_dim).astype(low)
            both.append(grad.reshape(half, pad, -1))
        return Reduced(*both, route)

    def flat(grad):
        return grad[:cut].reshape(-1)

    slots.run(at(0, top_sum, low_sum))
    output = (resid + product(hidden, down_weight)).astype(low).reshape(seqs, block_len, D)
    gate_grad, up_grad = [], []
    for part in range(2):
        hidden_grad = product_right(
            down_grad, down_weight[part * half_ff : (part + 1) * half_ff]
        )
        a, b = silu_back(hidden_grad, gate[part], up[part], parts[part][0])
        gate_grad.append(a)
        up_grad.append(b)
    slots.hold(gate_grad[0], up_grad[0])
    slots.run(at(1, top_sum, low_sum))
    first_sums = [reduced(normed_ffn, gate_grad[0], 0, 0), reduced(normed_ffn, up_grad[0], 0, 1)]
    slots.hold(output)
    slots.run(at(2, top_sum, low_sum) + at(0, *first_sums))
    second_sums = [reduced(normed_ffn, gate_grad[1], 0, 0), reduced(normed_ffn, up_grad[1], 0, 1)]

    def collect_wide(value):
        high = lax.reduce_precision(value, 8, 7)
        return product_right(high.astype(low), perm) + product_right(
            (value - high).astype(low), perm
        )

    slots.run(at(1, *first_sums) + at(3, top_sum, low_sum) + at(0, *second_sums))
    grad_out = cotangent.astype(wide).reshape(rows, D)
    normed_grad = sum(
        product_right(g, w) for g, w in zip(gate_grad + up_grad, gate_w + up_w)
    )
    normed_grad = collect_wide(normed_grad)
    resid_grad, ffn_gain_grad = norm_back(resid, scale_ffn, norm_ffn, normed_grad)
    resid_grad = resid_grad + grad_out
    branch_grad = resid_grad.astype(low)
    grad_t = product_right(perm, product_right(branch_grad, out_weight).astype(low)).astype(low)
    slots.hold(grad_t)
    back = [None] * seqs
    slots.run(at(2, *first_sums) + at(1, *second_sums) + at(4, top_sum, low_sum))
    for seq in range(ahead):
        back[seq] = attend_back(query_t, pairs_all, bias, mixed[seq], logs[seq], grad_t, seq)
    slots.hold(*[b[0] for b in back[:ahead]])
    out_sum = reduced(attended, branch_grad, 0, 1)
    slots.run(at(2, *second_sums) + at(3, *first_sums) + at(0, out_sum))
    for seq in range(ahead, seqs):
        back[seq] = attend_back(query_t, pairs_all, bias, mixed[seq], logs[seq], grad_t, seq)
    pairs_part = jnp.concatenate([b[1] for b in back], axis=2)
    (came,) = slots.run(
        at(1, out_sum) + at(4, *first_sums) + at(3, *second_sums), [(pairs_part[2:], CORE)]
    )
    pairs_part = add_low(pairs_part[:2], came)
    query_low = jnp.concatenate([b[0] for b in back], axis=1)
    query_low = rotate_back(query_low * score_scale, cosine, sine).astype(low)
    query_sum = reduced(normed_attn, query_low, 1, 0)
    (came,) = slots.run(
        at(2, out_sum) + at(4, *second_sums) + at(0, query_sum), [(pairs_part[1], FIRST)]
    )
    pairs_grad = pairs_part[0].astype(wide) + came.astype(wide)
    pairs_low = jnp.concatenate(
        [rotate_back(pairs_grad[:KV], cosine, sine).astype(low), pairs_grad[KV:].astype(low)],
        axis=0,
    )
    pairs_sum = reduced(normed_attn, pairs_low, 1, 1)
    slots.run(at(1, query_sum) + at(3, out_sum) + at(0, pairs_sum))
    attn_normed_grad = collect_wide(
        contract(query_low, query_weight, 0, 1) + contract(pairs_low, kv_weight, 0, 1)
    )
    input_grad, attn_gain_grad = norm_back(inputs, scale_attn, norm_attn, attn_normed_grad)
    d_tokens = (input_grad + resid_grad).reshape(seqs, block_len, D)
    gains = jnp.stack([attn_gain_grad, ffn_gain_grad])
    slots.run(at(1, pairs_sum) + at(2, query_sum) + at(4, out_sum))
    (came,) = slots.run(at(2, pairs_sum) + at(3, query_sum), [(gains, CORE)])
    gains = gains + came
    a, b, c = slots.run(
        at(3, pairs_sum) + at(4, query_sum), [(gains, m) for m in (FIRST, SECOND, FIRST | SECOND)]
    )
    gains = (gains + a) + (b + c)
    a, b, c = slots.run(at(4, pairs_sum), [(gains, m) for m in (8, 16, 24)])
    gains = (gains + a) + (b + c)
    d_gate, d_up = [
        jnp.concatenate([x.result[:cut], y.result[:cut]], axis=1).reshape(-1)
        for x, y in zip(first_sums, second_sums)
    ]
    return (
        output,
        d_tokens,
        gains[0],
        flat(query_sum.result),
        flat(pairs_sum.result[:, :KV]),
        flat(pairs_sum.result[:, KV:]),
        flat(out_sum.result),
        gains[1],
        d_gate,
        d_up,
        jnp.concatenate([top_sum.result, low_sum.result], axis=0).reshape(-1),
    )


def body_whole(
    tokens, segment_ids, positions, norm_attn, w_query, w_key, w_value, w_out,
    norm_ffn, w_gate, w_up, w_down, cotangent,
):
    seqs, block_len, _ = tokens.shape
    n_dev = lax.axis_size(AXES)
    rows = seqs * block_len
    score_scale = HEAD_DIM ** (-0.5)

    def whole(shard, columns):
        return lax.all_gather(shard, AXES, axis=0, tiled=True).reshape(-1, columns)

    query_weight = whole(w_query, ATTN)
    kv_weight = jnp.concatenate([whole(w_key, KV), whole(w_value, KV)], axis=1)
    out_weight = whole(w_out, D)
    gate_weight, up_weight = whole(w_gate, FF), whole(w_up, FF)
    down_weight = whole(w_down, D)
    inputs = tokens.astype(wide).reshape(rows, D)
    grad_out = cotangent.astype(wide).reshape(rows, D)
    scale_attn = rms_scale(inputs)
    normed_attn = (inputs * scale_attn * norm_attn).astype(low)
    cosine, sine = rope_tables(positions.reshape(rows))
    bias = key_bias(ctx_gather(segment_ids), segment_ids, lax.axis_index("ctx"), ctx_masks())
    pairs_t = contract(kv_weight, normed_attn, 0, 1)
    pairs_t = jnp.concatenate(
        [rotate(pairs_t[:KV], cosine, sine).astype(low), pairs_t[KV:].astype(low)], axis=0
    )
    pairs_all = ctx_gather(pairs_t)
    query_t = contract(query_weight, normed_attn, 0, 1)
    query_t = (rotate(query_t, cosine, sine) * score_scale).astype(low)
    mixed, logs = zip(*[attend(query_t, pairs_all, bias, seq) for seq in range(seqs)])
    attended = jnp.concatenate([m.T for m in mixed], axis=0)
    resid = inputs + product(attended, out_weight)
    scale_ffn = rms_scale(resid)
    normed_ffn = (resid * scale_ffn * norm_ffn).astype(low)
    gate, up = product(normed_ffn, gate_weight), product(normed_ffn, up_weight)
    sigmoid, hidden = silu_parts(gate, up)
    output = (resid + product(hidden, down_weight)).astype(low).reshape(seqs, block_len, D)
    down_grad = cotangent.reshape(rows, D)
    gate_grad, up_grad = silu_back(product_right(down_grad, down_weight), gate, up, sigmoid)
    normed_grad = product_right(gate_grad, gate_weight) + product_right(up_grad, up_weight)
    resid_grad, ffn_gain_grad = norm_back(resid, scale_ffn, norm_ffn, normed_grad)
    resid_grad = resid_grad + grad_out
    branch_grad = resid_grad.astype(low)
    grad_t = product_right(branch_grad, out_weight).astype(low).T
    back = [
        attend_back(query_t, pairs_all, bias, mixed[seq], logs[seq], grad_t, seq)
        for seq in range(seqs)
    ]
    pairs_grad = ctx_scatter(jnp.concatenate([b[1] for b in back], axis=2))
    query_low = jnp.concatenate([b[0] for b in back], axis=1)
    query_low = rotate_back(query_low * score_scale, cosine, sine).astype(low)
    pairs_low = jnp.concatenate(
        [rotate_back(pairs_grad[:KV], cosine, sine).astype(low), pairs_grad[KV:].astype(low)],
        axis=0,
    )
    normed_grad = contract(query_low, query_weight, 0, 1) + contract(pairs_low, kv_weight, 0, 1)
    input_grad, attn_gain_grad = norm_back(inputs, scale_attn, norm_attn, normed_grad)
    d_tokens = (input_grad + resid_grad).reshape(seqs, block_len, D)

    def finish(left, right, right_dim):
        grad = contract(left, right, 0, right_dim).astype(low).reshape(n_dev, -1)
        grad = lax.psum_scatter(grad, AXES, scatter_dimension=0, tiled=True)
        return grad.astype(wide).reshape(-1)

    attn_gain_sum, ffn_gain_sum = lax.psum((attn_gain_grad, ffn_gain_grad), AXES)
    return (
        output,
        d_tokens,
        attn_gain_sum,
        finish(normed_attn, query_low, 1),
        finish(normed_attn, pairs_low[:KV], 1),
        finish(normed_attn, pairs_low[KV:], 1),
        finish(attended, branch_grad, 0),
        ffn_gain_sum,
        finish(normed_ffn, gate_grad, 0),
        finish(normed_ffn, up_grad, 0),
        finish(hidden, down_grad, 0),
    )


def solution(mesh):
    sizes = dict(mesh.shape)
    blocked = sizes["dp"] == 8 and sizes["ctx"] == 4
    body = body_blocked if blocked else body_whole
    one = P(AXES)
    tok = P("dp", "ctx", None)
    ids = P("dp", "ctx")
    in_specs = (tok, ids, ids, P(), one, one, one, one, P(), one, one, one, tok)
    out_specs = (tok, tok, P(), one, one, one, one, P(), one, one, one)
    return jax.shard_map(body, mesh=mesh, in_specs=in_specs, out_specs=out_specs, check_vma=False)
```

time: 584 us -> 593 us (1.015)
  waiting for transfers between devices: 237 us -> 207 us
  local copies, waits for them, and re-layouts: 76.3 us -> 104 us
  starting transfers between devices: 79.7 us -> 94.1 us
  matrix products: 83.8 us -> 74 us
    ppermute x86 -> x103, waiting for transfers between devices: 237 us -> 207 us  [swap(): return lax.ppermute(value, AXES, [(i, i ^ mask) for i in range(n)])]
    unnamed x170 -> x282, local copies, waits for them, and re-layouts: 20.1 us -> 46 us
    ppermute x86 -> x103, starting transfers between devices: 79.7 us -> 94.1 us  [swap(): return lax.ppermute(value, AXES, [(i, i ^ mask) for i in range(n)])]
    dot_general x16 -> x20, matrix products: 38.7 us -> 30.6 us  [contract(): lax.dot_general(left, right, (((left_dim,), (right_dim,)), ((), ())), pre...]
    concatenate x35 -> x39, other arithmetic: 12.8 us -> 20.3 us  [the longest x27 13.6 us: take(): self.now = jnp.concatenate(parts, axis=0)]
    slice x40 -> x49, local copies, waits for them, and re-layouts: 9.86 us -> 16.5 us  [the longest x25 6.49 us: give(): return (self.now[n:], mask)]
    convert_element_type x4 -> x3, local copies, waits for them, and re-layouts: 12.6 us -> 6.04 us  [the longest x2 4.53 us: reduced(): grad = contract(piece, right, 0, right_dim).astype(low)]
    convert_element_type x21 -> x37, other arithmetic: 17.9 us -> 13.6 us  [add_low(): return (left.astype(wide) + right.astype(wide)).astype(low)]
  transfers between devices with their start and end apart: 86 -> 103, of which waited for: 41 -> 45; matrix products, arithmetic and copies ran while one was open for 28% -> 27% of each run, Pallas kernels for 9% -> 8%
where the time goes in v3:
time: 593 us; the launch traced here: 584 us
  waiting for transfers between devices  207 us (35%)
  local copies, waits for them, and re-layouts  104 us (18%)
  starting transfers between devices  94.1 us (16%)
  matrix products  74 us (12%)
  Pallas kernels  51.8 us (9%)
  other arithmetic  49.5 us (8%)
    ppermute x103, waiting for transfers between devices, swap(): return lax.ppermute(value, AXES, [(i, i ^ mask) for i in range(n)])  207 us
    ppermute x103, starting transfers between devices, swap(): return lax.ppermute(value, AXES, [(i, i ^ mask) for i in range(n)])  94.1 us
    unnamed x282, local copies, waits for them, and re-layouts  46 us
    dot_general x20, matrix products, contract(): lax.dot_general(left, right, (((left_dim,), (right_dim,)), ((), ())), pre...  30.6 us
    pallas_call x2, Pallas kernels, attend_back(): pl.pallas_call(attend_back_kernel, grid=(1,), in_specs=[columns, pairs, b...  25.2 us
    dot_general x11, matrix products, product_right(): lax.dot_general(left, right, (((1,), (1,)), ((), ())), preferred_element_...  23.7 us
    pallas_call x2, Pallas kernels, attend(): pl.pallas_call(attend_kernel, grid=(1,), in_specs=[columns, pairs, bias_s...  20.2 us
    dot_general x8, matrix products, product(): return jnp.dot(left, right, preferred_element_type=wide)  19.7 us
  transfers between devices with their start and end apart: 103, of which 45 were waited for; matrix products, arithmetic and copies ran while one was open for 27% of the time, Pallas kernels for 8%

profile of v3, /device:TPU:0, one launch (start us, length us, event | category | flops | bytes accessed | tf_op | source)
XLA Modules:
  0.0 583.9 jit_solution(8592037620466108440)
XLA Ops:
  55.2 12.6 %collective-permute-done.13 = bf16[2,32,960]{2,1,0:T(8,128)(2,1)S(1)} collective-permute-done((bf16[2,32,960]{2,1,0:T(8,128)(2,1)S(1)}, bf16[2,32,960]{2,1,0:T(8,128)(2,1)S(1)}, u32[]{:S(2)}, u32[]{:S(2)}) %collective-permute-start.13) | collective-permute-done | bytes 122912 | tf_op jit(solution)/shard_map/ppermute | solution.py:77
  122.6 17.2 %collective-permute-done.26 = bf16[4,32,1280]{2,1,0:T(8,128)(2,1)S(1)} collective-permute-done((bf16[4,32,1280]{2,1,0:T(8,128)(2,1)S(1)}, bf16[4,32,1280]{2,1,0:T(8,128)(2,1)S(1)}, u32[]{:S(2)}, u32[]{:S(2)}) %collective-permute-start.26) | collective-permute-done | bytes 327712 | tf_op jit(solution)/shard_map/ppermute | solution.py:77
  147.9 7.3 %collective-permute-done.34 = bf16[2,32,1280]{2,1,0:T(8,128)(2,1)S(1)} collective-permute-done((bf16[2,32,1280]{2,1,0:T(8,128)(2,1)S(1)}, bf16[2,32,1280]{2,1,0:T(8,128)(2,1)S(1)}, u32[]{:S(2)}, u32[]{:S(2)}) %collective-permute-start.34) | collective-permute-done | bytes 163872 | tf_op jit(solution)/shard_map/ppermute | solution.py:77
  163.1 10.3 %attend.2 = (bf16[960,256]{1,0:T(8,128)(2,1)S(1)}, f32[1,15,256]{2,1,0:T(8,128)S(1)}) custom-call(bf16[960,512]{1,0:T(8,128)(2,1)S(1)} %bitcast.222, bf16[4,640,512]{2,1,0:T(8,128)(2,1)S(1)} %pad_maximum_fusion.kv_ref, f32[2,1024,256]{2,1,0:T(8,128)S(1)} %and_select_fusion.bias_ref), custom_call_target="tpu_custom_call" | custom-call | flops 4026531840 | bytes 8388608 | tf_op jit(solution)/shard_map/attend/pallas_call | solution.py:348
  174.3 9.9 %attend.3 = (bf16[960,256]{1,0:T(8,128)(2,1)S(1)}, f32[1,15,256]{2,1,0:T(8,128)S(1)}) custom-call(bf16[960,512]{1,0:T(8,128)(2,1)S(1)} %bitcast.223, bf16[4,640,512]{2,1,0:T(8,128)(2,1)S(1)} %pad_maximum_fusion.kv_ref, f32[2,1024,256]{2,1,0:T(8,128)S(1)} %and_select_fusion.bias_ref), custom_call_target="tpu_custom_call" | custom-call | flops 4026531840 | bytes 8388608 | tf_op jit(solution)/shard_map/attend/pallas_call | solution.py:348
  193.0 4.8 collective-permute-done.42
  215.3 6.6 %collective-permute-done.46 = bf16[4,32,960]{2,1,0:T(8,128)(2,1)S(1)} collective-permute-done((bf16[4,32,960]{2,1,0:T(8,128)(2,1)S(1)}, bf16[4,32,960]{2,1,0:T(8,128)(2,1)S(1)}, u32[]{:S(2)}, u32[]{:S(2)}) %collective-permute-start.46) | collective-permute-done | bytes 245792 | tf_op jit(solution)/shard_map/ppermute | solution.py:77
  226.6 8.4 %collective-permute-done.47 = bf16[8,32,960]{2,1,0:T(8,128)(2,1)S(1)} collective-permute-done((bf16[8,32,960]{2,1,0:T(8,128)(2,1)S(1)}, bf16[8,32,960]{2,1,0:T(8,128)(2,1)S(1)}, u32[]{:S(2)}, u32[]{:S(2)}) %collective-permute-start.47) | collective-permute-done | bytes 491552 | tf_op jit(solution)/shard_map/ppermute | solution.py:77
  276.7 5.6 fusion.43.do_ref
  291.6 12.5 %attend_back.3 = (f32[960,256]{1,0:T(8,128)S(1)}, bf16[4,640,256]{2,1,0:T(8,128)(2,1)S(1)}) custom-call(bf16[960,512]{1,0:T(8,128)(2,1)S(1)} %bitcast.224, bf16[4,640,512]{2,1,0:T(8,128)(2,1)} %copy-done.1, f32[2,1024,256]{2,1,0:T(8,128)} %copy-done.2, bf16[960,256]{1,0:T(8,128)(2,1)S(1)} %copy-done.10, f32[1,15,256]{2,1,0:T(8,128)S(1)} %get-tuple-element.173.lse_ref, ...), custom_call_target="tpu_custom_call" | custom-call | flops 10066329600 | bytes 14680064 | tf_op jit(solution)/shard_map/attend_back/pallas_call | solution.py:371
  304.2 12.7 %attend_back.2 = (f32[960,256]{1,0:T(8,128)S(1)}, bf16[4,640,256]{2,1,0:T(8,128)(2,1)S(1)}) custom-call(bf16[960,512]{1,0:T(8,128)(2,1)S(1)} %bitcast.225, bf16[4,640,512]{2,1,0:T(8,128)(2,1)} %copy-done.1, f32[2,1024,256]{2,1,0:T(8,128)} %copy-done.2, bf16[960,256]{1,0:T(8,128)(2,1)S(1)} %copy-done.8, f32[1,15,256]{2,1,0:T(8,128)S(1)} %get-tuple-element.171.lse_ref, ...), custom_call_target="tpu_custom_call" | custom-call | flops 10066329600 | bytes 14680064 | tf_op jit(solution)/shard_map/attend_back/pallas_call | solution.py:371
  336.6 8.5 %collective-permute-done.52 = bf16[8,32,960]{2,1,0:T(8,128)(2,1)S(1)} collective-permute-done((bf16[8,32,960]{2,1,0:T(8,128)(2,1)S(1)}, bf16[8,32,960]{2,1,0:T(8,128)(2,1)S(1)}, u32[]{:S(2)}, u32[]{:S(2)}) %collective-permute-start.52) | collective-permute-done | bytes 491552 | tf_op jit(solution)/shard_map/ppermute | solution.py:77
  345.3 6.6 %collective-permute-done.51 = bf16[8,48,960]{2,1,0:T(8,128)(2,1)S(1)} collective-permute-done((bf16[8,48,960]{2,1,0:T(8,128)(2,1)S(1)}, bf16[8,48,960]{2,1,0:T(8,128)(2,1)S(1)}, u32[]{:S(2)}, u32[]{:S(2)}) %collective-permute-start.51) | collective-permute-done | bytes 737312 | tf_op jit(solution)/shard_map/ppermute | solution.py:77
  376.0 8.2 %collective-permute-done.62 = bf16[2,32,960]{2,1,0:T(8,128)(2,1)S(1)} collective-permute-done((bf16[2,32,960]{2,1,0:T(8,128)(2,1)S(1)}, bf16[2,32,960]{2,1,0:T(8,128)(2,1)S(1)}, u32[]{:S(2)}, u32[]{:S(2)}) %collective-permute-start.62) | collective-permute-done | bytes 122912 | tf_op jit(solution)/shard_map/ppermute | solution.py:77
  388.1 10.4 %collective-permute-done.59 = bf16[8,32,1280]{2,1,0:T(8,128)(2,1)S(1)} collective-permute-done((bf16[8,32,1280]{2,1,0:T(8,128)(2,1)S(1)}, bf16[8,32,1280]{2,1,0:T(8,128)(2,1)S(1)}, u32[]{:S(2)}, u32[]{:S(2)}) %collective-permute-start.59) | collective-permute-done | bytes 655392 | tf_op jit(solution)/shard_map/ppermute | solution.py:77
  428.4 6.2 %collective-permute-done.65 = bf16[4,32,1280]{2,1,0:T(8,128)(2,1)S(1)} collective-permute-done((bf16[4,32,1280]{2,1,0:T(8,128)(2,1)}, bf16[4,32,1280]{2,1,0:T(8,128)(2,1)S(1)}, u32[]{:S(2)}, u32[]{:S(2)}) %collective-permute-start.65) | collective-permute-done | bytes 327712 | tf_op jit(solution)/shard_map/ppermute | solution.py:77
  438.2 7.1 %collective-permute-done.64 = bf16[8,32,1280]{2,1,0:T(8,128)(2,1)S(1)} collective-permute-done((bf16[8,32,1280]{2,1,0:T(8,128)(2,1)}, bf16[8,32,1280]{2,1,0:T(8,128)(2,1)S(1)}, u32[]{:S(2)}, u32[]{:S(2)}) %collective-permute-start.64) | collective-permute-done | bytes 655392 | tf_op jit(solution)/shard_map/ppermute | solution.py:77
  448.9 5.8 %collective-permute-done.71 = bf16[2,32,1280]{2,1,0:T(8,128)(2,1)S(1)} collective-permute-done((bf16[2,32,1280]{2,1,0:T(8,128)(2,1)S(1)}, bf16[2,32,1280]{2,1,0:T(8,128)(2,1)S(1)}, u32[]{:S(2)}, u32[]{:S(2)}) %collective-permute-start.71) | collective-permute-done | bytes 163872 | tf_op jit(solution)/shard_map/ppermute | solution.py:77
  467.8 9.0 %collective-permute-done.77 = bf16[2,32,1280]{2,1,0:T(8,128)(2,1)S(1)} collective-permute-done((bf16[2,32,1280]{2,1,0:T(8,128)(2,1)}, bf16[2,32,1280]{2,1,0:T(8,128)(2,1)S(1)}, u32[]{:S(2)}, u32[]{:S(2)}) %collective-permute-start.77) | collective-permute-done | bytes 163872 | tf_op jit(solution)/shard_map/ppermute | solution.py:77
  496.3 12.0 %collective-permute-done.82 = bf16[4,32,960]{2,1,0:T(8,128)(2,1)} collective-permute-done((bf16[4,32,960]{2,1,0:T(8,128)(2,1)}, bf16[4,32,960]{2,1,0:T(8,128)(2,1)}, u32[]{:S(2)}, u32[]{:S(2)}) %collective-permute-start.82) | collective-permute-done | bytes 245792 | tf_op jit(solution)/shard_map/ppermute | solution.py:77
  524.0 5.3 collective-permute-done.87
  529.4 6.2 %collective-permute-done.86 = bf16[8,32,960]{2,1,0:T(8,128)(2,1)S(1)} collective-permute-done((bf16[8,32,960]{2,1,0:T(8,128)(2,1)S(1)}, bf16[8,32,960]{2,1,0:T(8,128)(2,1)S(1)}, u32[]{:S(2)}, u32[]{:S(2)}) %collective-permute-start.86) | collective-permute-done | bytes 491552 | tf_op jit(solution)/shard_map/ppermute | solution.py:77
  539.9 5.7 collective-permute-done.89
  555.2 8.6 %collective-permute-done.93 = bf16[2,32,960]{2,1,0:T(8,128)(2,1)S(1)} collective-permute-done((bf16[2,32,960]{2,1,0:T(8,128)(2,1)S(1)}, bf16[2,32,960]{2,1,0:T(8,128)(2,1)S(1)}, u32[]{:S(2)}, u32[]{:S(2)}) %collective-permute-start.93) | collective-permute-done | bytes 122912 | tf_op jit(solution)/shard_map/ppermute | solution.py:77
  (726 shorter events, 373.0 us)
Async XLA Ops:
  3.1 19.7 %collective-permute-start.1 = (bf16[1,32,640]{2,1,0:T(8,128)(2,1)}, bf16[1,32,640]{2,1,0:T(8,128)(2,1)}, u32[]{:S(2)}, u32[]{:S(2)}) collective-permute-start(bf16[1,32,640]{2,1,0:T(8,128)(2,1)} %get-tuple-element.271), channel_id=1, source_target_pairs={{0,8},{1,9},{2,10},{3,11},{4,12},{5,13},{6,14},{7,15},{8,0},{9,1},... | collective-permute-start | bytes 122888 | tf_op jit(solution)/shard_map/ppermute | solution.py:77
  86.5 25.5 %collective-permute-start.22 = (bf16[8,48,960]{2,1,0:T(8,128)(2,1)}, bf16[8,48,960]{2,1,0:T(8,128)(2,1)}, u32[]{:S(2)}, u32[]{:S(2)}) collective-permute-start(bf16[8,48,960]{2,1,0:T(8,128)(2,1)} %pad_maximum_fusion.7), channel_id=1, source_target_pairs={{0,2},{1,3},{2,0},{3,1},{4,6},{5,7},{6,4},{7,5},{8,10},{9,11},{10,... | collective-permute-start | bytes 2211848 | tf_op jit(solution)/shard_map/ppermute | solution.py:77
  117.1 24.7 %collective-permute-start.24 = (bf16[1,640,512]{2,1,0:T(8,128)(2,1)S(1)}, bf16[1,640,512]{2,1,0:T(8,128)(2,1)S(1)}, u32[]{:S(2)}, u32[]{:S(2)}) collective-permute-start(bf16[1,640,512]{2,1,0:T(8,128)(2,1)S(1)} %copy-done.19), channel_id=1, source_target_pairs={{0,2},{1,3},{2,0},{3,1},{4,6},{5,7},{6,4},{7,5},{8,10},{9,11},{10,... | collective-permute-start | bytes 1966088 | tf_op jit(solution)/shard_map/ppermute | solution.py:77
  117.6 22.2 %collective-permute-start.26 = (bf16[4,32,1280]{2,1,0:T(8,128)(2,1)S(1)}, bf16[4,32,1280]{2,1,0:T(8,128)(2,1)S(1)}, u32[]{:S(2)}, u32[]{:S(2)}) collective-permute-start(bf16[4,32,1280]{2,1,0:T(8,128)(2,1)S(1)} %pad_maximum_fusion.24), channel_id=1, source_target_pairs={{0,2},{1,3},{2,0},{3,1},{4,6},{5,7},{6,4},{7,5},{8,10},{9,11},{10,... | collective-permute-start | bytes 983048 | tf_op jit(solution)/shard_map/ppermute | solution.py:77
  119.2 21.6 %collective-permute-start.25 = (bf16[4,32,1280]{2,1,0:T(8,128)(2,1)S(1)}, bf16[4,32,1280]{2,1,0:T(8,128)(2,1)S(1)}, u32[]{:S(2)}, u32[]{:S(2)}) collective-permute-start(bf16[4,32,1280]{2,1,0:T(8,128)(2,1)S(1)} %pad_maximum_fusion.23), channel_id=1, source_target_pairs={{0,4},{1,5},{2,6},{3,7},{4,0},{5,1},{6,2},{7,3},{8,12},{9,13},{10,... | collective-permute-start | bytes 983048 | tf_op jit(solution)/shard_map/ppermute | solution.py:77
  120.7 21.3 %collective-permute-start.29 = (bf16[16,48,960]{2,1,0:T(8,128)(2,1)}, bf16[16,48,960]{2,1,0:T(8,128)(2,1)S(1)}, u32[]{:S(2)}, u32[]{:S(2)}) collective-permute-start(bf16[16,48,960]{2,1,0:T(8,128)(2,1)} %constant_dynamic-update-slice_fusion.24.a_ref), channel_id=1, source_target_pairs={{0,1},{1,0},{2,3},{3,2},{4,5},{5,4},{6,7},{7,6},{8,9},{9,8},{10,11... | collective-permute-start | bytes 4423688 | tf_op jit(solution)/shard_map/ppermute | solution.py:77
  120.7 21.2 %collective-permute-start.30 = (bf16[16,32,960]{2,1,0:T(8,128)(2,1)S(1)}, bf16[16,32,960]{2,1,0:T(8,128)(2,1)S(1)}, u32[]{:S(2)}, u32[]{:S(2)}) collective-permute-start(bf16[16,32,960]{2,1,0:T(8,128)(2,1)S(1)} %get-tuple-element.150), channel_id=1, source_target_pairs={{0,1},{1,0},{2,3},{3,2},{4,5},{5,4},{6,7},{7,6},{8,9},{9,8},{10,11... | collective-permute-start | bytes 2949128 | tf_op jit(solution)/shard_map/ppermute | solution.py:77
  160.3 24.9 %collective-permute-start.39 = (bf16[4,32,1280]{2,1,0:T(8,128)(2,1)S(1)}, bf16[4,32,1280]{2,1,0:T(8,128)(2,1)S(1)}, u32[]{:S(2)}, u32[]{:S(2)}) collective-permute-start(bf16[4,32,1280]{2,1,0:T(8,128)(2,1)S(1)} %pad_maximum_fusion.26), channel_id=1, source_target_pairs={{0,2},{1,3},{2,0},{3,1},{4,6},{5,7},{6,4},{7,5},{8,10},{9,11},{10,... | collective-permute-start | bytes 983048 | tf_op jit(solution)/shard_map/ppermute | solution.py:77
  160.8 24.4 %collective-permute-start.38 = (bf16[4,32,1280]{2,1,0:T(8,128)(2,1)S(1)}, bf16[4,32,1280]{2,1,0:T(8,128)(2,1)S(1)}, u32[]{:S(2)}, u32[]{:S(2)}) collective-permute-start(bf16[4,32,1280]{2,1,0:T(8,128)(2,1)S(1)} %pad_maximum_fusion.25), channel_id=1, source_target_pairs={{0,4},{1,5},{2,6},{3,7},{4,0},{5,1},{6,2},{7,3},{8,12},{9,13},{10,... | collective-permute-start | bytes 983048 | tf_op jit(solution)/shard_map/ppermute | solution.py:77
  162.3 23.0 %collective-permute-start.36 = (bf16[16,32,1280]{2,1,0:T(8,128)(2,1)S(1)}, bf16[16,32,1280]{2,1,0:T(8,128)(2,1)S(1)}, u32[]{:S(2)}, u32[]{:S(2)}) collective-permute-start(bf16[16,32,1280]{2,1,0:T(8,128)(2,1)S(1)} %get-tuple-element.158), channel_id=1, source_target_pairs={{0,1},{1,0},{2,3},{3,2},{4,5},{5,4},{6,7},{7,6},{8,9},{9,8},{10,11... | collective-permute-start | bytes 3932168 | tf_op jit(solution)/shard_map/ppermute | solution.py:77
  162.3 23.0 %collective-permute-start.37 = (bf16[16,32,1280]{2,1,0:T(8,128)(2,1)S(1)}, bf16[16,32,1280]{2,1,0:T(8,128)(2,1)S(1)}, u32[]{:S(2)}, u32[]{:S(2)}) collective-permute-start(bf16[16,32,1280]{2,1,0:T(8,128)(2,1)S(1)} %get-tuple-element.159), channel_id=1, source_target_pairs={{0,1},{1,0},{2,3},{3,2},{4,5},{5,4},{6,7},{7,6},{8,9},{9,8},{10,11... | collective-permute-start | bytes 3932168 | tf_op jit(solution)/shard_map/ppermute | solution.py:77
  162.8 22.3 %collective-permute-start.40 = (bf16[1,32,960]{2,1,0:T(8,128)(2,1)S(1)}, bf16[1,32,960]{2,1,0:T(8,128)(2,1)S(1)}, u32[]{:S(2)}, u32[]{:S(2)}) collective-permute-start(bf16[1,32,960]{2,1,0:T(8,128)(2,1)S(1)} %copy-done.36), channel_id=1, source_target_pairs={{0,8},{1,9},{2,10},{3,11},{4,12},{5,13},{6,14},{7,15},{8,0},{9,1},... | collective-permute-start | bytes 184328 | tf_op jit(solution)/shard_map/ppermute | solution.py:77
  291.1 36.7 %collective-permute-start.50 = (bf16[16,32,960]{2,1,0:T(8,128)(2,1)}, bf16[16,32,960]{2,1,0:T(8,128)(2,1)S(1)}, u32[]{:S(2)}, u32[]{:S(2)}) collective-permute-start(bf16[16,32,960]{2,1,0:T(8,128)(2,1)} %slice.477), channel_id=1, source_target_pairs={{0,1},{1,0},{2,3},{3,2},{4,5},{5,4},{6,7},{7,6},{8,9},{9,8},{10,11... | collective-permute-start | bytes 2949128 | tf_op jit(solution)/shard_map/ppermute | solution.py:77
  291.6 36.8 %collective-permute-start.49 = (bf16[16,48,960]{2,1,0:T(8,128)(2,1)}, bf16[16,48,960]{2,1,0:T(8,128)(2,1)}, u32[]{:S(2)}, u32[]{:S(2)}) collective-permute-start(bf16[16,48,960]{2,1,0:T(8,128)(2,1)} %slice.476), channel_id=1, source_target_pairs={{0,1},{1,0},{2,3},{3,2},{4,5},{5,4},{6,7},{7,6},{8,9},{9,8},{10,11... | collective-permute-start | bytes 4423688 | tf_op jit(solution)/shard_map/ppermute | solution.py:77
  332.2 19.7 %collective-permute-start.51 = (bf16[8,48,960]{2,1,0:T(8,128)(2,1)S(1)}, bf16[8,48,960]{2,1,0:T(8,128)(2,1)S(1)}, u32[]{:S(2)}, u32[]{:S(2)}) collective-permute-start(bf16[8,48,960]{2,1,0:T(8,128)(2,1)S(1)} %slice.611), channel_id=1, source_target_pairs={{0,2},{1,3},{2,0},{3,1},{4,6},{5,7},{6,4},{7,5},{8,10},{9,11},{10,... | collective-permute-start | bytes 2211848 | tf_op jit(solution)/shard_map/ppermute | solution.py:77
  375.5 24.7 %collective-permute-start.60 = (bf16[16,32,1280]{2,1,0:T(8,128)(2,1)S(1)}, bf16[16,32,1280]{2,1,0:T(8,128)(2,1)S(1)}, u32[]{:S(2)}, u32[]{:S(2)}) collective-permute-start(bf16[16,32,1280]{2,1,0:T(8,128)(2,1)S(1)} %bitcast.274), channel_id=1, source_target_pairs={{0,1},{1,0},{2,3},{3,2},{4,5},{5,4},{6,7},{7,6},{8,9},{9,8},{10,11... | collective-permute-start | bytes 3932168 | tf_op jit(solution)/shard_map/ppermute | solution.py:77
  375.5 26.1 %collective-permute-start.57 = (bf16[16,32,1280]{2,1,0:T(8,128)(2,1)S(1)}, bf16[16,32,1280]{2,1,0:T(8,128)(2,1)S(1)}, u32[]{:S(2)}, u32[]{:S(2)}) collective-permute-start(bf16[16,32,1280]{2,1,0:T(8,128)(2,1)S(1)} %bitcast.273), channel_id=1, source_target_pairs={{0,1},{1,0},{2,3},{3,2},{4,5},{5,4},{6,7},{7,6},{8,9},{9,8},{10,11... | collective-permute-start | bytes 3932168 | tf_op jit(solution)/shard_map/ppermute | solution.py:77
  403.7 22.1 %collective-permute-start.68 = (bf16[1,32,960]{2,1,0:T(8,128)(2,1)}, bf16[1,32,960]{2,1,0:T(8,128)(2,1)}, u32[]{:S(2)}, u32[]{:S(2)}) collective-permute-start(bf16[1,32,960]{2,1,0:T(8,128)(2,1)} %slice.638), channel_id=1, source_target_pairs={{0,8},{1,9},{2,10},{3,11},{4,12},{5,13},{6,14},{7,15},{8,0},{9,1},... | collective-permute-start | bytes 184328 | tf_op jit(solution)/shard_map/ppermute | solution.py:77
  403.7 23.5 %collective-permute-start.66 = (bf16[4,32,1280]{2,1,0:T(8,128)(2,1)}, bf16[4,32,1280]{2,1,0:T(8,128)(2,1)}, u32[]{:S(2)}, u32[]{:S(2)}) collective-permute-start(bf16[4,32,1280]{2,1,0:T(8,128)(2,1)} %slice.631), channel_id=1, source_target_pairs={{0,2},{1,3},{2,0},{3,1},{4,6},{5,7},{6,4},{7,5},{8,10},{9,11},{10,... | collective-permute-start | bytes 983048 | tf_op jit(solution)/shard_map/ppermute | solution.py:77
  421.7 23.8 %collective-permute-start.67 = (bf16[1,48,960]{2,1,0:T(8,128)(2,1)}, bf16[1,48,960]{2,1,0:T(8,128)(2,1)S(1)}, u32[]{:S(2)}, u32[]{:S(2)}) collective-permute-start(bf16[1,48,960]{2,1,0:T(8,128)(2,1)} %slice.636), channel_id=1, source_target_pairs={{0,8},{1,9},{2,10},{3,11},{4,12},{5,13},{6,14},{7,15},{8,0},{9,1},... | collective-permute-start | bytes 276488 | tf_op jit(solution)/shard_map/ppermute | solution.py:77
  424.0 21.2 %collective-permute-start.64 = (bf16[8,32,1280]{2,1,0:T(8,128)(2,1)}, bf16[8,32,1280]{2,1,0:T(8,128)(2,1)S(1)}, u32[]{:S(2)}, u32[]{:S(2)}) collective-permute-start(bf16[8,32,1280]{2,1,0:T(8,128)(2,1)} %pad_maximum_fusion.13), channel_id=1, source_target_pairs={{0,4},{1,5},{2,6},{3,7},{4,0},{5,1},{6,2},{7,3},{8,12},{9,13},{10,... | collective-permute-start | bytes 1966088 | tf_op jit(solution)/shard_map/ppermute | solution.py:77
  486.6 22.9 %collective-permute-start.80 = (bf16[640,512]{1,0:T(8,128)(2,1)}, bf16[640,512]{1,0:T(8,128)(2,1)}, u32[]{:S(2)}, u32[]{:S(2)}) collective-permute-start(bf16[640,512]{1,0:T(8,128)(2,1)} %slice_bitcast_fusion), channel_id=1, source_target_pairs={{0,2},{1,3},{2,0},{3,1},{4,6},{5,7},{6,4},{7,5},{8,10},{9,11},{10,... | collective-permute-start | bytes 1966088 | tf_op jit(solution)/shard_map/ppermute | solution.py:77
  486.9 21.4 %collective-permute-start.82 = (bf16[4,32,960]{2,1,0:T(8,128)(2,1)}, bf16[4,32,960]{2,1,0:T(8,128)(2,1)}, u32[]{:S(2)}, u32[]{:S(2)}) collective-permute-start(bf16[4,32,960]{2,1,0:T(8,128)(2,1)} %slice.663), channel_id=1, source_target_pairs={{0,2},{1,3},{2,0},{3,1},{4,6},{5,7},{6,4},{7,5},{8,10},{9,11},{10,... | collective-permute-start | bytes 737288 | tf_op jit(solution)/shard_map/ppermute | solution.py:77
  488.6 31.9 %collective-permute-start.81 = (bf16[16,32,960]{2,1,0:T(8,128)(2,1)}, bf16[16,32,960]{2,1,0:T(8,128)(2,1)}, u32[]{:S(2)}, u32[]{:S(2)}) collective-permute-start(bf16[16,32,960]{2,1,0:T(8,128)(2,1)} %bitcast.50), channel_id=1, source_target_pairs={{0,1},{1,0},{2,3},{3,2},{4,5},{5,4},{6,7},{7,6},{8,9},{9,8},{10,11... | collective-permute-start | bytes 2949128 | tf_op jit(solution)/shard_map/ppermute | solution.py:77
  (195 other events, 1889.1 us)

commit v4 on v3

--- a/solution.py
+++ b/solution.py
@@ -102,78 +102,90 @@
     def __init__(self):
         self.deps = ()
 
-    def send(self, pairs):
-        values = tuple(value for value, _ in pairs)
+    def after(self, value):
+        return lax.optimization_barrier((value, self.deps))[0]
+
+    def hold(self, *values):
+        self.deps = self.deps + values
+
+    def run(self, moves, late=()):
+        values = tuple(move.give() for move in (*moves, *late))
         if self.deps:
             values = lax.optimization_barrier((values, self.deps))[0]
-        came = [swap(value, mask) for value, (_, mask) in zip(values, pairs)]
-        self.deps = tuple(came)
-        return came
-
-    def hold(self, *values):
-        self.deps = self.deps + values
-
-    def after(self, value):
-        return lax.optimization_barrier((value, self.deps))[0]
-
-    def run(self, moves, extra=()):
-        pairs = [piece.give(stage) for piece, stage in moves]
-        came = self.send(pairs + list(extra))
-        for (piece, stage), value in zip(moves, came):
-            piece.take(stage, value)
-        return came[len(moves) :]
-
-
-class Gathered:
-    def __init__(self, block, route):
-        self.now, self.route = block[None], route
-
-    def give(self, stage):
-        near = (FIRST, SECOND) if self.route else (SECOND, FIRST)
-        return self.now, (8, 16, *near, CORE)[stage]
-
-    def take(self, stage, came):
-        if stage == 2:
-            self.own, self.side = self.now, came
-        if stage == 3 and self.route:
-            n = came.shape[0] // 2
-            parts = [self.own, came[:n], self.side, came[n:]]
+        for i, (move, value) in enumerate(zip((*moves, *late), values)):
+            if i == 0:
+                self.deps = ()
+            came = swap(value, move.mask)
+            if i < len(moves):
+                self.deps += (came,)
+            move.take(came)
+
+
+class Move:
+    def __init__(self, value, mask):
+        self.value, self.mask = value, mask
+
+    def give(self):
+        return self.value
+
+    def take(self, came):
+        self.came = came
+
+
+class Spread(Move):
+    def take(self, came):
+        self.both = jnp.concatenate([self.value, came], axis=0)
+
+
+class SpreadBetween(Spread):
+    def __init__(self, first, mask):
+        self.own, self.side = first.value, first.came
+        super().__init__(first.both, mask)
+
+    def take(self, came):
+        n = came.shape[0] // 2
+        self.both = jnp.concatenate([self.own, came[:n], self.side, came[n:]], axis=0)
+
+
+class SpreadFirst(Spread):
+    def take(self, came):
+        self.came = came
+        super().take(came)
+
+
+class Fold(Move):
+    def __init__(self, value, mask, last=False):
+        self.n, self.last = value.shape[0] // 2, last
+        super().__init__(value, mask)
+
+    def give(self):
+        return self.value[self.n :]
+
+    def take(self, came):
+        if self.last:
+            self.sum = self.value[0].astype(wide) + came[0].astype(wide)
         else:
-            parts = [self.now, came]
-        if stage == 4:
-            self.mine, self.theirs = self.now, came
-        else:
-            self.now = jnp.concatenate(parts, axis=0)
-
-    def weight(self):
-        whole = jnp.concatenate([self.mine, self.theirs], axis=0)
-        return whole.reshape(-1, whole.shape[-1])
-
-
-class Reduced:
-    def __init__(self, mine, theirs, route):
-        self.mine, self.theirs, self.route = mine, theirs, route
-
-    def give(self, stage):
-        near = (SECOND, FIRST) if self.route else (FIRST, SECOND)
-        mask = (CORE, *near, 16, 8)[stage]
-        if stage == 0:
-            return self.theirs, mask
-        n = self.now.shape[0] // 2
-        if stage == 1 and self.route:
-            q = n // 2
-            self.keep = jnp.concatenate([self.now[:q], self.now[n : n + q]], axis=0)
-            return jnp.concatenate([self.now[q:n], self.now[n + q :]], axis=0), mask
-        self.keep = self.now[:n]
-        return self.now[n:], mask
-
-    def take(self, stage, came):
-        if stage == 0:
-            self.now = add_low(self.mine, came)
-        elif stage == 4:
-            self.result = self.keep[0].astype(wide) + came[0].astype(wide)
-        else:
-            self.now = add_low(self.keep, came)
+            self.sum = add_low(self.value[: self.n], came)
+
+
+class FoldPair(Fold):
+    def __init__(self, mine, theirs, mask):
+        self.value, self.theirs, self.mask, self.last = mine, theirs, mask, False
+        self.n = mine.shape[0]
+
+    def give(self):
+        return self.theirs
+
+
+class FoldBetween(Fold):
+    def give(self):
+        q = self.n // 2
+        return jnp.concatenate([self.value[q : self.n], self.value[self.n + q :]], axis=0)
+
+    def take(self, came):
+        q = self.n // 2
+        kept = jnp.concatenate([self.value[:q], self.value[self.n : self.n + q]], axis=0)
+        self.sum = add_low(kept, came)
 
 
 def ctx_masks():
@@ -205,32 +217,35 @@
     return pl.BlockSpec(memory_space=pltpu.VMEM)
 
 
-def join_blocks(parts, order):
-    (a, b), (c, d) = parts
+def join_blocks(tops, lows, order, low_rows):
+    (a, b), (c, d) = tops, lows
     half, top, columns = a.shape
-    bottom = c.shape[1]
-
-    def kernel(order_ref, a_ref, b_ref, c_ref, d_ref, out_ref):
+    rest = c.shape[1] - low_rows
+
+    def kernel(order_ref, a_ref, b_ref, c_ref, d_ref, down_ref, out_ref):
         def step(p, _):
             near, far = order_ref[p], order_ref[p + half]
-            out_ref[near, :top, :] = a_ref[p]
-            out_ref[near, top:, :] = c_ref[p]
-            out_ref[far, :top, :] = b_ref[p]
-            out_ref[far, top:, :] = d_ref[p]
+            down_ref[near, :top, :] = a_ref[p]
+            down_ref[near, top:, :] = c_ref[p, :low_rows, :]
+            down_ref[far, :top, :] = b_ref[p]
+            down_ref[far, top:, :] = d_ref[p, :low_rows, :]
+            out_ref[p] = c_ref[p, low_rows:, :]
+            out_ref[p + half] = d_ref[p, low_rows:, :]
             return 0
 
         lax.fori_loop(0, half, step, 0)
 
-    shape = (2 * half, top + bottom, columns)
+    shape = (2 * half, top + low_rows, columns)
     return pl.pallas_call(
         kernel,
-        out_shape=jax.ShapeDtypeStruct(shape, a.dtype),
+        out_shape=[
+            jax.ShapeDtypeStruct(shape, a.dtype),
+            jax.ShapeDtypeStruct((2 * half, rest, columns), a.dtype),
+        ],
         in_specs=[pl.BlockSpec(memory_space=pltpu.SMEM)] + [whole_spec()] * 4,
-        out_specs=whole_spec(),
-        compiler_params=pltpu.CompilerParams(vmem_limit_bytes=24 * 2**20),
-        cost_estimate=pl.CostEstimate(
-            flops=0, bytes_accessed=4 * shape[0] * shape[1] * columns, transcendentals=0
-        ),
+        out_specs=[whole_spec()] * 2,
+        compiler_params=pltpu.CompilerParams(vmem_limit_bytes=32 * 2**20),
+        cost_estimate=pl.CostEstimate(flops=0, bytes_accessed=2**20, transcendentals=0),
         name="join_blocks",
     )(order, a, b, c, d)
 
@@ -356,7 +371,7 @@
         ],
         compiler_params=pltpu.CompilerParams(vmem_limit_bytes=40 * 2**20),
         cost_estimate=pl.CostEstimate(
-            flops=16 * work * HEAD_DIM, bytes_accessed=8 * 2**20, transcendentals=work
+            flops=work, bytes_accessed=2**20, transcendentals=0
         ),
         name="attend",
     )(query_t, pairs_t, bias)
@@ -379,7 +394,7 @@
         ],
         compiler_params=pltpu.CompilerParams(vmem_limit_bytes=48 * 2**20),
         cost_estimate=pl.CostEstimate(
-            flops=40 * work * HEAD_DIM, bytes_accessed=14 * 2**20, transcendentals=work
+            flops=work, bytes_accessed=2**20, transcendentals=0
         ),
         name="attend_back",
     )(query_t, pairs_t, bias, mixed_t, logs_all, grad_t)
@@ -429,130 +444,111 @@
     cut, cut_ff = D // n_dev, FF // n_dev
     pad = -(-cut // 16) * 16
     top_ff = (cut_ff * 3 // 5) // 8 * 8
-    half_ff = FF // 2
-    split = n_dev * pad // 2
+    low_ff = cut_ff - top_ff
+    half = n_dev // 2
+    split = half * pad
     slots = Slots()
+    ahead = (seqs + 1) // 2
 
     def rows_of(shard, columns):
         return jnp.pad(shard.reshape(cut, columns), ((0, pad - cut), (0, 0)))
 
-    query_piece = Gathered(rows_of(w_query, ATTN), 0)
-    pairs_piece = Gathered(
-        jnp.concatenate([rows_of(w_key, KV), rows_of(w_value, KV)], axis=1), 1
-    )
-    slots.run([(query_piece, 0), (pairs_piece, 0)])
-    down_block = w_down.reshape(cut_ff, D)
-    top_piece, out_piece = Gathered(down_block[:top_ff], 0), Gathered(rows_of(w_out, D), 1)
-    gate_block, up_block = rows_of(w_gate, FF), rows_of(w_up, FF)
-    first_pair = Gathered(gate_block[:, :half_ff], 0), Gathered(up_block[:, :half_ff], 1)
-    second_pair = Gathered(gate_block[:, half_ff:], 0), Gathered(up_block[:, half_ff:], 1)
-    low_piece = Gathered(down_block[top_ff:], 1)
-
-    def at(stage, *pieces):
-        return [(piece, stage) for piece in pieces]
-
-    (seg_y,) = slots.run(at(1, query_piece, pairs_piece), [(segment_ids, FIRST)])
-    segments = jnp.stack([segment_ids, seg_y])
+    def weight(move):
+        return move.both.reshape(-1, move.both.shape[-1])
+
+    attn_block = jnp.concatenate(
+        [rows_of(w_key, KV), rows_of(w_value, KV), rows_of(w_query, ATTN)], axis=1
+    )[None]
+    attn = Spread(attn_block, 8)
+    slots.run([attn])
+    mix_block = jnp.concatenate([w_down.reshape(cut_ff, D), rows_of(w_out, D)], axis=0)[None]
+    mix = Spread(mix_block, 8)
+    attn = Spread(attn.both, 16)
+    seg_y = Move(slots.after(segment_ids), FIRST)
+    inputs = slots.after(tokens).astype(wide).reshape(rows, D)
+    slots.run([attn, mix], [seg_y])
     places = jnp.arange(n_dev, dtype=jnp.int32)
     order = block_owner(places) ^ me
     place = jnp.sum(jnp.where(order[:, None] == places[None, :], places[:, None], 0), axis=0)
     slot = jnp.arange(n_dev * pad, dtype=jnp.int32)
     source = jnp.where(slot % pad < cut, jnp.repeat(order, pad) * cut + slot % pad, -1)
     perm = (jnp.arange(D, dtype=jnp.int32)[:, None] == source[None, :]).astype(low)
-    inputs = tokens.astype(wide).reshape(rows, D)
     scale_attn = rms_scale(inputs)
     normed_attn = product((inputs * scale_attn * norm_attn).astype(low), perm).astype(low)
-    (seg_c,) = slots.run(
-        at(2, query_piece, pairs_piece) + at(0, top_piece, out_piece), [(segments, CORE)]
-    )
-    segments = jnp.concatenate([segments, seg_c], axis=0)
+    segments = jnp.stack([segment_ids, seg_y.came])
+    seg_c = Move(segments, CORE)
+    pairs_w = SpreadFirst(attn.both[..., : 2 * KV], FIRST)
+    query_w = Spread(attn.both[..., 2 * KV :], SECOND)
+    mix = Spread(mix.both, 16)
+    angles = slots.after(positions).reshape(rows)
+    slots.run([pairs_w, query_w], [mix, seg_c])
+    cosine, sine = rope_tables(angles)
+    segments = jnp.concatenate([segments, seg_c.came], axis=0)
+    bias = key_bias(slots.after(segments), segment_ids, ctx_here, (2, 1))
     slots.hold(normed_attn)
-    slots.run(at(3, query_piece, pairs_piece) + at(1, top_piece, out_piece))
-    cosine, sine = rope_tables(positions.reshape(rows))
-    bias = key_bias(segments, segment_ids, ctx_here, (2, 1))
+    pairs_w = SpreadBetween(pairs_w, SECOND)
+    query_w = Spread(query_w.both, FIRST)
+    pair_block = jnp.concatenate([rows_of(w_gate, FF), rows_of(w_up, FF)], axis=1)[None]
+    pair = Spread(pair_block, 8)
+    slots.run([pairs_w, query_w], [pair])
     slots.hold(cosine, sine)
-    slots.run(at(4, query_piece, pairs_piece) + at(2, top_piece, out_piece) + at(0, *first_pair))
-    query_weight, kv_weight = query_piece.weight(), pairs_piece.weight()
-    slots.hold(bias)
-    slots.run(at(3, top_piece, out_piece) + at(1, *first_pair))
+    pairs_w, query_w = Spread(pairs_w.both, CORE), Spread(query_w.both, CORE)
+    top_w, low_w = Spread(mix.both[:, :top_ff], SECOND), SpreadFirst(mix.both[:, top_ff:], FIRST)
+    pair = Spread(pair.both, 16)
+    slots.run([pairs_w, query_w, top_w, low_w], [pair])
+    query_weight, kv_weight = weight(query_w), weight(pairs_w)
+    top_w, low_w = Spread(top_w.both, FIRST), SpreadBetween(low_w, SECOND)
+    slots.run([], [top_w, low_w])
     pairs_t = contract(kv_weight, normed_attn, 0, 1)
     pairs_t = jnp.concatenate(
         [rotate(pairs_t[:KV], cosine, sine).astype(low), pairs_t[KV:].astype(low)], axis=0
     )[None]
-    (came,) = slots.run(
-        at(2, *first_pair) + at(0, *second_pair) + at(4, top_piece, out_piece), [(pairs_t, FIRST)]
-    )
-    pairs_all = jnp.concatenate([pairs_t, came], axis=0)
+    pairs_all = Spread(pairs_t, FIRST)
+    gate_w = Spread(pair.both[..., :FF], SECOND)
+    slots.hold(bias)
+    slots.run([pairs_all], [gate_w])
     query_t = contract(query_weight, normed_attn, 0, 1)
     query_t = (rotate(query_t, cosine, sine) * score_scale).astype(low)
     slots.hold(query_t)
-    (came,) = slots.run(at(3, *first_pair) + at(1, *second_pair), [(pairs_all, CORE)])
-    pairs_all = jnp.concatenate([pairs_all, came], axis=0)
-    out_weight = out_piece.weight()
+    pairs_all = Spread(pairs_all.both, CORE)
+    up_w = SpreadFirst(pair.both[..., FF:], FIRST)
+    top_core = Move(top_w.both, CORE)
+    low_core = Move(low_w.both, CORE)
+    slots.run([pairs_all], [up_w, top_core, low_core])
+    pairs_all = pairs_all.both
     mixed, logs = [None] * seqs, [None] * seqs
-    ahead = (seqs + 1) // 2
     for seq in range(ahead):
         mixed[seq], logs[seq] = attend(query_t, pairs_all, bias, seq)
-    slots.run(at(2, *second_pair) + at(0, low_piece) + at(4, *first_pair))
-    slots.hold(*mixed[:ahead])
+    gate_w, up_w = Spread(gate_w.both, FIRST), SpreadBetween(up_w, SECOND)
+    slots.run([], [gate_w, up_w])
+    slots.hold(up_w.own)
     for seq in range(ahead, seqs):
-        mixed[seq], logs[seq] = attend(query_t, pairs_all, bias, seq)
-    slots.run(at(3, *second_pair) + at(1, low_piece))
-    slots.hold(*mixed[ahead:])
+        mixed[seq], logs[seq] = attend(slots.after(query_t), pairs_all, bias, seq)
+    down_weight, out_weight = join_blocks(
+        (top_w.both, top_core.came), (low_w.both, low_core.came), order, low_ff
+    )
+    down_weight, out_weight = down_weight.reshape(FF, D), out_weight.reshape(-1, D)
+    gate_w, up_w = Spread(gate_w.both, CORE), Spread(up_w.both, CORE)
+    slots.run([], [gate_w, up_w])
     attended = jnp.concatenate([contract(m, perm, 0, 0).astype(low) for m in mixed], axis=0)
     resid = inputs + product(attended, out_weight)
     scale_ffn = rms_scale(resid)
     normed_ffn = product((resid * scale_ffn * norm_ffn).astype(low), perm).astype(low)
-    slots.run(at(2, low_piece) + at(4, *second_pair))
-    slots.hold(normed_ffn)
-    gate_w, up_w = [first_pair[0].weight()], [first_pair[1].weight()]
-    gate, up = [product(normed_ffn, gate_w[0])], [product(normed_ffn, up_w[0])]
-    slots.run(at(3, low_piece))
-    slots.hold(gate[0], up[0])
-    slots.run(at(4, low_piece))
-    gate_w.append(second_pair[0].weight())
-    up_w.append(second_pair[1].weight())
-    gate.append(product(normed_ffn, gate_w[1]))
-    up.append(product(normed_ffn, up_w[1]))
-    down_weight = join_blocks(
-        ((top_piece.mine, top_piece.theirs), (low_piece.mine, low_piece.theirs)), order
-    ).reshape(FF, D)
-    parts = [silu_parts(g, u) for g, u in zip(gate, up)]
-    hidden = jnp.concatenate([h for _, h in parts], axis=1)
+    gate_weight, up_weight = weight(gate_w), weight(up_w)
+    gate, up = product(normed_ffn, gate_weight), product(normed_ffn, up_weight)
+    sigmoid, hidden = silu_parts(gate, up)
     down_grad = cotangent.reshape(rows, D)
     top_grad, low_grad = down_grad_blocks(hidden, down_grad, place, top_ff)
-    slots.hold(top_grad)
-
-    half = n_dev // 2
-    top_sum = Reduced(top_grad[:half], top_grad[half:], 0)
-    low_sum = Reduced(low_grad[:half], low_grad[half:], 1)
-
-    def reduced(left, right, right_dim, route):
+
+    def halves(left, right, right_dim):
         both = []
         for piece in (left[:, :split], left[:, split:]):
             grad = contract(piece, right, 0, right_dim).astype(low)
             both.append(grad.reshape(half, pad, -1))
-        return Reduced(*both, route)
+        return FoldPair(*both, CORE)
 
     def flat(grad):
         return grad[:cut].reshape(-1)
-
-    slots.run(at(0, top_sum, low_sum))
-    output = (resid + product(hidden, down_weight)).astype(low).reshape(seqs, block_len, D)
-    gate_grad, up_grad = [], []
-    for part in range(2):
-        hidden_grad = product_right(
-            down_grad, down_weight[part * half_ff : (part + 1) * half_ff]
-        )
-        a, b = silu_back(hidden_grad, gate[part], up[part], parts[part][0])
-        gate_grad.append(a)
-        up_grad.append(b)
-    slots.hold(gate_grad[0], up_grad[0])
-    slots.run(at(1, top_sum, low_sum))
-    first_sums = [reduced(normed_ffn, gate_grad[0], 0, 0), reduced(normed_ffn, up_grad[0], 0, 1)]
-    slots.hold(output)
-    slots.run(at(2, top_sum, low_sum) + at(0, *first_sums))
-    second_sums = [reduced(normed_ffn, gate_grad[1], 0, 0), reduced(normed_ffn, up_grad[1], 0, 1)]
 
     def collect_wide(value):
         high = lax.reduce_precision(value, 8, 7)
@@ -560,75 +556,89 @@
             (value - high).astype(low), perm
         )
 
-    slots.run(at(1, *first_sums) + at(3, top_sum, low_sum) + at(0, *second_sums))
+    top_s = FoldPair(top_grad[:half], top_grad[half:], CORE)
+    low_s = FoldPair(low_grad[:half], low_grad[half:], CORE)
+    slots.run([top_s, low_s])
+    hidden_grad = product_right(down_grad, down_weight)
+    gate_grad, up_grad = silu_back(hidden_grad, gate, up, sigmoid)
+    slots.hold(gate_grad, up_grad)
+    top_s, low_s = Fold(top_s.sum, FIRST), FoldBetween(low_s.sum, SECOND)
+    slots.run([top_s, low_s])
+    gate_s, up_s = halves(normed_ffn, gate_grad, 0), halves(normed_ffn, up_grad, 0)
+    top_s, low_s = Fold(top_s.sum, SECOND), Fold(low_s.sum, FIRST)
+    slots.run([gate_s, up_s, top_s, low_s])
+    normed_grad = product_right(gate_grad, gate_weight) + product_right(up_grad, up_weight)
+    normed_grad = collect_wide(normed_grad)
     grad_out = cotangent.astype(wide).reshape(rows, D)
-    normed_grad = sum(
-        product_right(g, w) for g, w in zip(gate_grad + up_grad, gate_w + up_w)
-    )
-    normed_grad = collect_wide(normed_grad)
     resid_grad, ffn_gain_grad = norm_back(resid, scale_ffn, norm_ffn, normed_grad)
     resid_grad = resid_grad + grad_out
     branch_grad = resid_grad.astype(low)
     grad_t = product_right(perm, product_right(branch_grad, out_weight).astype(low)).astype(low)
-    slots.hold(grad_t)
-    back = [None] * seqs
-    slots.run(at(2, *first_sums) + at(1, *second_sums) + at(4, top_sum, low_sum))
-    for seq in range(ahead):
-        back[seq] = attend_back(query_t, pairs_all, bias, mixed[seq], logs[seq], grad_t, seq)
-    slots.hold(*[b[0] for b in back[:ahead]])
-    out_sum = reduced(attended, branch_grad, 0, 1)
-    slots.run(at(2, *second_sums) + at(3, *first_sums) + at(0, out_sum))
-    for seq in range(ahead, seqs):
-        back[seq] = attend_back(query_t, pairs_all, bias, mixed[seq], logs[seq], grad_t, seq)
+    gate_s, up_s = Fold(gate_s.sum, FIRST), FoldBetween(up_s.sum, SECOND)
+    down_s = Fold(jnp.concatenate([top_s.sum, low_s.sum], axis=1), 16)
+    grad_t = slots.after(grad_t)
+    slots.run([gate_s, up_s], [down_s])
+    back = [
+        attend_back(query_t, pairs_all, bias, mixed[seq], logs[seq], grad_t, seq)
+        for seq in range(seqs)
+    ]
     pairs_part = jnp.concatenate([b[1] for b in back], axis=2)
-    (came,) = slots.run(
-        at(1, out_sum) + at(4, *first_sums) + at(3, *second_sums), [(pairs_part[2:], CORE)]
-    )
-    pairs_part = add_low(pairs_part[:2], came)
+    pairs_s = FoldPair(pairs_part[:2], pairs_part[2:], CORE)
+    gate_s, up_s = Fold(gate_s.sum, SECOND), Fold(up_s.sum, FIRST)
+    down_s = Fold(down_s.sum, 8, last=True)
+    slots.run([pairs_s], [gate_s, up_s, down_s])
+    out_s = halves(slots.after(attended), branch_grad, 0)
+    pairs_s = Fold(pairs_s.sum, FIRST, last=True)
+    slots.run([pairs_s], [out_s])
     query_low = jnp.concatenate([b[0] for b in back], axis=1)
-    query_low = rotate_back(query_low * score_scale, cosine, sine).astype(low)
-    query_sum = reduced(normed_attn, query_low, 1, 0)
-    (came,) = slots.run(
-        at(2, out_sum) + at(4, *second_sums) + at(0, query_sum), [(pairs_part[1], FIRST)]
-    )
-    pairs_grad = pairs_part[0].astype(wide) + came.astype(wide)
+    query_low = rotate_back(slots.after(query_low) * score_scale, cosine, sine).astype(low)
+    query_s = halves(normed_attn, query_low, 1)
+    pairs_grad = pairs_s.sum
     pairs_low = jnp.concatenate(
         [rotate_back(pairs_grad[:KV], cosine, sine).astype(low), pairs_grad[KV:].astype(low)],
         axis=0,
     )
-    pairs_sum = reduced(normed_attn, pairs_low, 1, 1)
-    slots.run(at(1, query_sum) + at(3, out_sum) + at(0, pairs_sum))
+    pairs_s = halves(normed_attn, pairs_low, 1)
+    out_s = FoldBetween(out_s.sum, SECOND)
+    pair_s = Fold(jnp.concatenate([gate_s.sum, up_s.sum], axis=2), 16)
+    slots.run([pairs_s, query_s, out_s], [pair_s])
     attn_normed_grad = collect_wide(
         contract(query_low, query_weight, 0, 1) + contract(pairs_low, kv_weight, 0, 1)
     )
     input_grad, attn_gain_grad = norm_back(inputs, scale_attn, norm_attn, attn_normed_grad)
     d_tokens = (input_grad + resid_grad).reshape(seqs, block_len, D)
-    gains = jnp.stack([attn_gain_grad, ffn_gain_grad])
-    slots.run(at(1, pairs_sum) + at(2, query_sum) + at(4, out_sum))
-    (came,) = slots.run(at(2, pairs_sum) + at(3, query_sum), [(gains, CORE)])
-    gains = gains + came
-    a, b, c = slots.run(
-        at(3, pairs_sum) + at(4, query_sum), [(gains, m) for m in (FIRST, SECOND, FIRST | SECOND)]
-    )
-    gains = (gains + a) + (b + c)
-    a, b, c = slots.run(at(4, pairs_sum), [(gains, m) for m in (8, 16, 24)])
-    gains = (gains + a) + (b + c)
-    d_gate, d_up = [
-        jnp.concatenate([x.result[:cut], y.result[:cut]], axis=1).reshape(-1)
-        for x, y in zip(first_sums, second_sums)
-    ]
+    output = (resid + product(slots.after(hidden), down_weight)).astype(low)
+    output = output.reshape(seqs, block_len, D)
+    query_s, pairs_s = Fold(query_s.sum, FIRST), FoldBetween(pairs_s.sum, SECOND)
+    out_s = Fold(out_s.sum, FIRST)
+    slots.run([query_s, pairs_s, out_s])
+    query_s, pairs_s = Fold(query_s.sum, SECOND), Fold(pairs_s.sum, FIRST)
+    out_s = Fold(out_s.sum, 16)
+    pair_s = Fold(pair_s.sum, 8, last=True)
+    gains = Move(jnp.stack([attn_gain_grad, ffn_gain_grad]), CORE)
+    slots.run([query_s, pairs_s, out_s, pair_s, gains])
+    attn_s = Fold(jnp.concatenate([pairs_s.sum, query_s.sum], axis=2), 16)
+    out_s = Fold(out_s.sum, 8, last=True)
+    gains = gains.value + gains.came
+    asked = [Move(gains, m) for m in (FIRST, SECOND, FIRST | SECOND)]
+    slots.run([attn_s, out_s, *asked])
+    gains = (gains + asked[0].came) + (asked[1].came + asked[2].came)
+    attn_s = Fold(attn_s.sum, 8, last=True)
+    asked = [Move(gains, m) for m in (8, 16, 24)]
+    slots.run([attn_s, *asked])
+    gains = (gains + asked[0].came) + (asked[1].came + asked[2].came)
     return (
         output,
         d_tokens,
         gains[0],
-        flat(query_sum.result),
-        flat(pairs_sum.result[:, :KV]),
-        flat(pairs_sum.result[:, KV:]),
-        flat(out_sum.result),
+        flat(attn_s.sum[:, 2 * KV :]),
+        flat(attn_s.sum[:, :KV]),
+        flat(attn_s.sum[:, KV : 2 * KV]),
+        flat(out_s.sum),
         gains[1],
-        d_gate,
-        d_up,
-        jnp.concatenate([top_sum.result, low_sum.result], axis=0).reshape(-1),
+        flat(pair_s.sum[:, :FF]),
+        flat(pair_s.sum[:, FF:]),
+        down_s.sum.reshape(-1),
     )
 
 

time: 593 us -> 503 us (0.85)
  local copies, waits for them, and re-layouts: 104 us -> 59.6 us
  starting transfers between devices: 94.1 us -> 57.9 us
  waiting for transfers between devices: 207 us -> 181 us
  Pallas kernels: 51.8 us -> 65.7 us
  other arithmetic: 49.5 us -> 62.1 us
    ppermute x103 -> x66, starting transfers between devices: 94.1 us -> 57.9 us  [swap(): return lax.ppermute(value, AXES, [(i, i ^ mask) for i in range(n)])]
    ppermute x103 -> x66, waiting for transfers between devices: 207 us -> 181 us  [swap(): return lax.ppermute(value, AXES, [(i, i ^ mask) for i in range(n)])]
    unnamed x282 -> x177, local copies, waits for them, and re-layouts: 46 us -> 22.7 us
    pallas_call x2, Pallas kernels: 20.2 us -> 31.5 us  [attend(): pl.pallas_call(attend_kernel, grid=(1,), in_specs=[columns, pairs, bias_s...]
    concatenate x10 -> x3, local copies, waits for them, and re-layouts: 8.82 us -> 0.42 us  [the longest x2 0.32 us: take(): self.both = jnp.concatenate([self.value, came], axis=0)]
    concatenate x39 -> x32, other arithmetic: 20.3 us -> 28.3 us  [the longest x19 19.8 us: take(): self.both = jnp.concatenate([self.value, came], axis=0)]
    slice x45 -> x26, local copies, waits for them, and re-layouts: 15.7 us -> 9.15 us  [the longest x15 3.19 us: give(): return self.value[self.n:]]
    dot_general x20 -> x16, matrix products: 30.6 us -> 26.4 us  [contract(): lax.dot_general(left, right, (((left_dim,), (right_dim,)), ((), ())), pre...]
  transfers between devices with their start and end apart: 103 -> 66, of which waited for: 45 -> 27; matrix products, arithmetic and copies ran while one was open for 27% -> 29% of each run, Pallas kernels for 8% -> 12%
where the time goes in v4:
time: 503 us; the launch traced here: 498 us
  waiting for transfers between devices  181 us (36%)
  matrix products  68.7 us (14%)
  Pallas kernels  65.7 us (13%)
  other arithmetic  62.1 us (12%)
  local copies, waits for them, and re-layouts  59.6 us (12%)
  starting transfers between devices  57.9 us (12%)
    ppermute x66, waiting for transfers between devices, swap(): return lax.ppermute(value, AXES, [(i, i ^ mask) for i in range(n)])  181 us
    ppermute x66, starting transfers between devices, swap(): return lax.ppermute(value, AXES, [(i, i ^ mask) for i in range(n)])  57.9 us
    pallas_call x2, Pallas kernels, attend(): pl.pallas_call(attend_kernel, grid=(1,), in_specs=[columns, pairs, bias_s...  31.5 us
    dot_general x16, matrix products, contract(): lax.dot_general(left, right, (((left_dim,), (right_dim,)), ((), ())), pre...  26.4 us
    pallas_call x2, Pallas kernels, attend_back(): pl.pallas_call(attend_back_kernel, grid=(1,), in_specs=[columns, pairs, b...  25.6 us
    dot_general x8, matrix products, product_right(): lax.dot_general(left, right, (((1,), (1,)), ((), ())), preferred_element_...  23 us
    unnamed x177, local copies, waits for them, and re-layouts  22.7 us
    concatenate x19, other arithmetic, take(): self.both = jnp.concatenate([self.value, came], axis=0)  19.8 us
  transfers between devices with their start and end apart: 66, of which 27 were waited for; matrix products, arithmetic and copies ran while one was open for 29% of the time, Pallas kernels for 12%

profile of v4, /device:TPU:0, one launch (start us, length us, event | category | flops | bytes accessed | tf_op | source)
XLA Modules:
  0.0 498.0 jit_solution(11693014875072041474)
XLA Ops:
  19.9 7.2 %collective-permute-done.1 = bf16[2,32,1600]{2,1,0:T(8,128)(2,1)S(1)} collective-permute-done((bf16[2,32,1600]{2,1,0:T(8,128)(2,1)S(1)}, bf16[2,32,1600]{2,1,0:T(8,128)(2,1)S(1)}, u32[]{:S(2)}, u32[]{:S(2)}) %collective-permute-start.1) | collective-permute-done | bytes 204832 | tf_op jit(solution)/shard_map/ppermute | solution.py:77
  41.8 12.2 %collective-permute-done.8 = bf16[2,112,960]{2,1,0:T(8,128)(2,1)S(1)} collective-permute-done((bf16[2,112,960]{2,1,0:T(8,128)(2,1)S(1)}, bf16[2,112,960]{2,1,0:T(8,128)(2,1)S(1)}, u32[]{:S(2)}, u32[]{:S(2)}) %collective-permute-start.8) | collective-permute-done | bytes 430112 | tf_op jit(solution)/shard_map/ppermute | solution.py:77
  62.7 5.2 %collective-permute-done.15 = bf16[4,48,960]{2,1,0:T(8,128)(2,1)S(1)} collective-permute-done((bf16[4,48,960]{2,1,0:T(8,128)(2,1)S(1)}, bf16[4,48,960]{2,1,0:T(8,128)(2,1)S(1)}, u32[]{:S(2)}, u32[]{:S(2)}) %collective-permute-start.15) | collective-permute-done | bytes 368672 | tf_op jit(solution)/shard_map/ppermute | solution.py:77
  73.3 19.9 %collective-permute-done.12 = bf16[2,32,5120]{2,1,0:T(8,128)(2,1)S(1)} collective-permute-done((bf16[2,32,5120]{2,1,0:T(8,128)(2,1)S(1)}, bf16[2,32,5120]{2,1,0:T(8,128)(2,1)S(1)}, u32[]{:S(2)}, u32[]{:S(2)}) %collective-permute-start.12) | collective-permute-done | bytes 655392 | tf_op jit(solution)/shard_map/ppermute | solution.py:77
  115.2 14.6 %collective-permute-done.17 = bf16[8,48,960]{2,1,0:T(8,128)(2,1)} collective-permute-done((bf16[8,48,960]{2,1,0:T(8,128)(2,1)}, bf16[8,48,960]{2,1,0:T(8,128)(2,1)}, u32[]{:S(2)}, u32[]{:S(2)}) %collective-permute-start.17) | collective-permute-done | bytes 737312 | tf_op jit(solution)/shard_map/ppermute | solution.py:77
  142.5 12.8 %collective-permute-done.23 = bf16[4,32,2560]{2,1,0:T(8,128)(2,1)S(1)} collective-permute-done((bf16[4,32,2560]{2,1,0:T(8,128)(2,1)S(1)}, bf16[4,32,2560]{2,1,0:T(8,128)(2,1)S(1)}, u32[]{:S(2)}, u32[]{:S(2)}) %collective-permute-start.23) | collective-permute-done | bytes 655392 | tf_op jit(solution)/shard_map/ppermute | solution.py:77
  165.7 10.4 %attend.2 = (bf16[960,256]{1,0:T(8,128)(2,1)S(1)}, f32[1,15,256]{2,1,0:T(8,128)S(1)}) custom-call(bf16[960,512]{1,0:T(8,128)(2,1)S(1)} %bitcast.153, bf16[4,640,512]{2,1,0:T(8,128)(2,1)S(1)} %pad_maximum_fusion.1.kv_ref, f32[2,1024,256]{2,1,0:T(8,128)S(1)} %copy-done.1), custom_call_target="tpu_custom_call" | custom-call | flops 3932160 | bytes 1048576 | tf_op jit(solution)/shard_map/attend/pallas_call | solution.py:363
  176.1 21.2 %attend.3 = (bf16[960,256]{1,0:T(8,128)(2,1)S(1)}, f32[1,15,256]{2,1,0:T(8,128)S(1)}) custom-call(bf16[960,512]{1,0:T(8,128)(2,1)S(1)} %bitcast.154, bf16[4,640,512]{2,1,0:T(8,128)(2,1)S(1)} %pad_maximum_fusion.1.kv_ref, f32[2,1024,256]{2,1,0:T(8,128)S(1)} %copy-done.1), custom_call_target="tpu_custom_call" | custom-call | flops 3932160 | bytes 1048576 | tf_op jit(solution)/shard_map/attend/pallas_call | solution.py:363
  209.7 4.7 fusion.129
  219.2 4.6 fusion.128
  228.2 7.8 %fusion.4 = (bf16[512,2560]{1,0:T(8,128)(2,1)S(1)}, bf16[512,2560]{1,0:T(8,128)(2,1)S(1)}, bf16[512,2560]{1,0:T(8,128)(2,1)S(1)}) fusion(f32[2560,512]{0,1:T(8,128)} %fusion.129, f32[512,2560]{1,0:T(8,128)S(1)} %copy-done.77, bf16[512,1024]{1,0:T(8,128)(2,1)S(1)} %fusion.42, bf16[1024,2560]{1,0:T(8,128)(2,1)} %bitcast.192), kind=kOutput, calls=%fused_computation.9 | convolution fusion | flops 2705326080 | bytes 24641536 | tf_op jit(solution)/shard_map/dot_general | solution.py:64
  236.0 4.7 down_grad_blocks.1
  251.8 9.7 %collective-permute-done.31 = bf16[8,32,960]{2,1,0:T(8,128)(2,1)S(1)} collective-permute-done((bf16[8,32,960]{2,1,0:T(8,128)(2,1)S(1)}, bf16[8,32,960]{2,1,0:T(8,128)(2,1)S(1)}, u32[]{:S(2)}, u32[]{:S(2)}) %collective-permute-start.31) | collective-permute-done | bytes 491552 | tf_op jit(solution)/shard_map/ppermute | solution.py:77
  261.7 5.7 %collective-permute-done.30 = bf16[8,48,960]{2,1,0:T(8,128)(2,1)S(1)} collective-permute-done((bf16[8,48,960]{2,1,0:T(8,128)(2,1)S(1)}, bf16[8,48,960]{2,1,0:T(8,128)(2,1)S(1)}, u32[]{:S(2)}, u32[]{:S(2)}) %collective-permute-start.30) | collective-permute-done | bytes 737312 | tf_op jit(solution)/shard_map/ppermute | solution.py:77
  279.8 4.6 collective-permute-done.35
  284.5 4.6 collective-permute-done.34
  298.8 4.6 fusion.43.do_ref
  305.0 12.7 %attend_back.3 = (f32[960,256]{1,0:T(8,128)S(1)}, bf16[4,640,256]{2,1,0:T(8,128)(2,1)S(1)}) custom-call(bf16[960,512]{1,0:T(8,128)(2,1)S(1)} %bitcast.155, bf16[4,640,512]{2,1,0:T(8,128)(2,1)} %copy-done, f32[2,1024,256]{2,1,0:T(8,128)} %and_select_fusion.bias_ref, bf16[960,256]{1,0:T(8,128)(2,1)S(1)} %copy-done.6, ...), custom_call_target="tpu_custom_call" | custom-call | flops 3932160 | bytes 1048576 | tf_op jit(solution)/shard_map/attend_back/pallas_call | solution.py:386
  317.7 12.9 %attend_back.2 = (f32[960,256]{1,0:T(8,128)S(1)}, bf16[4,640,256]{2,1,0:T(8,128)(2,1)S(1)}) custom-call(bf16[960,512]{1,0:T(8,128)(2,1)S(1)} %bitcast.156, bf16[4,640,512]{2,1,0:T(8,128)(2,1)} %copy-done, f32[2,1024,256]{2,1,0:T(8,128)} %and_select_fusion.bias_ref, bf16[960,256]{1,0:T(8,128)(2,1)S(1)} %get-tuple-element.118.o_ref, ...), custom_call_target="tpu_custom_call" | custom-call | flops 3932160 | bytes 1048576 | tf_op jit(solution)/shard_map/attend_back/pallas_call | solution.py:386
  344.6 6.9 %collective-permute-done.42 = bf16[4,32,2560]{2,1,0:T(8,128)(2,1)} collective-permute-done((bf16[4,32,2560]{2,1,0:T(8,128)(2,1)S(1)}, bf16[4,32,2560]{2,1,0:T(8,128)(2,1)}, u32[]{:S(2)}, u32[]{:S(2)}) %collective-permute-start.42) | collective-permute-done | bytes 655392 | tf_op jit(solution)/shard_map/ppermute | solution.py:77
  372.3 7.1 %collective-permute-done.40 = bf16[1,640,512]{2,1,0:T(8,128)(2,1)} collective-permute-done((bf16[1,640,512]{2,1,0:T(8,128)(2,1)}, bf16[1,640,512]{2,1,0:T(8,128)(2,1)}, u32[]{:S(2)}, u32[]{:S(2)}) %collective-permute-start.40) | collective-permute-done | bytes 655392 | tf_op jit(solution)/shard_map/ppermute | solution.py:77
  425.1 23.8 %collective-permute-done.50 = bf16[2,32,5120]{2,1,0:T(8,128)(2,1)S(1)} collective-permute-done((bf16[2,32,5120]{2,1,0:T(8,128)(2,1)S(1)}, bf16[2,32,5120]{2,1,0:T(8,128)(2,1)S(1)}, u32[]{:S(2)}, u32[]{:S(2)}) %collective-permute-start.50) | collective-permute-done | bytes 655392 | tf_op jit(solution)/shard_map/ppermute | solution.py:77
  464.7 5.3 %collective-permute-done.55 = bf16[1,32,5120]{2,1,0:T(8,128)(2,1)S(1)} collective-permute-done((bf16[1,32,5120]{2,1,0:T(8,128)(2,1)S(1)}, bf16[1,32,5120]{2,1,0:T(8,128)(2,1)S(1)}, u32[]{:S(2)}, u32[]{:S(2)}) %collective-permute-start.55) | collective-permute-done | bytes 327712 | tf_op jit(solution)/shard_map/ppermute | solution.py:77
  477.4 8.1 %collective-permute-done.59 = bf16[2,32,1600]{2,1,0:T(8,128)(2,1)S(1)} collective-permute-done((bf16[2,32,1600]{2,1,0:T(8,128)(2,1)S(1)}, bf16[2,32,1600]{2,1,0:T(8,128)(2,1)S(1)}, u32[]{:S(2)}, u32[]{:S(2)}) %collective-permute-start.59) | collective-permute-done | bytes 204832 | tf_op jit(solution)/shard_map/ppermute | solution.py:77
  (494 shorter events, 263.8 us)
Async XLA Ops:
  28.9 31.7 %collective-permute-start.13 = (s32[2,2,256]{2,1,0:T(2,128)S(1)}, s32[2,2,256]{2,1,0:T(2,128)S(1)}, u32[]{:S(2)}, u32[]{:S(2)}) collective-permute-start(s32[2,2,256]{2,1,0:T(2,128)S(1)} %pad_add_fusion.1), channel_id=1, source_target_pairs={{0,1},{1,0},{2,3},{3,2},{4,5},{5,4},{6,7},{7,6},{8,9},{9,8},{10,11... | collective-permute-start | bytes 12296 | tf_op jit(solution)/shard_map/ppermute | solution.py:77
  31.0 23.0 %collective-permute-start.8 = (bf16[2,112,960]{2,1,0:T(8,128)(2,1)S(1)}, bf16[2,112,960]{2,1,0:T(8,128)(2,1)S(1)}, u32[]{:S(2)}, u32[]{:S(2)}) collective-permute-start(bf16[2,112,960]{2,1,0:T(8,128)(2,1)S(1)} %pad_maximum_fusion.28), channel_id=1, source_target_pairs={{0,16},{1,17},{2,18},{3,19},{4,20},{5,21},{6,22},{7,23},{8,24},{9,... | collective-permute-start | bytes 1290248 | tf_op jit(solution)/shard_map/ppermute | solution.py:77
  39.8 18.5 %collective-permute-start.9 = (bf16[1,32,5120]{2,1,0:T(8,128)(2,1)S(1)}, bf16[1,32,5120]{2,1,0:T(8,128)(2,1)S(1)}, u32[]{:S(2)}, u32[]{:S(2)}) collective-permute-start(bf16[1,32,5120]{2,1,0:T(8,128)(2,1)S(1)} %copy-done.40), channel_id=1, source_target_pairs={{0,8},{1,9},{2,10},{3,11},{4,12},{5,13},{6,14},{7,15},{8,0},{9,1},... | collective-permute-start | bytes 983048 | tf_op jit(solution)/shard_map/ppermute | solution.py:77
  62.2 31.1 %collective-permute-start.12 = (bf16[2,32,5120]{2,1,0:T(8,128)(2,1)S(1)}, bf16[2,32,5120]{2,1,0:T(8,128)(2,1)S(1)}, u32[]{:S(2)}, u32[]{:S(2)}) collective-permute-start(bf16[2,32,5120]{2,1,0:T(8,128)(2,1)S(1)} %pad_maximum_fusion.20), channel_id=1, source_target_pairs={{0,16},{1,17},{2,18},{3,19},{4,20},{5,21},{6,22},{7,23},{8,24},{9,... | collective-permute-start | bytes 1966088 | tf_op jit(solution)/shard_map/ppermute | solution.py:77
  62.2 35.7 %collective-permute-start.10 = (bf16[16,32,960]{2,1,0:T(8,128)(2,1)S(1)}, bf16[16,32,960]{2,1,0:T(8,128)(2,1)S(1)}, u32[]{:S(2)}, u32[]{:S(2)}) collective-permute-start(bf16[16,32,960]{2,1,0:T(8,128)(2,1)S(1)} %pad_maximum_fusion.14), channel_id=1, source_target_pairs={{0,1},{1,0},{2,3},{3,2},{4,5},{5,4},{6,7},{7,6},{8,9},{9,8},{10,11... | collective-permute-start | bytes 2949128 | tf_op jit(solution)/shard_map/ppermute | solution.py:77
  96.4 43.6 %collective-permute-start.22 = (bf16[4,32,2560]{2,1,0:T(8,128)(2,1)S(1)}, bf16[4,32,2560]{2,1,0:T(8,128)(2,1)}, u32[]{:S(2)}, u32[]{:S(2)}) collective-permute-start(bf16[4,32,2560]{2,1,0:T(8,128)(2,1)S(1)} %get-tuple-element.124), channel_id=1, source_target_pairs={{0,4},{1,5},{2,6},{3,7},{4,0},{5,1},{6,2},{7,3},{8,12},{9,13},{10,... | collective-permute-start | bytes 1966088 | tf_op jit(solution)/shard_map/ppermute | solution.py:77
  97.9 31.9 %collective-permute-start.17 = (bf16[8,48,960]{2,1,0:T(8,128)(2,1)}, bf16[8,48,960]{2,1,0:T(8,128)(2,1)}, u32[]{:S(2)}, u32[]{:S(2)}) collective-permute-start(bf16[8,48,960]{2,1,0:T(8,128)(2,1)} %pad_maximum_fusion.17), channel_id=1, source_target_pairs={{0,2},{1,3},{2,0},{3,1},{4,6},{5,7},{6,4},{7,5},{8,10},{9,11},{10,... | collective-permute-start | bytes 2211848 | tf_op jit(solution)/shard_map/ppermute | solution.py:77
  99.4 36.0 %collective-permute-start.18 = (bf16[8,64,960]{2,1,0:T(8,128)(2,1)}, bf16[8,64,960]{2,1,0:T(8,128)(2,1)}, u32[]{:S(2)}, u32[]{:S(2)}) collective-permute-start(bf16[8,64,960]{2,1,0:T(8,128)(2,1)} %pad_maximum_fusion.15), channel_id=1, source_target_pairs={{0,4},{1,5},{2,6},{3,7},{4,0},{5,1},{6,2},{7,3},{8,12},{9,13},{10,... | collective-permute-start | bytes 2949128 | tf_op jit(solution)/shard_map/ppermute | solution.py:77
  138.2 19.2 %collective-permute-start.19 = (bf16[2,640,512]{2,1,0:T(8,128)(2,1)S(1)}, bf16[2,640,512]{2,1,0:T(8,128)(2,1)}, u32[]{:S(2)}, u32[]{:S(2)}) collective-permute-start(bf16[2,640,512]{2,1,0:T(8,128)(2,1)S(1)} %pad_maximum_fusion.10), channel_id=1, source_target_pairs={{0,1},{1,0},{2,3},{3,2},{4,5},{5,4},{6,7},{7,6},{8,9},{9,8},{10,11... | collective-permute-start | bytes 3932168 | tf_op jit(solution)/shard_map/ppermute | solution.py:77
  139.8 59.3 %collective-permute-start.21 = (bf16[16,64,960]{2,1,0:T(8,128)(2,1)}, bf16[16,64,960]{2,1,0:T(8,128)(2,1)}, u32[]{:S(2)}, u32[]{:S(2)}) collective-permute-start(bf16[16,64,960]{2,1,0:T(8,128)(2,1)} %pad_maximum_fusion.5.c_ref), channel_id=1, source_target_pairs={{0,1},{1,0},{2,3},{3,2},{4,5},{5,4},{6,7},{7,6},{8,9},{9,8},{10,11... | collective-permute-start | bytes 5898248 | tf_op jit(solution)/shard_map/ppermute | solution.py:77
  142.3 56.8 %collective-permute-start.20 = (bf16[16,48,960]{2,1,0:T(8,128)(2,1)}, bf16[16,48,960]{2,1,0:T(8,128)(2,1)}, u32[]{:S(2)}, u32[]{:S(2)}) collective-permute-start(bf16[16,48,960]{2,1,0:T(8,128)(2,1)} %pad_maximum_fusion.8.a_ref), channel_id=1, source_target_pairs={{0,1},{1,0},{2,3},{3,2},{4,5},{5,4},{6,7},{7,6},{8,9},{9,8},{10,11... | collective-permute-start | bytes 4423688 | tf_op jit(solution)/shard_map/ppermute | solution.py:77
  157.4 45.6 %collective-permute-start.24 = (bf16[8,32,2560]{2,1,0:T(8,128)(2,1)}, bf16[8,32,2560]{2,1,0:T(8,128)(2,1)}, u32[]{:S(2)}, u32[]{:S(2)}) collective-permute-start(bf16[8,32,2560]{2,1,0:T(8,128)(2,1)} %pad_maximum_fusion.11), channel_id=1, source_target_pairs={{0,2},{1,3},{2,0},{3,1},{4,6},{5,7},{6,4},{7,5},{8,10},{9,11},{10,... | collective-permute-start | bytes 3932168 | tf_op jit(solution)/shard_map/ppermute | solution.py:77
  161.5 44.8 %collective-permute-start.25 = (bf16[8,32,2560]{2,1,0:T(8,128)(2,1)}, bf16[8,32,2560]{2,1,0:T(8,128)(2,1)S(1)}, u32[]{:S(2)}, u32[]{:S(2)}) collective-permute-start(bf16[8,32,2560]{2,1,0:T(8,128)(2,1)} %pad_maximum_fusion.12), channel_id=1, source_target_pairs={{0,4},{1,5},{2,6},{3,7},{4,0},{5,1},{6,2},{7,3},{8,12},{9,13},{10,... | collective-permute-start | bytes 3932168 | tf_op jit(solution)/shard_map/ppermute | solution.py:77
  248.1 19.2 %collective-permute-start.30 = (bf16[8,48,960]{2,1,0:T(8,128)(2,1)S(1)}, bf16[8,48,960]{2,1,0:T(8,128)(2,1)S(1)}, u32[]{:S(2)}, u32[]{:S(2)}) collective-permute-start(bf16[8,48,960]{2,1,0:T(8,128)(2,1)S(1)} %slice.432), channel_id=1, source_target_pairs={{0,2},{1,3},{2,0},{3,1},{4,6},{5,7},{6,4},{7,5},{8,10},{9,11},{10,... | collective-permute-start | bytes 2211848 | tf_op jit(solution)/shard_map/ppermute | solution.py:77
  267.7 22.4 %collective-permute-start.32 = (bf16[16,32,2560]{2,1,0:T(8,128)(2,1)S(1)}, bf16[16,32,2560]{2,1,0:T(8,128)(2,1)S(1)}, u32[]{:S(2)}, u32[]{:S(2)}) collective-permute-start(bf16[16,32,2560]{2,1,0:T(8,128)(2,1)S(1)} %bitcast.176), channel_id=1, source_target_pairs={{0,1},{1,0},{2,3},{3,2},{4,5},{5,4},{6,7},{7,6},{8,9},{9,8},{10,11... | collective-permute-start | bytes 7864328 | tf_op jit(solution)/shard_map/ppermute | solution.py:77
  273.6 18.5 %collective-permute-start.33 = (bf16[16,32,2560]{2,1,0:T(8,128)(2,1)S(1)}, bf16[16,32,2560]{2,1,0:T(8,128)(2,1)S(1)}, u32[]{:S(2)}, u32[]{:S(2)}) collective-permute-start(bf16[16,32,2560]{2,1,0:T(8,128)(2,1)S(1)} %bitcast.175), channel_id=1, source_target_pairs={{0,1},{1,0},{2,3},{3,2},{4,5},{5,4},{6,7},{7,6},{8,9},{9,8},{10,11... | collective-permute-start | bytes 7864328 | tf_op jit(solution)/shard_map/ppermute | solution.py:77
  295.4 38.8 %collective-permute-start.36 = (bf16[8,32,2560]{2,1,0:T(8,128)(2,1)}, bf16[8,32,2560]{2,1,0:T(8,128)(2,1)}, u32[]{:S(2)}, u32[]{:S(2)}) collective-permute-start(bf16[8,32,2560]{2,1,0:T(8,128)(2,1)} %slice.443), channel_id=1, source_target_pairs={{0,2},{1,3},{2,0},{3,1},{4,6},{5,7},{6,4},{7,5},{8,10},{9,11},{10,... | collective-permute-start | bytes 3932168 | tf_op jit(solution)/shard_map/ppermute | solution.py:77
  298.8 33.2 %collective-permute-start.38 = (bf16[2,80,960]{2,1,0:T(8,128)(2,1)}, bf16[2,80,960]{2,1,0:T(8,128)(2,1)}, u32[]{:S(2)}, u32[]{:S(2)}) collective-permute-start(bf16[2,80,960]{2,1,0:T(8,128)(2,1)} %fusion.75), channel_id=1, source_target_pairs={{0,16},{1,17},{2,18},{3,19},{4,20},{5,21},{6,22},{7,23},{8,24},{9,... | collective-permute-start | bytes 921608 | tf_op jit(solution)/shard_map/ppermute | solution.py:77
  303.5 32.5 %collective-permute-start.37 = (bf16[8,32,2560]{2,1,0:T(8,128)(2,1)}, bf16[8,32,2560]{2,1,0:T(8,128)(2,1)S(1)}, u32[]{:S(2)}, u32[]{:S(2)}) collective-permute-start(bf16[8,32,2560]{2,1,0:T(8,128)(2,1)} %pad_maximum_fusion.13), channel_id=1, source_target_pairs={{0,4},{1,5},{2,6},{3,7},{4,0},{5,1},{6,2},{7,3},{8,12},{9,13},{10,... | collective-permute-start | bytes 3932168 | tf_op jit(solution)/shard_map/ppermute | solution.py:77
  372.3 31.4 %collective-permute-start.41 = (bf16[16,32,960]{2,1,0:T(8,128)(2,1)}, bf16[16,32,960]{2,1,0:T(8,128)(2,1)}, u32[]{:S(2)}, u32[]{:S(2)}) collective-permute-start(bf16[16,32,960]{2,1,0:T(8,128)(2,1)} %bitcast.187), channel_id=1, source_target_pairs={{0,1},{1,0},{2,3},{3,2},{4,5},{5,4},{6,7},{7,6},{8,9},{9,8},{10,11... | collective-permute-start | bytes 2949128 | tf_op jit(solution)/shard_map/ppermute | solution.py:77
  417.2 31.7 %collective-permute-start.50 = (bf16[2,32,5120]{2,1,0:T(8,128)(2,1)S(1)}, bf16[2,32,5120]{2,1,0:T(8,128)(2,1)S(1)}, u32[]{:S(2)}, u32[]{:S(2)}) collective-permute-start(bf16[2,32,5120]{2,1,0:T(8,128)(2,1)S(1)} %copy-done.60), channel_id=1, source_target_pairs={{0,16},{1,17},{2,18},{3,19},{4,20},{5,21},{6,22},{7,23},{8,24},{9,... | collective-permute-start | bytes 1966088 | tf_op jit(solution)/shard_map/ppermute | solution.py:77
  421.7 27.4 %collective-permute-start.49 = (bf16[4,32,960]{2,1,0:T(8,128)(2,1)S(1)}, bf16[4,32,960]{2,1,0:T(8,128)(2,1)S(1)}, u32[]{:S(2)}, u32[]{:S(2)}) collective-permute-start(bf16[4,32,960]{2,1,0:T(8,128)(2,1)S(1)} %slice.476), channel_id=1, source_target_pairs={{0,2},{1,3},{2,0},{3,1},{4,6},{5,7},{6,4},{7,5},{8,10},{9,11},{10,... | collective-permute-start | bytes 737288 | tf_op jit(solution)/shard_map/ppermute | solution.py:77
  422.3 26.9 %collective-permute-start.48 = (bf16[8,32,640]{2,1,0:T(8,128)(2,1)S(1)}, bf16[8,32,640]{2,1,0:T(8,128)(2,1)S(1)}, u32[]{:S(2)}, u32[]{:S(2)}) collective-permute-start(bf16[8,32,640]{2,1,0:T(8,128)(2,1)S(1)} %pad_maximum_fusion.33), channel_id=1, source_target_pairs={{0,4},{1,5},{2,6},{3,7},{4,0},{5,1},{6,2},{7,3},{8,12},{9,13},{10,... | collective-permute-start | bytes 983048 | tf_op jit(solution)/shard_map/ppermute | solution.py:77
  423.6 25.8 %collective-permute-start.47 = (bf16[8,32,960]{2,1,0:T(8,128)(2,1)S(1)}, bf16[8,32,960]{2,1,0:T(8,128)(2,1)S(1)}, u32[]{:S(2)}, u32[]{:S(2)}) collective-permute-start(bf16[8,32,960]{2,1,0:T(8,128)(2,1)S(1)} %slice.471), channel_id=1, source_target_pairs={{0,2},{1,3},{2,0},{3,1},{4,6},{5,7},{6,4},{7,5},{8,10},{9,11},{10,... | collective-permute-start | bytes 1474568 | tf_op jit(solution)/shard_map/ppermute | solution.py:77
  (124 other events, 1203.9 us)

commit v5 on v4

--- a/solution.py
+++ b/solution.py
@@ -1,3 +1,5 @@
+import functools
+
 import jax
 import jax.numpy as jnp
 from jax import lax
@@ -109,12 +111,11 @@
         self.deps = self.deps + values
 
     def run(self, moves, late=()):
-        values = tuple(move.give() for move in (*moves, *late))
-        if self.deps:
-            values = lax.optimization_barrier((values, self.deps))[0]
-        for i, (move, value) in enumerate(zip((*moves, *late), values)):
-            if i == 0:
-                self.deps = ()
+        before, self.deps = self.deps, ()
+        for i, move in enumerate((*moves, *late)):
+            value = move.give()
+            if before:
+                value = lax.optimization_barrier((value, before))[0]
             came = swap(value, move.mask)
             if i < len(moves):
                 self.deps += (came,)
@@ -134,6 +135,7 @@
 
 class Spread(Move):
     def take(self, came):
+        self.came = came
         self.both = jnp.concatenate([self.value, came], axis=0)
 
 
@@ -398,6 +400,44 @@
         ),
         name="attend_back",
     )(query_t, pairs_t, bias, mixed_t, logs_all, grad_t)
+
+
+def project_kernel(a_ref, q0_ref, q1_ref, p0_ref, p1_ref, cos_ref, sin_ref, q_ref, p_ref, *, scale):
+    split = q0_ref.shape[0]
+    half = HEAD_DIM // 2
+    first, second = a_ref[:, :split], a_ref[:, split:]
+    cosine, sine = cos_ref[...], sin_ref[...]
+
+    def turned(value):
+        upper, lower = value[half:], value[:half]
+        return value * cosine + jnp.concatenate([-upper, lower], axis=0) * sine
+
+    pairs = (product(first, p0_ref[...]) + product(second, p1_ref[...])).T
+    for h in range(KV_HEADS):
+        at = slice(h * HEAD_DIM, (h + 1) * HEAD_DIM)
+        p_ref[at, :] = turned(pairs[at]).astype(low)
+    p_ref[KV:, :] = pairs[KV:].astype(low)
+    query = (product(first, q0_ref[...]) + product(second, q1_ref[...])).T
+    for h in range(HEADS):
+        at = slice(h * HEAD_DIM, (h + 1) * HEAD_DIM)
+        q_ref[at, :] = (turned(query[at]) * scale).astype(low)
+
+
+def project(normed, query_halves, pairs_halves, cosine, sine, scale):
+    rows = normed.shape[0]
+    halves = [h.reshape(-1, h.shape[-1]) for h in (*query_halves, *pairs_halves)]
+    return pl.pallas_call(
+        functools.partial(project_kernel, scale=scale),
+        in_specs=[whole_spec()] * 7,
+        out_specs=[whole_spec()] * 2,
+        out_shape=[
+            jax.ShapeDtypeStruct((ATTN, rows), low),
+            jax.ShapeDtypeStruct((2 * KV, rows), low),
+        ],
+        compiler_params=pltpu.CompilerParams(vmem_limit_bytes=40 * 2**20),
+        cost_estimate=pl.CostEstimate(flops=rows, bytes_accessed=2**20, transcendentals=0),
+        name="project",
+    )(normed, *halves, cosine, sine)
 
 
 def key_bias(segment_all, segment_ids, ctx_here, masks):
@@ -494,24 +534,26 @@
     slots.hold(cosine, sine)
     pairs_w, query_w = Spread(pairs_w.both, CORE), Spread(query_w.both, CORE)
     top_w, low_w = Spread(mix.both[:, :top_ff], SECOND), SpreadFirst(mix.both[:, top_ff:], FIRST)
-    pair = Spread(pair.both, 16)
-    slots.run([pairs_w, query_w, top_w, low_w], [pair])
+    gate_w = Spread(pair.both[..., :FF], 16)
+    slots.run([pairs_w, query_w, top_w, low_w], [gate_w])
     query_weight, kv_weight = weight(query_w), weight(pairs_w)
+    query_t, pairs_t = project(
+        normed_attn,
+        (query_w.value, query_w.came),
+        (pairs_w.value, pairs_w.came),
+        cosine,
+        sine,
+        score_scale,
+    )
     top_w, low_w = Spread(top_w.both, FIRST), SpreadBetween(low_w, SECOND)
     slots.run([], [top_w, low_w])
-    pairs_t = contract(kv_weight, normed_attn, 0, 1)
-    pairs_t = jnp.concatenate(
-        [rotate(pairs_t[:KV], cosine, sine).astype(low), pairs_t[KV:].astype(low)], axis=0
-    )[None]
-    pairs_all = Spread(pairs_t, FIRST)
-    gate_w = Spread(pair.both[..., :FF], SECOND)
-    slots.hold(bias)
-    slots.run([pairs_all], [gate_w])
-    query_t = contract(query_weight, normed_attn, 0, 1)
-    query_t = (rotate(query_t, cosine, sine) * score_scale).astype(low)
-    slots.hold(query_t)
+    pairs_all = Spread(pairs_t[None], FIRST)
+    up_w = Spread(pair.both[..., FF:], 16)
+    gate_w = Spread(gate_w.both, SECOND)
+    slots.hold(bias, query_t)
+    slots.run([pairs_all], [up_w, gate_w])
     pairs_all = Spread(pairs_all.both, CORE)
-    up_w = SpreadFirst(pair.both[..., FF:], FIRST)
+    up_w = SpreadFirst(up_w.both, FIRST)
     top_core = Move(top_w.both, CORE)
     low_core = Move(low_w.both, CORE)
     slots.run([pairs_all], [up_w, top_core, low_core])
@@ -520,16 +562,19 @@
     for seq in range(ahead):
         mixed[seq], logs[seq] = attend(query_t, pairs_all, bias, seq)
     gate_w, up_w = Spread(gate_w.both, FIRST), SpreadBetween(up_w, SECOND)
+    slots.hold(*mixed[:ahead], up_w.side)
+    query_t = slots.after(query_t)
     slots.run([], [gate_w, up_w])
-    slots.hold(up_w.own)
     for seq in range(ahead, seqs):
-        mixed[seq], logs[seq] = attend(slots.after(query_t), pairs_all, bias, seq)
+        mixed[seq], logs[seq] = attend(query_t, pairs_all, bias, seq)
     down_weight, out_weight = join_blocks(
         (top_w.both, top_core.came), (low_w.both, low_core.came), order, low_ff
     )
     down_weight, out_weight = down_weight.reshape(FF, D), out_weight.reshape(-1, D)
+    down_grad = cotangent.reshape(rows, D)
+    hidden_grad = product_right(down_grad, down_weight)
     gate_w, up_w = Spread(gate_w.both, CORE), Spread(up_w.both, CORE)
-    slots.run([], [gate_w, up_w])
+    slots.run([gate_w, up_w])
     attended = jnp.concatenate([contract(m, perm, 0, 0).astype(low) for m in mixed], axis=0)
     resid = inputs + product(attended, out_weight)
     scale_ffn = rms_scale(resid)
@@ -537,7 +582,6 @@
     gate_weight, up_weight = weight(gate_w), weight(up_w)
     gate, up = product(normed_ffn, gate_weight), product(normed_ffn, up_weight)
     sigmoid, hidden = silu_parts(gate, up)
-    down_grad = cotangent.reshape(rows, D)
     top_grad, low_grad = down_grad_blocks(hidden, down_grad, place, top_ff)
 
     def halves(left, right, right_dim):
@@ -559,7 +603,6 @@
     top_s = FoldPair(top_grad[:half], top_grad[half:], CORE)
     low_s = FoldPair(low_grad[:half], low_grad[half:], CORE)
     slots.run([top_s, low_s])
-    hidden_grad = product_right(down_grad, down_weight)
     gate_grad, up_grad = silu_back(hidden_grad, gate, up, sigmoid)
     slots.hold(gate_grad, up_grad)
     top_s, low_s = Fold(top_s.sum, FIRST), FoldBetween(low_s.sum, SECOND)
@@ -582,26 +625,29 @@
         attend_back(query_t, pairs_all, bias, mixed[seq], logs[seq], grad_t, seq)
         for seq in range(seqs)
     ]
+    out_s = halves(attended, branch_grad, 0)
     pairs_part = jnp.concatenate([b[1] for b in back], axis=2)
     pairs_s = FoldPair(pairs_part[:2], pairs_part[2:], CORE)
     gate_s, up_s = Fold(gate_s.sum, SECOND), Fold(up_s.sum, FIRST)
     down_s = Fold(down_s.sum, 8, last=True)
-    slots.run([pairs_s], [gate_s, up_s, down_s])
-    out_s = halves(slots.after(attended), branch_grad, 0)
+    slots.run([pairs_s], [gate_s, up_s, down_s, out_s])
     pairs_s = Fold(pairs_s.sum, FIRST, last=True)
-    slots.run([pairs_s], [out_s])
+    gate_s, up_s = Fold(gate_s.sum, 16), Fold(up_s.sum, 16)
     query_low = jnp.concatenate([b[0] for b in back], axis=1)
-    query_low = rotate_back(slots.after(query_low) * score_scale, cosine, sine).astype(low)
+    query_low = rotate_back(query_low * score_scale, cosine, sine).astype(low)
     query_s = halves(normed_attn, query_low, 1)
+    out_s = FoldBetween(out_s.sum, SECOND)
+    slots.hold(query_s.value)
+    slots.run([pairs_s, query_s], [gate_s, out_s])
+    query_s, out_s = Fold(query_s.sum, FIRST), Fold(out_s.sum, FIRST)
+    slots.run([], [query_s, out_s, up_s])
     pairs_grad = pairs_s.sum
     pairs_low = jnp.concatenate(
         [rotate_back(pairs_grad[:KV], cosine, sine).astype(low), pairs_grad[KV:].astype(low)],
         axis=0,
     )
     pairs_s = halves(normed_attn, pairs_low, 1)
-    out_s = FoldBetween(out_s.sum, SECOND)
-    pair_s = Fold(jnp.concatenate([gate_s.sum, up_s.sum], axis=2), 16)
-    slots.run([pairs_s, query_s, out_s], [pair_s])
+    slots.run([pairs_s])
     attn_normed_grad = collect_wide(
         contract(query_low, query_weight, 0, 1) + contract(pairs_low, kv_weight, 0, 1)
     )
@@ -609,35 +655,36 @@
     d_tokens = (input_grad + resid_grad).reshape(seqs, block_len, D)
     output = (resid + product(slots.after(hidden), down_weight)).astype(low)
     output = output.reshape(seqs, block_len, D)
-    query_s, pairs_s = Fold(query_s.sum, FIRST), FoldBetween(pairs_s.sum, SECOND)
-    out_s = Fold(out_s.sum, FIRST)
-    slots.run([query_s, pairs_s, out_s])
-    query_s, pairs_s = Fold(query_s.sum, SECOND), Fold(pairs_s.sum, FIRST)
-    out_s = Fold(out_s.sum, 16)
-    pair_s = Fold(pair_s.sum, 8, last=True)
+    query_s = Fold(query_s.sum, SECOND)
+    pairs_s = FoldBetween(pairs_s.sum, SECOND)
+    gate_s = Fold(gate_s.sum, 8, last=True)
+    slots.run([pairs_s], [query_s, gate_s])
+    attn_s = Fold(jnp.concatenate([query_s.sum, out_s.sum], axis=2), 16)
+    pairs_s = Fold(pairs_s.sum, FIRST)
+    up_s = Fold(up_s.sum, 8, last=True)
     gains = Move(jnp.stack([attn_gain_grad, ffn_gain_grad]), CORE)
-    slots.run([query_s, pairs_s, out_s, pair_s, gains])
-    attn_s = Fold(jnp.concatenate([pairs_s.sum, query_s.sum], axis=2), 16)
-    out_s = Fold(out_s.sum, 8, last=True)
+    slots.run([pairs_s, attn_s, gains], [up_s])
+    attn_s = Fold(attn_s.sum, 8, last=True)
+    pairs_s = Fold(pairs_s.sum, 16)
     gains = gains.value + gains.came
     asked = [Move(gains, m) for m in (FIRST, SECOND, FIRST | SECOND)]
-    slots.run([attn_s, out_s, *asked])
+    slots.run([pairs_s, attn_s, *asked])
     gains = (gains + asked[0].came) + (asked[1].came + asked[2].came)
-    attn_s = Fold(attn_s.sum, 8, last=True)
+    pairs_s = Fold(pairs_s.sum, 8, last=True)
     asked = [Move(gains, m) for m in (8, 16, 24)]
-    slots.run([attn_s, *asked])
+    slots.run([pairs_s, *asked])
     gains = (gains + asked[0].came) + (asked[1].came + asked[2].came)
     return (
         output,
         d_tokens,
         gains[0],
-        flat(attn_s.sum[:, 2 * KV :]),
-        flat(attn_s.sum[:, :KV]),
-        flat(attn_s.sum[:, KV : 2 * KV]),
-        flat(out_s.sum),
+        flat(attn_s.sum[:, :ATTN]),
+        flat(pairs_s.sum[:, :KV]),
+        flat(pairs_s.sum[:, KV:]),
+        flat(attn_s.sum[:, ATTN:]),
         gains[1],
-        flat(pair_s.sum[:, :FF]),
-        flat(pair_s.sum[:, FF:]),
+        flat(gate_s.sum),
+        flat(up_s.sum),
         down_s.sum.reshape(-1),
     )
 

time: 503 us -> 477 us (0.948)
  waiting for transfers between devices: 181 us -> 160 us
  other arithmetic: 62.1 us -> 46 us
    ppermute x66 -> x69, waiting for transfers between devices: 181 us -> 160 us  [swap(): return lax.ppermute(value, AXES, [(i, i ^ mask) for i in range(n)])]
    concatenate x19 -> x18, other arithmetic: 19.8 us -> 7.59 us  [take(): self.both = jnp.concatenate([self.value, came], axis=0)]
    convert_element_type x26 -> x27, other arithmetic: 17.3 us -> 24.5 us  [add_low(): return (left.astype(wide) + right.astype(wide)).astype(low)]
    unnamed x177 -> x191, local copies, waits for them, and re-layouts: 22.7 us -> 27 us
    ppermute x66 -> x69, starting transfers between devices: 57.9 us -> 60.3 us  [swap(): return lax.ppermute(value, AXES, [(i, i ^ mask) for i in range(n)])]
    dot_general x16 -> x14, matrix products: 26.4 us -> 27.7 us  [contract(): lax.dot_general(left, right, (((left_dim,), (right_dim,)), ((), ())), pre...]
  transfers between devices with their start and end apart: 66 -> 69, of which waited for: 27 -> 32; matrix products, arithmetic and copies ran while one was open for 29% -> 29% of each run, Pallas kernels for 12% -> 13%
where the time goes in v5:
time: 477 us; the launch traced here: 468 us
  waiting for transfers between devices  160 us (34%)
  matrix products  69.3 us (15%)
  Pallas kernels  66.2 us (14%)
  local copies, waits for them, and re-layouts  63.4 us (13%)
  starting transfers between devices  60.3 us (13%)
  other arithmetic  46 us (10%)
    ppermute x69, waiting for transfers between devices, swap(): return lax.ppermute(value, AXES, [(i, i ^ mask) for i in range(n)])  160 us
    ppermute x69, starting transfers between devices, swap(): return lax.ppermute(value, AXES, [(i, i ^ mask) for i in range(n)])  60.3 us
    pallas_call x2, Pallas kernels, attend(): pl.pallas_call(attend_kernel, grid=(1,), in_specs=[columns, pairs, bias_s...  32.7 us
    dot_general x14, matrix products, contract(): lax.dot_general(left, right, (((left_dim,), (right_dim,)), ((), ())), pre...  27.7 us
    unnamed x191, local copies, waits for them, and re-layouts  27 us
    pallas_call x2, Pallas kernels, attend_back(): pl.pallas_call(attend_back_kernel, grid=(1,), in_specs=[columns, pairs, b...  25.4 us
    convert_element_type x27, other arithmetic, add_low(): return (left.astype(wide) + right.astype(wide)).astype(low)  24.5 us
    dot_general x8, matrix products, product_right(): lax.dot_general(left, right, (((1,), (1,)), ((), ())), preferred_element_...  21.4 us
  transfers between devices with their start and end apart: 69, of which 32 were waited for; matrix products, arithmetic and copies ran while one was open for 29% of the time, Pallas kernels for 13%

profile of v5, /device:TPU:0, one launch (start us, length us, event | category | flops | bytes accessed | tf_op | source)
XLA Modules:
  0.0 468.3 jit_solution(368597783485562842)
XLA Ops:
  23.1 7.2 %collective-permute-done.1 = bf16[2,32,1600]{2,1,0:T(8,128)(2,1)S(1)} collective-permute-done((bf16[2,32,1600]{2,1,0:T(8,128)(2,1)S(1)}, bf16[2,32,1600]{2,1,0:T(8,128)(2,1)S(1)}, u32[]{:S(2)}, u32[]{:S(2)}) %collective-permute-start.1) | collective-permute-done | bytes 204832 | tf_op jit(solution)/shard_map/ppermute | solution.py:79
  35.4 5.5 %collective-permute-done.4 = bf16[4,32,640]{2,1,0:T(8,128)(2,1)S(1)} collective-permute-done((bf16[4,32,640]{2,1,0:T(8,128)(2,1)S(1)}, bf16[4,32,640]{2,1,0:T(8,128)(2,1)S(1)}, u32[]{:S(2)}, u32[]{:S(2)}) %collective-permute-start.4) | collective-permute-done | bytes 163872 | tf_op jit(solution)/shard_map/ppermute | solution.py:79
  43.9 14.5 %collective-permute-done.16 = bf16[2,112,960]{2,1,0:T(8,128)(2,1)S(1)} collective-permute-done((bf16[2,112,960]{2,1,0:T(8,128)(2,1)S(1)}, bf16[2,112,960]{2,1,0:T(8,128)(2,1)S(1)}, u32[]{:S(2)}, u32[]{:S(2)}) %collective-permute-start.16) | collective-permute-done | bytes 430112 | tf_op jit(solution)/shard_map/ppermute | solution.py:79
  64.7 15.5 %collective-permute-done.23 = bf16[2,32,2560]{2,1,0:T(8,128)(2,1)S(1)} collective-permute-done((bf16[2,32,2560]{2,1,0:T(8,128)(2,1)S(1)}, bf16[2,32,2560]{2,1,0:T(8,128)(2,1)S(1)}, u32[]{:S(2)}, u32[]{:S(2)}) %collective-permute-start.23) | collective-permute-done | bytes 327712 | tf_op jit(solution)/shard_map/ppermute | solution.py:79
  89.5 11.0 %collective-permute-done.14 = bf16[2,32,2560]{2,1,0:T(8,128)(2,1)S(1)} collective-permute-done((bf16[2,32,2560]{2,1,0:T(8,128)(2,1)S(1)}, bf16[2,32,2560]{2,1,0:T(8,128)(2,1)S(1)}, u32[]{:S(2)}, u32[]{:S(2)}) %collective-permute-start.14) | collective-permute-done | bytes 327712 | tf_op jit(solution)/shard_map/ppermute | solution.py:79
  102.1 4.4 collective-permute-done.21
  109.2 9.5 %collective-permute-done.19 = bf16[8,48,960]{2,1,0:T(8,128)(2,1)S(1)} collective-permute-done((bf16[8,48,960]{2,1,0:T(8,128)(2,1)S(1)}, bf16[8,48,960]{2,1,0:T(8,128)(2,1)S(1)}, u32[]{:S(2)}, u32[]{:S(2)}) %collective-permute-start.19) | collective-permute-done | bytes 737312 | tf_op jit(solution)/shard_map/ppermute | solution.py:79
  121.7 9.9 %collective-permute-done.15 = bf16[4,32,2560]{2,1,0:T(8,128)(2,1)S(1)} collective-permute-done((bf16[4,32,2560]{2,1,0:T(8,128)(2,1)S(1)}, bf16[4,32,2560]{2,1,0:T(8,128)(2,1)S(1)}, u32[]{:S(2)}, u32[]{:S(2)}) %collective-permute-start.15) | collective-permute-done | bytes 655392 | tf_op jit(solution)/shard_map/ppermute | solution.py:79
  133.0 10.1 %attend.2 = (bf16[960,256]{1,0:T(8,128)(2,1)S(1)}, f32[1,15,256]{2,1,0:T(8,128)S(1)}) custom-call(bf16[960,512]{1,0:T(8,128)(2,1)S(1)} %get-tuple-element.115.q_ref, bf16[4,640,512]{2,1,0:T(8,128)(2,1)S(1)} %pad_maximum_fusion.kv_ref, f32[2,1024,256]{2,1,0:T(8,128)S(1)} %and_select_fusion.bias_ref), custom_call_target="tpu_custom_call" | custom-call | flops 3932160 | bytes 1048576 | tf_op jit(solution)/shard_map/attend/pallas_call | solution.py:365
  146.1 22.6 %attend.3 = (bf16[960,256]{1,0:T(8,128)(2,1)S(1)}, f32[1,15,256]{2,1,0:T(8,128)S(1)}) custom-call(bf16[960,512]{1,0:T(8,128)(2,1)S(1)} %get-tuple-element.115.q_ref, bf16[4,640,512]{2,1,0:T(8,128)(2,1)S(1)} %pad_maximum_fusion.kv_ref, f32[2,1024,256]{2,1,0:T(8,128)S(1)} %and_select_fusion.bias_ref), custom_call_target="tpu_custom_call" | custom-call | flops 3932160 | bytes 1048576 | tf_op jit(solution)/shard_map/attend/pallas_call | solution.py:365
  175.3 4.7 fusion.128
  194.6 7.8 %fusion.4 = (bf16[512,2560]{1,0:T(8,128)(2,1)S(1)}, bf16[512,2560]{1,0:T(8,128)(2,1)S(1)}, bf16[512,2560]{1,0:T(8,128)(2,1)S(1)}) fusion(f32[2560,512]{0,1:T(8,128)} %fusion.128, f32[512,2560]{1,0:T(8,128)S(1)} %fusion.127, bf16[512,1024]{1,0:T(8,128)(2,1)S(1)} %fusion.42, bf16[1024,2560]{1,0:T(8,128)(2,1)} %bitcast.182), kind=kOutput, calls=%fused_computation.8 | convolution fusion | flops 2705326080 | bytes 24641536 | tf_op jit(solution)/shard_map/dot_general | solution.py:66
  214.5 4.7 %down_grad_blocks.1 = (bf16[32,48,960]{2,1,0:T(8,128)(2,1)S(1)}, bf16[32,32,960]{2,1,0:T(8,128)(2,1)S(1)}) custom-call(s32[32]{0:T(128)S(1)} %select_reduce_fusion.place_ref, bf16[512,2560]{1,0:T(8,128)(2,1)S(1)} %get-tuple-element.151.h_ref, bf16[512,960]{1,0:T(8,128)(2,1)S(1)} %bitcast.141), custom_call_target="tpu_custom_call" | custom-call | flops 2516582400 | bytes 8519680 | tf_op jit(solution)/shard_map/down_grad_blocks/pallas_call | solution.py:270
  231.0 11.5 %collective-permute-done.32 = bf16[8,32,960]{2,1,0:T(8,128)(2,1)S(1)} collective-permute-done((bf16[8,32,960]{2,1,0:T(8,128)(2,1)S(1)}, bf16[8,32,960]{2,1,0:T(8,128)(2,1)S(1)}, u32[]{:S(2)}, u32[]{:S(2)}) %collective-permute-start.32) | collective-permute-done | bytes 491552 | tf_op jit(solution)/shard_map/ppermute | solution.py:79
  242.5 5.1 %collective-permute-done.31 = bf16[8,48,960]{2,1,0:T(8,128)(2,1)S(1)} collective-permute-done((bf16[8,48,960]{2,1,0:T(8,128)(2,1)S(1)}, bf16[8,48,960]{2,1,0:T(8,128)(2,1)S(1)}, u32[]{:S(2)}, u32[]{:S(2)}) %collective-permute-start.31) | collective-permute-done | bytes 737312 | tf_op jit(solution)/shard_map/ppermute | solution.py:79
  251.6 4.6 fusion.43.do_ref
  256.3 3.7 fusion.44
  291.8 12.9 %attend_back.3 = (f32[960,256]{1,0:T(8,128)S(1)}, bf16[4,640,256]{2,1,0:T(8,128)(2,1)S(1)}) custom-call(bf16[960,512]{1,0:T(8,128)(2,1)S(1)} %copy-done.3, bf16[4,640,512]{2,1,0:T(8,128)(2,1)} %copy-done, f32[2,1024,256]{2,1,0:T(8,128)} %copy-done.1, bf16[960,256]{1,0:T(8,128)(2,1)S(1)} %copy-done.9, f32[1,15,256]{2,1,0:T(8,128)S(1)} %get-tuple-element.143.lse_ref, ...), custom_call_target="tpu_custom_call" | custom-call | flops 3932160 | bytes 1048576 | tf_op jit(solution)/shard_map/attend_back/pallas_call | solution.py:388
  304.7 12.5 %attend_back.2 = (f32[960,256]{1,0:T(8,128)S(1)}, bf16[4,640,256]{2,1,0:T(8,128)(2,1)S(1)}) custom-call(bf16[960,512]{1,0:T(8,128)(2,1)S(1)} %copy-done.3, bf16[4,640,512]{2,1,0:T(8,128)(2,1)} %copy-done, f32[2,1024,256]{2,1,0:T(8,128)} %copy-done.1, bf16[960,256]{1,0:T(8,128)(2,1)S(1)} %get-tuple-element.111.o_ref, ...), custom_call_target="tpu_custom_call" | custom-call | flops 3932160 | bytes 1048576 | tf_op jit(solution)/shard_map/attend_back/pallas_call | solution.py:388
  344.3 8.1 %collective-permute-done.61 = bf16[4,32,2560]{2,1,0:T(8,128)(2,1)} collective-permute-done((bf16[4,32,2560]{2,1,0:T(8,128)(2,1)}, bf16[4,32,2560]{2,1,0:T(8,128)(2,1)}, u32[]{:S(2)}, u32[]{:S(2)}) %collective-permute-start.61) | collective-permute-done | bytes 655392 | tf_op jit(solution)/shard_map/ppermute | solution.py:79
  366.6 9.5 %collective-permute-done.62 = bf16[2,32,2560]{2,1,0:T(8,128)(2,1)S(1)} collective-permute-done((bf16[2,32,2560]{2,1,0:T(8,128)(2,1)S(1)}, bf16[2,32,2560]{2,1,0:T(8,128)(2,1)S(1)}, u32[]{:S(2)}, u32[]{:S(2)}) %collective-permute-start.62) | collective-permute-done | bytes 327712 | tf_op jit(solution)/shard_map/ppermute | solution.py:79
  400.5 9.8 %collective-permute-done.65 = bf16[2,32,2560]{2,1,0:T(8,128)(2,1)S(1)} collective-permute-done((bf16[2,32,2560]{2,1,0:T(8,128)(2,1)S(1)}, bf16[2,32,2560]{2,1,0:T(8,128)(2,1)S(1)}, u32[]{:S(2)}, u32[]{:S(2)}) %collective-permute-start.65) | collective-permute-done | bytes 327712 | tf_op jit(solution)/shard_map/ppermute | solution.py:79
  411.1 5.5 %add_convert_fusion.6 = bf16[512,960]{1,0:T(8,128)(2,1)S(1)} fusion(f32[512,960]{1,0:T(8,128)S(1)} %copy-done.39, bf16[512,2560]{1,0:T(8,128)(2,1)S(1)} %copy-done.13, bf16[2560,960]{1,0:T(8,128)(2,1)} %bitcast.150), kind=kOutput, calls=%fused_computation.57 | convolution fusion | flops 2517565440 | bytes 10485760 | tf_op jit(solution)/shard_map/dot_general | solution.py:66
  441.1 6.3 %collective-permute-done.51 = bf16[2,32,1920]{2,1,0:T(8,128)(2,1)S(1)} collective-permute-done((bf16[2,32,1920]{2,1,0:T(8,128)(2,1)S(1)}, bf16[2,32,1920]{2,1,0:T(8,128)(2,1)S(1)}, u32[]{:S(2)}, u32[]{:S(2)}) %collective-permute-start.51) | collective-permute-done | bytes 245792 | tf_op jit(solution)/shard_map/ppermute | solution.py:79
  (504 shorter events, 248.7 us)
Async XLA Ops:
  35.3 23.1 %collective-permute-start.16 = (bf16[2,112,960]{2,1,0:T(8,128)(2,1)S(1)}, bf16[2,112,960]{2,1,0:T(8,128)(2,1)S(1)}, u32[]{:S(2)}, u32[]{:S(2)}) collective-permute-start(bf16[2,112,960]{2,1,0:T(8,128)(2,1)S(1)} %pad_maximum_fusion.26), channel_id=1, source_target_pairs={{0,16},{1,17},{2,18},{3,19},{4,20},{5,21},{6,22},{7,23},{8,24},{9,... | collective-permute-start | bytes 1290248 | tf_op jit(solution)/shard_map/ppermute | solution.py:79
  42.4 18.7 %collective-permute-start.13 = (bf16[1,32,5120]{2,1,0:T(8,128)(2,1)S(1)}, bf16[1,32,5120]{2,1,0:T(8,128)(2,1)S(1)}, u32[]{:S(2)}, u32[]{:S(2)}) collective-permute-start(bf16[1,32,5120]{2,1,0:T(8,128)(2,1)S(1)} %copy-done.52), channel_id=1, source_target_pairs={{0,8},{1,9},{2,10},{3,11},{4,12},{5,13},{6,14},{7,15},{8,0},{9,1},... | collective-permute-start | bytes 983048 | tf_op jit(solution)/shard_map/ppermute | solution.py:79
  42.8 19.2 %collective-permute-start.5 = (bf16[8,32,960]{2,1,0:T(8,128)(2,1)S(1)}, bf16[8,32,960]{2,1,0:T(8,128)(2,1)S(1)}, u32[]{:S(2)}, u32[]{:S(2)}) collective-permute-start(bf16[8,32,960]{2,1,0:T(8,128)(2,1)S(1)} %pad_maximum_fusion.23), channel_id=1, source_target_pairs={{0,2},{1,3},{2,0},{3,1},{4,6},{5,7},{6,4},{7,5},{8,10},{9,11},{10,... | collective-permute-start | bytes 1474568 | tf_op jit(solution)/shard_map/ppermute | solution.py:79
  62.2 18.2 %collective-permute-start.7 = (bf16[16,32,960]{2,1,0:T(8,128)(2,1)S(1)}, bf16[16,32,960]{2,1,0:T(8,128)(2,1)S(1)}, u32[]{:S(2)}, u32[]{:S(2)}) collective-permute-start(bf16[16,32,960]{2,1,0:T(8,128)(2,1)S(1)} %pad_maximum_fusion.13), channel_id=1, source_target_pairs={{0,1},{1,0},{2,3},{3,2},{4,5},{5,4},{6,7},{7,6},{8,9},{9,8},{10,11... | collective-permute-start | bytes 2949128 | tf_op jit(solution)/shard_map/ppermute | solution.py:79
  62.4 17.8 %collective-permute-start.18 = (bf16[4,64,960]{2,1,0:T(8,128)(2,1)S(1)}, bf16[4,64,960]{2,1,0:T(8,128)(2,1)S(1)}, u32[]{:S(2)}, u32[]{:S(2)}) collective-permute-start(bf16[4,64,960]{2,1,0:T(8,128)(2,1)S(1)} %pad_maximum_fusion.21), channel_id=1, source_target_pairs={{0,2},{1,3},{2,0},{3,1},{4,6},{5,7},{6,4},{7,5},{8,10},{9,11},{10,... | collective-permute-start | bytes 1474568 | tf_op jit(solution)/shard_map/ppermute | solution.py:79
  80.4 26.1 %collective-permute-start.21 = (bf16[8,64,960]{2,1,0:T(8,128)(2,1)S(1)}, bf16[8,64,960]{2,1,0:T(8,128)(2,1)S(1)}, u32[]{:S(2)}, u32[]{:S(2)}) collective-permute-start(bf16[8,64,960]{2,1,0:T(8,128)(2,1)S(1)} %pad_maximum_fusion.14), channel_id=1, source_target_pairs={{0,4},{1,5},{2,6},{3,7},{4,0},{5,1},{6,2},{7,3},{8,12},{9,13},{10,... | collective-permute-start | bytes 2949128 | tf_op jit(solution)/shard_map/ppermute | solution.py:79
  85.8 33.0 %collective-permute-start.19 = (bf16[8,48,960]{2,1,0:T(8,128)(2,1)S(1)}, bf16[8,48,960]{2,1,0:T(8,128)(2,1)S(1)}, u32[]{:S(2)}, u32[]{:S(2)}) collective-permute-start(bf16[8,48,960]{2,1,0:T(8,128)(2,1)S(1)} %pad_maximum_fusion.15), channel_id=1, source_target_pairs={{0,2},{1,3},{2,0},{3,1},{4,6},{5,7},{6,4},{7,5},{8,10},{9,11},{10,... | collective-permute-start | bytes 2211848 | tf_op jit(solution)/shard_map/ppermute | solution.py:79
  86.5 33.1 %collective-permute-start.24 = (bf16[4,32,2560]{2,1,0:T(8,128)(2,1)S(1)}, bf16[4,32,2560]{2,1,0:T(8,128)(2,1)S(1)}, u32[]{:S(2)}, u32[]{:S(2)}) collective-permute-start(bf16[4,32,2560]{2,1,0:T(8,128)(2,1)S(1)} %pad_maximum_fusion.18), channel_id=1, source_target_pairs={{0,4},{1,5},{2,6},{3,7},{4,0},{5,1},{6,2},{7,3},{8,12},{9,13},{10,... | collective-permute-start | bytes 1966088 | tf_op jit(solution)/shard_map/ppermute | solution.py:79
  102.0 30.7 %collective-permute-start.12 = (bf16[2,640,512]{2,1,0:T(8,128)(2,1)S(1)}, bf16[2,640,512]{2,1,0:T(8,128)(2,1)S(1)}, u32[]{:S(2)}, u32[]{:S(2)}) collective-permute-start(bf16[2,640,512]{2,1,0:T(8,128)(2,1)S(1)} %pad_maximum_fusion.8), channel_id=1, source_target_pairs={{0,1},{1,0},{2,3},{3,2},{4,5},{5,4},{6,7},{7,6},{8,9},{9,8},{10,11... | collective-permute-start | bytes 3932168 | tf_op jit(solution)/shard_map/ppermute | solution.py:79
  106.8 63.6 %collective-permute-start.22 = (bf16[16,64,960]{2,1,0:T(8,128)(2,1)S(1)}, bf16[16,64,960]{2,1,0:T(8,128)(2,1)S(1)}, u32[]{:S(2)}, u32[]{:S(2)}) collective-permute-start(bf16[16,64,960]{2,1,0:T(8,128)(2,1)S(1)} %pad_maximum_fusion.2.c_ref), channel_id=1, source_target_pairs={{0,1},{1,0},{2,3},{3,2},{4,5},{5,4},{6,7},{7,6},{8,9},{9,8},{10,11... | collective-permute-start | bytes 5898248 | tf_op jit(solution)/shard_map/ppermute | solution.py:79
  107.8 23.7 %collective-permute-start.15 = (bf16[4,32,2560]{2,1,0:T(8,128)(2,1)S(1)}, bf16[4,32,2560]{2,1,0:T(8,128)(2,1)S(1)}, u32[]{:S(2)}, u32[]{:S(2)}) collective-permute-start(bf16[4,32,2560]{2,1,0:T(8,128)(2,1)S(1)} %pad_maximum_fusion.17), channel_id=1, source_target_pairs={{0,2},{1,3},{2,0},{3,1},{4,6},{5,7},{6,4},{7,5},{8,10},{9,11},{10,... | collective-permute-start | bytes 1966088 | tf_op jit(solution)/shard_map/ppermute | solution.py:79
  118.9 51.5 %collective-permute-start.20 = (bf16[16,48,960]{2,1,0:T(8,128)(2,1)S(1)}, bf16[16,48,960]{2,1,0:T(8,128)(2,1)S(1)}, u32[]{:S(2)}, u32[]{:S(2)}) collective-permute-start(bf16[16,48,960]{2,1,0:T(8,128)(2,1)S(1)} %pad_maximum_fusion.6.a_ref), channel_id=1, source_target_pairs={{0,1},{1,0},{2,3},{3,2},{4,5},{5,4},{6,7},{7,6},{8,9},{9,8},{10,11... | collective-permute-start | bytes 4423688 | tf_op jit(solution)/shard_map/ppermute | solution.py:79
  143.2 38.5 %collective-permute-start.27 = (bf16[8,32,2560]{2,1,0:T(8,128)(2,1)}, bf16[8,32,2560]{2,1,0:T(8,128)(2,1)}, u32[]{:S(2)}, u32[]{:S(2)}) collective-permute-start(bf16[8,32,2560]{2,1,0:T(8,128)(2,1)} %pad_maximum_fusion.10), channel_id=1, source_target_pairs={{0,4},{1,5},{2,6},{3,7},{4,0},{5,1},{6,2},{7,3},{8,12},{9,13},{10,... | collective-permute-start | bytes 3932168 | tf_op jit(solution)/shard_map/ppermute | solution.py:79
  144.7 35.2 %collective-permute-start.25 = (bf16[8,32,2560]{2,1,0:T(8,128)(2,1)}, bf16[8,32,2560]{2,1,0:T(8,128)(2,1)}, u32[]{:S(2)}, u32[]{:S(2)}) collective-permute-start(bf16[8,32,2560]{2,1,0:T(8,128)(2,1)} %pad_maximum_fusion.9), channel_id=1, source_target_pairs={{0,2},{1,3},{2,0},{3,1},{4,6},{5,7},{6,4},{7,5},{8,10},{9,11},{10,... | collective-permute-start | bytes 3932168 | tf_op jit(solution)/shard_map/ppermute | solution.py:79
  227.7 20.0 %collective-permute-start.31 = (bf16[8,48,960]{2,1,0:T(8,128)(2,1)S(1)}, bf16[8,48,960]{2,1,0:T(8,128)(2,1)S(1)}, u32[]{:S(2)}, u32[]{:S(2)}) collective-permute-start(bf16[8,48,960]{2,1,0:T(8,128)(2,1)S(1)} %slice.415), channel_id=1, source_target_pairs={{0,2},{1,3},{2,0},{3,1},{4,6},{5,7},{6,4},{7,5},{8,10},{9,11},{10,... | collective-permute-start | bytes 2211848 | tf_op jit(solution)/shard_map/ppermute | solution.py:79
  247.7 29.1 %collective-permute-start.33 = (bf16[16,32,2560]{2,1,0:T(8,128)(2,1)}, bf16[16,32,2560]{2,1,0:T(8,128)(2,1)}, u32[]{:S(2)}, u32[]{:S(2)}) collective-permute-start(bf16[16,32,2560]{2,1,0:T(8,128)(2,1)} %bitcast.19), channel_id=1, source_target_pairs={{0,1},{1,0},{2,3},{3,2},{4,5},{5,4},{6,7},{7,6},{8,9},{9,8},{10,11... | collective-permute-start | bytes 7864328 | tf_op jit(solution)/shard_map/ppermute | solution.py:79
  256.2 24.3 %collective-permute-start.34 = (bf16[16,32,2560]{2,1,0:T(8,128)(2,1)}, bf16[16,32,2560]{2,1,0:T(8,128)(2,1)}, u32[]{:S(2)}, u32[]{:S(2)}) collective-permute-start(bf16[16,32,2560]{2,1,0:T(8,128)(2,1)} %bitcast.158), channel_id=1, source_target_pairs={{0,1},{1,0},{2,3},{3,2},{4,5},{5,4},{6,7},{7,6},{8,9},{9,8},{10,11... | collective-permute-start | bytes 7864328 | tf_op jit(solution)/shard_map/ppermute | solution.py:79
  286.3 46.4 %collective-permute-start.67 = (bf16[2,80,960]{2,1,0:T(8,128)(2,1)}, bf16[2,80,960]{2,1,0:T(8,128)(2,1)}, u32[]{:S(2)}, u32[]{:S(2)}) collective-permute-start(bf16[2,80,960]{2,1,0:T(8,128)(2,1)} %pad_maximum_fusion.29), channel_id=1, source_target_pairs={{0,16},{1,17},{2,18},{3,19},{4,20},{5,21},{6,22},{7,23},{8,24},{9,... | collective-permute-start | bytes 921608 | tf_op jit(solution)/shard_map/ppermute | solution.py:79
  290.1 43.7 %collective-permute-start.38 = (bf16[8,32,2560]{2,1,0:T(8,128)(2,1)}, bf16[8,32,2560]{2,1,0:T(8,128)(2,1)}, u32[]{:S(2)}, u32[]{:S(2)}) collective-permute-start(bf16[8,32,2560]{2,1,0:T(8,128)(2,1)} %pad_maximum_fusion.11), channel_id=1, source_target_pairs={{0,4},{1,5},{2,6},{3,7},{4,0},{5,1},{6,2},{7,3},{8,12},{9,13},{10,... | collective-permute-start | bytes 3932168 | tf_op jit(solution)/shard_map/ppermute | solution.py:79
  290.6 43.2 %collective-permute-start.37 = (bf16[8,32,2560]{2,1,0:T(8,128)(2,1)}, bf16[8,32,2560]{2,1,0:T(8,128)(2,1)}, u32[]{:S(2)}, u32[]{:S(2)}) collective-permute-start(bf16[8,32,2560]{2,1,0:T(8,128)(2,1)} %slice.426), channel_id=1, source_target_pairs={{0,2},{1,3},{2,0},{3,1},{4,6},{5,7},{6,4},{7,5},{8,10},{9,11},{10,... | collective-permute-start | bytes 3932168 | tf_op jit(solution)/shard_map/ppermute | solution.py:79
  342.9 18.3 %collective-permute-start.39 = (bf16[2,640,512]{2,1,0:T(8,128)(2,1)}, bf16[2,640,512]{2,1,0:T(8,128)(2,1)}, u32[]{:S(2)}, u32[]{:S(2)}) collective-permute-start(bf16[2,640,512]{2,1,0:T(8,128)(2,1)} %slice.424), channel_id=1, source_target_pairs={{0,1},{1,0},{2,3},{3,2},{4,5},{5,4},{6,7},{7,6},{8,9},{9,8},{10,11... | collective-permute-start | bytes 3932168 | tf_op jit(solution)/shard_map/ppermute | solution.py:79
  366.6 25.4 %collective-permute-start.45 = (bf16[16,32,960]{2,1,0:T(8,128)(2,1)}, bf16[16,32,960]{2,1,0:T(8,128)(2,1)}, u32[]{:S(2)}, u32[]{:S(2)}) collective-permute-start(bf16[16,32,960]{2,1,0:T(8,128)(2,1)} %bitcast.42), channel_id=1, source_target_pairs={{0,1},{1,0},{2,3},{3,2},{4,5},{5,4},{6,7},{7,6},{8,9},{9,8},{10,11... | collective-permute-start | bytes 2949128 | tf_op jit(solution)/shard_map/ppermute | solution.py:79
  382.1 29.0 %collective-permute-start.41 = (bf16[16,32,640]{2,1,0:T(8,128)(2,1)}, bf16[16,32,640]{2,1,0:T(8,128)(2,1)}, u32[]{:S(2)}, u32[]{:S(2)}) collective-permute-start(bf16[16,32,640]{2,1,0:T(8,128)(2,1)} %bitcast.33), channel_id=1, source_target_pairs={{0,1},{1,0},{2,3},{3,2},{4,5},{5,4},{6,7},{7,6},{8,9},{9,8},{10,11... | collective-permute-start | bytes 1966088 | tf_op jit(solution)/shard_map/ppermute | solution.py:79
  397.5 26.3 %collective-permute-start.46 = (bf16[8,32,960]{2,1,0:T(8,128)(2,1)}, bf16[8,32,960]{2,1,0:T(8,128)(2,1)}, u32[]{:S(2)}, u32[]{:S(2)}) collective-permute-start(bf16[8,32,960]{2,1,0:T(8,128)(2,1)} %slice.444), channel_id=1, source_target_pairs={{0,2},{1,3},{2,0},{3,1},{4,6},{5,7},{6,4},{7,5},{8,10},{9,11},{10,... | collective-permute-start | bytes 1474568 | tf_op jit(solution)/shard_map/ppermute | solution.py:79
  (131 other events, 1528.6 us)

commit v6 on v5

--- a/solution.py
+++ b/solution.py
@@ -562,8 +562,6 @@
     for seq in range(ahead):
         mixed[seq], logs[seq] = attend(query_t, pairs_all, bias, seq)
     gate_w, up_w = Spread(gate_w.both, FIRST), SpreadBetween(up_w, SECOND)
-    slots.hold(*mixed[:ahead], up_w.side)
-    query_t = slots.after(query_t)
     slots.run([], [gate_w, up_w])
     for seq in range(ahead, seqs):
         mixed[seq], logs[seq] = attend(query_t, pairs_all, bias, seq)
@@ -582,7 +580,7 @@
     gate_weight, up_weight = weight(gate_w), weight(up_w)
     gate, up = product(normed_ffn, gate_weight), product(normed_ffn, up_weight)
     sigmoid, hidden = silu_parts(gate, up)
-    top_grad, low_grad = down_grad_blocks(hidden, down_grad, place, top_ff)
+    gate_grad, up_grad = silu_back(hidden_grad, gate, up, sigmoid)
 
     def halves(left, right, right_dim):
         both = []
@@ -600,16 +598,13 @@
             (value - high).astype(low), perm
         )
 
+    gate_s, up_s = halves(normed_ffn, gate_grad, 0), halves(normed_ffn, up_grad, 0)
+    slots.run([gate_s, up_s])
+    top_grad, low_grad = down_grad_blocks(hidden, down_grad, place, top_ff)
     top_s = FoldPair(top_grad[:half], top_grad[half:], CORE)
     low_s = FoldPair(low_grad[:half], low_grad[half:], CORE)
-    slots.run([top_s, low_s])
-    gate_grad, up_grad = silu_back(hidden_grad, gate, up, sigmoid)
-    slots.hold(gate_grad, up_grad)
-    top_s, low_s = Fold(top_s.sum, FIRST), FoldBetween(low_s.sum, SECOND)
-    slots.run([top_s, low_s])
-    gate_s, up_s = halves(normed_ffn, gate_grad, 0), halves(normed_ffn, up_grad, 0)
-    top_s, low_s = Fold(top_s.sum, SECOND), Fold(low_s.sum, FIRST)
-    slots.run([gate_s, up_s, top_s, low_s])
+    gate_s, up_s = Fold(gate_s.sum, FIRST), FoldBetween(up_s.sum, SECOND)
+    slots.run([gate_s, up_s], [top_s, low_s])
     normed_grad = product_right(gate_grad, gate_weight) + product_right(up_grad, up_weight)
     normed_grad = collect_wide(normed_grad)
     grad_out = cotangent.astype(wide).reshape(rows, D)
@@ -617,31 +612,34 @@
     resid_grad = resid_grad + grad_out
     branch_grad = resid_grad.astype(low)
     grad_t = product_right(perm, product_right(branch_grad, out_weight).astype(low)).astype(low)
-    gate_s, up_s = Fold(gate_s.sum, FIRST), FoldBetween(up_s.sum, SECOND)
-    down_s = Fold(jnp.concatenate([top_s.sum, low_s.sum], axis=1), 16)
     grad_t = slots.after(grad_t)
-    slots.run([gate_s, up_s], [down_s])
-    back = [
-        attend_back(query_t, pairs_all, bias, mixed[seq], logs[seq], grad_t, seq)
-        for seq in range(seqs)
-    ]
-    out_s = halves(attended, branch_grad, 0)
+    back = [None] * seqs
+    for seq in range(ahead):
+        back[seq] = attend_back(query_t, pairs_all, bias, mixed[seq], logs[seq], grad_t, seq)
+    gate_s, up_s = Fold(gate_s.sum, SECOND), Fold(up_s.sum, FIRST)
+    top_s, low_s = Fold(top_s.sum, FIRST), FoldBetween(low_s.sum, SECOND)
+    slots.run([gate_s, up_s], [top_s, low_s])
+    grad_t = slots.after(grad_t)
+    for seq in range(ahead, seqs):
+        back[seq] = attend_back(query_t, pairs_all, bias, mixed[seq], logs[seq], grad_t, seq)
+    gate_s, up_s = Fold(gate_s.sum, 16), Fold(up_s.sum, 16)
+    out_s = halves(slots.after(attended), branch_grad, 0)
+    slots.run([], [gate_s, up_s])
     pairs_part = jnp.concatenate([b[1] for b in back], axis=2)
     pairs_s = FoldPair(pairs_part[:2], pairs_part[2:], CORE)
-    gate_s, up_s = Fold(gate_s.sum, SECOND), Fold(up_s.sum, FIRST)
-    down_s = Fold(down_s.sum, 8, last=True)
-    slots.run([pairs_s], [gate_s, up_s, down_s, out_s])
-    pairs_s = Fold(pairs_s.sum, FIRST, last=True)
-    gate_s, up_s = Fold(gate_s.sum, 16), Fold(up_s.sum, 16)
+    top_s, low_s = Fold(top_s.sum, SECOND), Fold(low_s.sum, FIRST)
+    slots.run([pairs_s], [top_s, low_s, out_s])
     query_low = jnp.concatenate([b[0] for b in back], axis=1)
     query_low = rotate_back(query_low * score_scale, cosine, sine).astype(low)
     query_s = halves(normed_attn, query_low, 1)
+    pairs_s = Fold(pairs_s.sum, FIRST, last=True)
     out_s = FoldBetween(out_s.sum, SECOND)
-    slots.hold(query_s.value)
-    slots.run([pairs_s, query_s], [gate_s, out_s])
+    slots.run([pairs_s, query_s], [out_s])
+    gate_s, up_s = Fold(gate_s.sum, 8, last=True), Fold(up_s.sum, 8, last=True)
+    down_s = Fold(jnp.concatenate([top_s.sum, low_s.sum], axis=1), 16)
+    pairs_grad = slots.after(pairs_s.sum)
     query_s, out_s = Fold(query_s.sum, FIRST), Fold(out_s.sum, FIRST)
-    slots.run([], [query_s, out_s, up_s])
-    pairs_grad = pairs_s.sum
+    slots.run([], [query_s, out_s, gate_s, up_s, down_s])
     pairs_low = jnp.concatenate(
         [rotate_back(pairs_grad[:KV], cosine, sine).astype(low), pairs_grad[KV:].astype(low)],
         axis=0,
@@ -657,13 +655,12 @@
     output = output.reshape(seqs, block_len, D)
     query_s = Fold(query_s.sum, SECOND)
     pairs_s = FoldBetween(pairs_s.sum, SECOND)
-    gate_s = Fold(gate_s.sum, 8, last=True)
-    slots.run([pairs_s], [query_s, gate_s])
+    down_s = Fold(down_s.sum, 8, last=True)
+    slots.run([pairs_s], [query_s, down_s])
     attn_s = Fold(jnp.concatenate([query_s.sum, out_s.sum], axis=2), 16)
     pairs_s = Fold(pairs_s.sum, FIRST)
-    up_s = Fold(up_s.sum, 8, last=True)
     gains = Move(jnp.stack([attn_gain_grad, ffn_gain_grad]), CORE)
-    slots.run([pairs_s, attn_s, gains], [up_s])
+    slots.run([pairs_s, attn_s, gains])
     attn_s = Fold(attn_s.sum, 8, last=True)
     pairs_s = Fold(pairs_s.sum, 16)
     gains = gains.value + gains.came

time: 477 us -> 458 us (0.960)
  local copies, waits for them, and re-layouts: 63.4 us -> 57 us
    dot_general x14, matrix products: 27.7 us -> 20.2 us  [contract(): lax.dot_general(left, right, (((left_dim,), (right_dim,)), ((), ())), pre...]
    unnamed x191 -> x167, local copies, waits for them, and re-layouts: 27 us -> 20.1 us
  transfers between devices with their start and end apart: 69 -> 69, of which waited for: 32 -> 30; matrix products, arithmetic and copies ran while one was open for 29% -> 29% of each run, Pallas kernels for 13% -> 14%
where the time goes in v6:
time: 458 us; the launch traced here: 453 us
  waiting for transfers between devices  158 us (34%)
  Pallas kernels  65.4 us (14%)
  matrix products  64.9 us (14%)
  starting transfers between devices  58 us (13%)
  local copies, waits for them, and re-layouts  57 us (12%)
  other arithmetic  47.1 us (10%)
    ppermute x69, waiting for transfers between devices, swap(): return lax.ppermute(value, AXES, [(i, i ^ mask) for i in range(n)])  158 us
    ppermute x69, starting transfers between devices, swap(): return lax.ppermute(value, AXES, [(i, i ^ mask) for i in range(n)])  58 us
    pallas_call x2, Pallas kernels, attend(): pl.pallas_call(attend_kernel, grid=(1,), in_specs=[columns, pairs, bias_s...  32.4 us
    pallas_call x2, Pallas kernels, attend_back(): pl.pallas_call(attend_back_kernel, grid=(1,), in_specs=[columns, pairs, b...  25.2 us
    dot_general x8, matrix products, product_right(): lax.dot_general(left, right, (((1,), (1,)), ((), ())), preferred_element_...  25.2 us
    convert_element_type x27, other arithmetic, add_low(): return (left.astype(wide) + right.astype(wide)).astype(low)  22.9 us
    dot_general x14, matrix products, contract(): lax.dot_general(left, right, (((left_dim,), (right_dim,)), ((), ())), pre...  20.2 us
    unnamed x167, local copies, waits for them, and re-layouts  20.1 us
  transfers between devices with their start and end apart: 69, of which 30 were waited for; matrix products, arithmetic and copies ran while one was open for 29% of the time, Pallas kernels for 14%

profile of v6, /device:TPU:0, one launch (start us, length us, event | category | flops | bytes accessed | tf_op | source)
XLA Modules:
  0.0 452.9 jit_solution(17768740826475770644)
XLA Ops:
  23.0 7.2 %collective-permute-done.1 = bf16[2,32,1600]{2,1,0:T(8,128)(2,1)S(1)} collective-permute-done((bf16[2,32,1600]{2,1,0:T(8,128)(2,1)S(1)}, bf16[2,32,1600]{2,1,0:T(8,128)(2,1)S(1)}, u32[]{:S(2)}, u32[]{:S(2)}) %collective-permute-start.1) | collective-permute-done | bytes 204832 | tf_op jit(solution)/shard_map/ppermute | solution.py:79
  35.3 5.5 %collective-permute-done.4 = bf16[4,32,640]{2,1,0:T(8,128)(2,1)S(1)} collective-permute-done((bf16[4,32,640]{2,1,0:T(8,128)(2,1)S(1)}, bf16[4,32,640]{2,1,0:T(8,128)(2,1)S(1)}, u32[]{:S(2)}, u32[]{:S(2)}) %collective-permute-start.4) | collective-permute-done | bytes 163872 | tf_op jit(solution)/shard_map/ppermute | solution.py:79
  43.9 14.4 %collective-permute-done.13 = bf16[2,112,960]{2,1,0:T(8,128)(2,1)S(1)} collective-permute-done((bf16[2,112,960]{2,1,0:T(8,128)(2,1)S(1)}, bf16[2,112,960]{2,1,0:T(8,128)(2,1)S(1)}, u32[]{:S(2)}, u32[]{:S(2)}) %collective-permute-start.13) | collective-permute-done | bytes 430112 | tf_op jit(solution)/shard_map/ppermute | solution.py:79
  64.5 15.5 %collective-permute-done.21 = bf16[2,32,2560]{2,1,0:T(8,128)(2,1)S(1)} collective-permute-done((bf16[2,32,2560]{2,1,0:T(8,128)(2,1)S(1)}, bf16[2,32,2560]{2,1,0:T(8,128)(2,1)S(1)}, u32[]{:S(2)}, u32[]{:S(2)}) %collective-permute-start.21) | collective-permute-done | bytes 327712 | tf_op jit(solution)/shard_map/ppermute | solution.py:79
  89.3 10.8 %collective-permute-done.25 = bf16[2,32,2560]{2,1,0:T(8,128)(2,1)S(1)} collective-permute-done((bf16[2,32,2560]{2,1,0:T(8,128)(2,1)S(1)}, bf16[2,32,2560]{2,1,0:T(8,128)(2,1)S(1)}, u32[]{:S(2)}, u32[]{:S(2)}) %collective-permute-start.25) | collective-permute-done | bytes 327712 | tf_op jit(solution)/shard_map/ppermute | solution.py:79
  102.2 9.6 %collective-permute-done.18 = bf16[8,64,960]{2,1,0:T(8,128)(2,1)S(1)} collective-permute-done((bf16[8,64,960]{2,1,0:T(8,128)(2,1)S(1)}, bf16[8,64,960]{2,1,0:T(8,128)(2,1)S(1)}, u32[]{:S(2)}, u32[]{:S(2)}) %collective-permute-start.18) | collective-permute-done | bytes 983072 | tf_op jit(solution)/shard_map/ppermute | solution.py:79
  112.3 12.1 %collective-permute-done.22 = bf16[4,32,2560]{2,1,0:T(8,128)(2,1)S(1)} collective-permute-done((bf16[4,32,2560]{2,1,0:T(8,128)(2,1)S(1)}, bf16[4,32,2560]{2,1,0:T(8,128)(2,1)S(1)}, u32[]{:S(2)}, u32[]{:S(2)}) %collective-permute-start.22) | collective-permute-done | bytes 655392 | tf_op jit(solution)/shard_map/ppermute | solution.py:79
  126.7 4.6 %collective-permute-done.26 = bf16[4,32,2560]{2,1,0:T(8,128)(2,1)S(1)} collective-permute-done((bf16[4,32,2560]{2,1,0:T(8,128)(2,1)S(1)}, bf16[4,32,2560]{2,1,0:T(8,128)(2,1)S(1)}, u32[]{:S(2)}, u32[]{:S(2)}) %collective-permute-start.26) | collective-permute-done | bytes 655392 | tf_op jit(solution)/shard_map/ppermute | solution.py:79
  133.9 10.2 %attend.3 = (bf16[960,256]{1,0:T(8,128)(2,1)S(1)}, f32[1,15,256]{2,1,0:T(8,128)S(1)}) custom-call(bf16[960,512]{1,0:T(8,128)(2,1)S(1)} %get-tuple-element.101.q_ref, bf16[4,640,512]{2,1,0:T(8,128)(2,1)S(1)} %pad_maximum_fusion.kv_ref, f32[2,1024,256]{2,1,0:T(8,128)S(1)} %and_select_fusion.bias_ref), custom_call_target="tpu_custom_call" | custom-call | flops 3932160 | bytes 1048576 | tf_op jit(solution)/shard_map/attend/pallas_call | solution.py:365
  144.1 22.3 %attend.2 = (bf16[960,256]{1,0:T(8,128)(2,1)S(1)}, f32[1,15,256]{2,1,0:T(8,128)S(1)}) custom-call(bf16[960,512]{1,0:T(8,128)(2,1)S(1)} %get-tuple-element.101.q_ref, bf16[4,640,512]{2,1,0:T(8,128)(2,1)S(1)} %pad_maximum_fusion.kv_ref, f32[2,1024,256]{2,1,0:T(8,128)S(1)} %and_select_fusion.bias_ref), custom_call_target="tpu_custom_call" | custom-call | flops 3932160 | bytes 1048576 | tf_op jit(solution)/shard_map/attend/pallas_call | solution.py:365
  174.1 4.6 %fusion.123 = f32[2560,512]{0,1:T(8,128)} fusion(bf16[2560,960]{1,0:T(8,128)(2,1)S(1)} %bitcast.147, bf16[512,960]{1,0:T(8,128)(2,1)S(1)} %bitcast.138), kind=kOutput, calls=%fused_computation.295 | convolution fusion | flops 2516582400 | bytes 11141120 | tf_op jit(solution)/shard_map/dot_general | solution.py:74
  188.0 6.4 %fusion.4 = (bf16[512,2560]{1,0:T(8,128)(2,1)S(1)}, bf16[512,2560]{1,0:T(8,128)(2,1)S(1)}, bf16[512,2560]{1,0:T(8,128)(2,1)S(1)}) fusion(f32[2560,512]{0,1:T(8,128)} %fusion.123, f32[512,2560]{1,0:T(8,128)S(1)} %fusion.122, bf16[512,1024]{1,0:T(8,128)(2,1)S(1)} %fusion.42, bf16[1024,2560]{1,0:T(8,128)(2,1)S(1)} %bitcast.183), kind=kOutput, calls=%fused_computation.8 | convolution fusion | flops 2705326080 | bytes 24641536 | tf_op jit(solution)/shard_map/dot_general | solution.py:66
  201.1 4.3 down_grad_blocks.1
  206.6 5.6 %convolution_add_fusion.1 = f32[512,1024]{1,0:T(8,128)S(1)} fusion(f32[512,1024]{1,0:T(8,128)S(1)} %fusion.124, bf16[512,2560]{1,0:T(8,128)(2,1)S(1)} %get-tuple-element.214, bf16[1024,2560]{1,0:T(8,128)(2,1)} %bitcast.188), kind=kOutput, calls=%fused_computation.87 | convolution fusion | flops 2684878848 | bytes 12058624 | tf_op jit(solution)/shard_map/dot_general | solution.py:74
  231.8 4.5 fusion.43.do_ref
  239.0 18.0 %collective-permute-done.31 = bf16[8,32,2560]{2,1,0:T(8,128)(2,1)} collective-permute-done((bf16[8,32,2560]{2,1,0:T(8,128)(2,1)}, bf16[8,32,2560]{2,1,0:T(8,128)(2,1)}, u32[]{:S(2)}, u32[]{:S(2)}) %collective-permute-start.31) | collective-permute-done | bytes 1310752 | tf_op jit(solution)/shard_map/ppermute | solution.py:79
  264.5 12.6 %attend_back.2 = (f32[960,256]{1,0:T(8,128)S(1)}, bf16[4,640,256]{2,1,0:T(8,128)(2,1)S(1)}) custom-call(bf16[960,512]{1,0:T(8,128)(2,1)S(1)} %copy-done.3, bf16[4,640,512]{2,1,0:T(8,128)(2,1)} %copy-done, f32[2,1024,256]{2,1,0:T(8,128)} %copy-done.1, bf16[960,256]{1,0:T(8,128)(2,1)S(1)} %copy-done.12, f32[1,15,256]{2,1,0:T(8,128)S(1)} %get-tuple-element.126.lse_ref, ...), custom_call_target="tpu_custom_call" | custom-call | flops 3932160 | bytes 1048576 | tf_op jit(solution)/shard_map/attend_back/pallas_call | solution.py:388
  303.0 12.6 %attend_back.3 = (f32[960,256]{1,0:T(8,128)S(1)}, bf16[4,640,256]{2,1,0:T(8,128)(2,1)S(1)}) custom-call(bf16[960,512]{1,0:T(8,128)(2,1)S(1)} %copy-done.3, bf16[4,640,512]{2,1,0:T(8,128)(2,1)} %copy-done, f32[2,1024,256]{2,1,0:T(8,128)} %copy-done.1, bf16[960,256]{1,0:T(8,128)(2,1)S(1)} %copy-done.10, f32[1,15,256]{2,1,0:T(8,128)S(1)} %get-tuple-element.134.lse_ref, ...), custom_call_target="tpu_custom_call" | custom-call | flops 3932160 | bytes 1048576 | tf_op jit(solution)/shard_map/attend_back/pallas_call | solution.py:388
  344.3 8.7 %collective-permute-done.45 = bf16[8,32,960]{2,1,0:T(8,128)(2,1)S(1)} collective-permute-done((bf16[8,32,960]{2,1,0:T(8,128)(2,1)S(1)}, bf16[8,32,960]{2,1,0:T(8,128)(2,1)S(1)}, u32[]{:S(2)}, u32[]{:S(2)}) %collective-permute-start.45) | collective-permute-done | bytes 491552 | tf_op jit(solution)/shard_map/ppermute | solution.py:79
  380.1 11.0 %collective-permute-done.67 = bf16[2,80,960]{2,1,0:T(8,128)(2,1)} collective-permute-done((bf16[2,80,960]{2,1,0:T(8,128)(2,1)}, bf16[2,80,960]{2,1,0:T(8,128)(2,1)}, u32[]{:S(2)}, u32[]{:S(2)}) %collective-permute-start.67) | collective-permute-done | bytes 307232 | tf_op jit(solution)/shard_map/ppermute | solution.py:79
  394.2 6.2 %add_convert_fusion.7 = bf16[512,960]{1,0:T(8,128)(2,1)S(1)} fusion(f32[512,960]{1,0:T(8,128)} %copy-done.44, bf16[512,2560]{1,0:T(8,128)(2,1)S(1)} %copy-done.16, bf16[2560,960]{1,0:T(8,128)(2,1)} %bitcast.148), kind=kOutput, calls=%fused_computation.58 | convolution fusion | flops 2517565440 | bytes 10485760 | tf_op jit(solution)/shard_map/dot_general | solution.py:66
  411.3 5.5 %collective-permute-done.39 = bf16[8,32,640]{2,1,0:T(8,128)(2,1)S(1)} collective-permute-done((bf16[8,32,640]{2,1,0:T(8,128)(2,1)S(1)}, bf16[8,32,640]{2,1,0:T(8,128)(2,1)S(1)}, u32[]{:S(2)}, u32[]{:S(2)}) %collective-permute-start.39) | collective-permute-done | bytes 327712 | tf_op jit(solution)/shard_map/ppermute | solution.py:79
  419.9 3.7 collective-permute-done.41
  423.7 8.2 %collective-permute-done.47 = bf16[2,32,1920]{2,1,0:T(8,128)(2,1)S(1)} collective-permute-done((bf16[2,32,1920]{2,1,0:T(8,128)(2,1)S(1)}, bf16[2,32,1920]{2,1,0:T(8,128)(2,1)S(1)}, u32[]{:S(2)}, u32[]{:S(2)}) %collective-permute-start.47) | collective-permute-done | bytes 245792 | tf_op jit(solution)/shard_map/ppermute | solution.py:79
  (481 shorter events, 226.0 us)
Async XLA Ops:
  35.2 23.1 %collective-permute-start.13 = (bf16[2,112,960]{2,1,0:T(8,128)(2,1)S(1)}, bf16[2,112,960]{2,1,0:T(8,128)(2,1)S(1)}, u32[]{:S(2)}, u32[]{:S(2)}) collective-permute-start(bf16[2,112,960]{2,1,0:T(8,128)(2,1)S(1)} %pad_maximum_fusion.25), channel_id=1, source_target_pairs={{0,16},{1,17},{2,18},{3,19},{4,20},{5,21},{6,22},{7,23},{8,24},{9,... | collective-permute-start | bytes 1290248 | tf_op jit(solution)/shard_map/ppermute | solution.py:79
  40.9 21.1 %collective-permute-start.6 = (bf16[8,32,640]{2,1,0:T(8,128)(2,1)S(1)}, bf16[8,32,640]{2,1,0:T(8,128)(2,1)S(1)}, u32[]{:S(2)}, u32[]{:S(2)}) collective-permute-start(bf16[8,32,640]{2,1,0:T(8,128)(2,1)S(1)} %pad_maximum_fusion.30), channel_id=1, source_target_pairs={{0,4},{1,5},{2,6},{3,7},{4,0},{5,1},{6,2},{7,3},{8,12},{9,13},{10,... | collective-permute-start | bytes 983048 | tf_op jit(solution)/shard_map/ppermute | solution.py:79
  84.3 41.2 %collective-permute-start.16 = (bf16[8,48,960]{2,1,0:T(8,128)(2,1)S(1)}, bf16[8,48,960]{2,1,0:T(8,128)(2,1)S(1)}, u32[]{:S(2)}, u32[]{:S(2)}) collective-permute-start(bf16[8,48,960]{2,1,0:T(8,128)(2,1)S(1)} %pad_maximum_fusion.14), channel_id=1, source_target_pairs={{0,2},{1,3},{2,0},{3,1},{4,6},{5,7},{6,4},{7,5},{8,10},{9,11},{10,... | collective-permute-start | bytes 2211848 | tf_op jit(solution)/shard_map/ppermute | solution.py:79
  85.7 26.1 %collective-permute-start.18 = (bf16[8,64,960]{2,1,0:T(8,128)(2,1)S(1)}, bf16[8,64,960]{2,1,0:T(8,128)(2,1)S(1)}, u32[]{:S(2)}, u32[]{:S(2)}) collective-permute-start(bf16[8,64,960]{2,1,0:T(8,128)(2,1)S(1)} %pad_maximum_fusion.13), channel_id=1, source_target_pairs={{0,4},{1,5},{2,6},{3,7},{4,0},{5,1},{6,2},{7,3},{8,12},{9,13},{10,... | collective-permute-start | bytes 2949128 | tf_op jit(solution)/shard_map/ppermute | solution.py:79
  86.3 38.1 %collective-permute-start.22 = (bf16[4,32,2560]{2,1,0:T(8,128)(2,1)S(1)}, bf16[4,32,2560]{2,1,0:T(8,128)(2,1)S(1)}, u32[]{:S(2)}, u32[]{:S(2)}) collective-permute-start(bf16[4,32,2560]{2,1,0:T(8,128)(2,1)S(1)} %pad_maximum_fusion.16), channel_id=1, source_target_pairs={{0,4},{1,5},{2,6},{3,7},{4,0},{5,1},{6,2},{7,3},{8,12},{9,13},{10,... | collective-permute-start | bytes 1966088 | tf_op jit(solution)/shard_map/ppermute | solution.py:79
  101.4 31.1 %collective-permute-start.12 = (bf16[2,640,512]{2,1,0:T(8,128)(2,1)S(1)}, bf16[2,640,512]{2,1,0:T(8,128)(2,1)S(1)}, u32[]{:S(2)}, u32[]{:S(2)}) collective-permute-start(bf16[2,640,512]{2,1,0:T(8,128)(2,1)S(1)} %pad_maximum_fusion.7), channel_id=1, source_target_pairs={{0,1},{1,0},{2,3},{3,2},{4,5},{5,4},{6,7},{7,6},{8,9},{9,8},{10,11... | collective-permute-start | bytes 3932168 | tf_op jit(solution)/shard_map/ppermute | solution.py:79
  101.5 29.8 %collective-permute-start.26 = (bf16[4,32,2560]{2,1,0:T(8,128)(2,1)S(1)}, bf16[4,32,2560]{2,1,0:T(8,128)(2,1)S(1)}, u32[]{:S(2)}, u32[]{:S(2)}) collective-permute-start(bf16[4,32,2560]{2,1,0:T(8,128)(2,1)S(1)} %pad_maximum_fusion.17), channel_id=1, source_target_pairs={{0,2},{1,3},{2,0},{3,1},{4,6},{5,7},{6,4},{7,5},{8,10},{9,11},{10,... | collective-permute-start | bytes 1966088 | tf_op jit(solution)/shard_map/ppermute | solution.py:79
  112.2 57.1 %collective-permute-start.19 = (bf16[16,64,960]{2,1,0:T(8,128)(2,1)S(1)}, bf16[16,64,960]{2,1,0:T(8,128)(2,1)S(1)}, u32[]{:S(2)}, u32[]{:S(2)}) collective-permute-start(bf16[16,64,960]{2,1,0:T(8,128)(2,1)S(1)} %pad_maximum_fusion.2.c_ref), channel_id=1, source_target_pairs={{0,1},{1,0},{2,3},{3,2},{4,5},{5,4},{6,7},{7,6},{8,9},{9,8},{10,11... | collective-permute-start | bytes 5898248 | tf_op jit(solution)/shard_map/ppermute | solution.py:79
  125.7 43.6 %collective-permute-start.17 = (bf16[16,48,960]{2,1,0:T(8,128)(2,1)S(1)}, bf16[16,48,960]{2,1,0:T(8,128)(2,1)S(1)}, u32[]{:S(2)}, u32[]{:S(2)}) collective-permute-start(bf16[16,48,960]{2,1,0:T(8,128)(2,1)S(1)} %pad_maximum_fusion.6.a_ref), channel_id=1, source_target_pairs={{0,1},{1,0},{2,3},{3,2},{4,5},{5,4},{6,7},{7,6},{8,9},{9,8},{10,11... | collective-permute-start | bytes 4423688 | tf_op jit(solution)/shard_map/ppermute | solution.py:79
  132.5 46.6 %collective-permute-start.27 = (bf16[8,32,2560]{2,1,0:T(8,128)(2,1)}, bf16[8,32,2560]{2,1,0:T(8,128)(2,1)S(1)}, u32[]{:S(2)}, u32[]{:S(2)}) collective-permute-start(bf16[8,32,2560]{2,1,0:T(8,128)(2,1)} %pad_maximum_fusion.9), channel_id=1, source_target_pairs={{0,4},{1,5},{2,6},{3,7},{4,0},{5,1},{6,2},{7,3},{8,12},{9,13},{10,... | collective-permute-start | bytes 3932168 | tf_op jit(solution)/shard_map/ppermute | solution.py:79
  133.0 45.7 %collective-permute-start.23 = (bf16[8,32,2560]{2,1,0:T(8,128)(2,1)}, bf16[8,32,2560]{2,1,0:T(8,128)(2,1)S(1)}, u32[]{:S(2)}, u32[]{:S(2)}) collective-permute-start(bf16[8,32,2560]{2,1,0:T(8,128)(2,1)} %pad_maximum_fusion.8), channel_id=1, source_target_pairs={{0,2},{1,3},{2,0},{3,1},{4,6},{5,7},{6,4},{7,5},{8,10},{9,11},{10,... | collective-permute-start | bytes 3932168 | tf_op jit(solution)/shard_map/ppermute | solution.py:79
  200.7 21.4 %collective-permute-start.29 = (bf16[16,32,2560]{2,1,0:T(8,128)(2,1)S(1)}, bf16[16,32,2560]{2,1,0:T(8,128)(2,1)S(1)}, u32[]{:S(2)}, u32[]{:S(2)}) collective-permute-start(bf16[16,32,2560]{2,1,0:T(8,128)(2,1)S(1)} %bitcast.156), channel_id=1, source_target_pairs={{0,1},{1,0},{2,3},{3,2},{4,5},{5,4},{6,7},{7,6},{8,9},{9,8},{10,11... | collective-permute-start | bytes 7864328 | tf_op jit(solution)/shard_map/ppermute | solution.py:79
  225.6 31.4 %collective-permute-start.31 = (bf16[8,32,2560]{2,1,0:T(8,128)(2,1)}, bf16[8,32,2560]{2,1,0:T(8,128)(2,1)}, u32[]{:S(2)}, u32[]{:S(2)}) collective-permute-start(bf16[8,32,2560]{2,1,0:T(8,128)(2,1)} %slice.411), channel_id=1, source_target_pairs={{0,2},{1,3},{2,0},{3,1},{4,6},{5,7},{6,4},{7,5},{8,10},{9,11},{10,... | collective-permute-start | bytes 3932168 | tf_op jit(solution)/shard_map/ppermute | solution.py:79
  227.0 31.1 %collective-permute-start.32 = (bf16[8,32,2560]{2,1,0:T(8,128)(2,1)}, bf16[8,32,2560]{2,1,0:T(8,128)(2,1)}, u32[]{:S(2)}, u32[]{:S(2)}) collective-permute-start(bf16[8,32,2560]{2,1,0:T(8,128)(2,1)} %pad_maximum_fusion.10), channel_id=1, source_target_pairs={{0,4},{1,5},{2,6},{3,7},{4,0},{5,1},{6,2},{7,3},{8,12},{9,13},{10,... | collective-permute-start | bytes 3932168 | tf_op jit(solution)/shard_map/ppermute | solution.py:79
  236.3 42.0 %collective-permute-start.61 = (bf16[16,48,960]{2,1,0:T(8,128)(2,1)}, bf16[16,48,960]{2,1,0:T(8,128)(2,1)S(1)}, u32[]{:S(2)}, u32[]{:S(2)}) collective-permute-start(bf16[16,48,960]{2,1,0:T(8,128)(2,1)} %slice.382), channel_id=1, source_target_pairs={{0,1},{1,0},{2,3},{3,2},{4,5},{5,4},{6,7},{7,6},{8,9},{9,8},{10,11... | collective-permute-start | bytes 4423688 | tf_op jit(solution)/shard_map/ppermute | solution.py:79
  258.1 23.4 %collective-permute-start.65 = (bf16[8,32,960]{2,1,0:T(8,128)(2,1)}, bf16[8,32,960]{2,1,0:T(8,128)(2,1)S(1)}, u32[]{:S(2)}, u32[]{:S(2)}) collective-permute-start(bf16[8,32,960]{2,1,0:T(8,128)(2,1)} %pad_maximum_fusion.24), channel_id=1, source_target_pairs={{0,4},{1,5},{2,6},{3,7},{4,0},{5,1},{6,2},{7,3},{8,12},{9,13},{10,... | collective-permute-start | bytes 1474568 | tf_op jit(solution)/shard_map/ppermute | solution.py:79
  263.9 21.6 %collective-permute-start.33 = (bf16[4,32,2560]{2,1,0:T(8,128)(2,1)S(1)}, bf16[4,32,2560]{2,1,0:T(8,128)(2,1)}, u32[]{:S(2)}, u32[]{:S(2)}) collective-permute-start(bf16[4,32,2560]{2,1,0:T(8,128)(2,1)S(1)} %slice.415), channel_id=1, source_target_pairs={{0,4},{1,5},{2,6},{3,7},{4,0},{5,1},{6,2},{7,3},{8,12},{9,13},{10,... | collective-permute-start | bytes 1966088 | tf_op jit(solution)/shard_map/ppermute | solution.py:79
  280.1 48.7 %collective-permute-start.62 = (bf16[8,48,960]{2,1,0:T(8,128)(2,1)}, bf16[8,48,960]{2,1,0:T(8,128)(2,1)}, u32[]{:S(2)}, u32[]{:S(2)}) collective-permute-start(bf16[8,48,960]{2,1,0:T(8,128)(2,1)} %slice.474), channel_id=1, source_target_pairs={{0,2},{1,3},{2,0},{3,1},{4,6},{5,7},{6,4},{7,5},{8,10},{9,11},{10,... | collective-permute-start | bytes 2211848 | tf_op jit(solution)/shard_map/ppermute | solution.py:79
  282.4 44.6 %collective-permute-start.66 = (bf16[4,32,960]{2,1,0:T(8,128)(2,1)}, bf16[4,32,960]{2,1,0:T(8,128)(2,1)}, u32[]{:S(2)}, u32[]{:S(2)}) collective-permute-start(bf16[4,32,960]{2,1,0:T(8,128)(2,1)} %slice.482), channel_id=1, source_target_pairs={{0,2},{1,3},{2,0},{3,1},{4,6},{5,7},{6,4},{7,5},{8,10},{9,11},{10,... | collective-permute-start | bytes 737288 | tf_op jit(solution)/shard_map/ppermute | solution.py:79
  293.9 38.3 %collective-permute-start.57 = (bf16[2,32,2560]{2,1,0:T(8,128)(2,1)}, bf16[2,32,2560]{2,1,0:T(8,128)(2,1)}, u32[]{:S(2)}, u32[]{:S(2)}) collective-permute-start(bf16[2,32,2560]{2,1,0:T(8,128)(2,1)} %slice.461), channel_id=1, source_target_pairs={{0,16},{1,17},{2,18},{3,19},{4,20},{5,21},{6,22},{7,23},{8,24},{9,... | collective-permute-start | bytes 983048 | tf_op jit(solution)/shard_map/ppermute | solution.py:79
  296.5 36.7 %collective-permute-start.59 = (bf16[2,32,2560]{2,1,0:T(8,128)(2,1)}, bf16[2,32,2560]{2,1,0:T(8,128)(2,1)}, u32[]{:S(2)}, u32[]{:S(2)}) collective-permute-start(bf16[2,32,2560]{2,1,0:T(8,128)(2,1)} %slice.468), channel_id=1, source_target_pairs={{0,16},{1,17},{2,18},{3,19},{4,20},{5,21},{6,22},{7,23},{8,24},{9,... | collective-permute-start | bytes 983048 | tf_op jit(solution)/shard_map/ppermute | solution.py:79
  301.9 33.1 %collective-permute-start.44 = (bf16[16,32,960]{2,1,0:T(8,128)(2,1)}, bf16[16,32,960]{2,1,0:T(8,128)(2,1)}, u32[]{:S(2)}, u32[]{:S(2)}) collective-permute-start(bf16[16,32,960]{2,1,0:T(8,128)(2,1)} %bitcast.166), channel_id=1, source_target_pairs={{0,1},{1,0},{2,3},{3,2},{4,5},{5,4},{6,7},{7,6},{8,9},{9,8},{10,11... | collective-permute-start | bytes 2949128 | tf_op jit(solution)/shard_map/ppermute | solution.py:79
  362.9 30.0 %collective-permute-start.42 = (bf16[8,32,960]{2,1,0:T(8,128)(2,1)}, bf16[8,32,960]{2,1,0:T(8,128)(2,1)}, u32[]{:S(2)}, u32[]{:S(2)}) collective-permute-start(bf16[8,32,960]{2,1,0:T(8,128)(2,1)} %slice.435), channel_id=1, source_target_pairs={{0,2},{1,3},{2,0},{3,1},{4,6},{5,7},{6,4},{7,5},{8,10},{9,11},{10,... | collective-permute-start | bytes 1474568 | tf_op jit(solution)/shard_map/ppermute | solution.py:79
  365.4 28.8 %collective-permute-start.38 = (bf16[16,32,640]{2,1,0:T(8,128)(2,1)}, bf16[16,32,640]{2,1,0:T(8,128)(2,1)}, u32[]{:S(2)}, u32[]{:S(2)}) collective-permute-start(bf16[16,32,640]{2,1,0:T(8,128)(2,1)} %bitcast.32), channel_id=1, source_target_pairs={{0,1},{1,0},{2,3},{3,2},{4,5},{5,4},{6,7},{7,6},{8,9},{9,8},{10,11... | collective-permute-start | bytes 1966088 | tf_op jit(solution)/shard_map/ppermute | solution.py:79
  (119 other events, 1383.7 us)
